TPU v7x, 32 devices: a whole 2x2x4 slice. The times are simulated.
32 devices in a mesh: dp: 8 (over z, y), fsdp: 4 (over x, core).
Axes of the slice: x: 2, y: 2, z: 4, core: 2. Of those that a mesh axis runs over, the one named last changes fastest.
Arguments:
- suffix: bfloat16 [4, 32, 64, 768], P('fsdp', 'dp'), may hold values from -6 to 6
- memory: bfloat16 [4, 32, 256, 768], P('fsdp', None, 'dp'), may hold values from -6 to 6
- prefix_lengths: int32 [4, 32], P('fsdp', 'dp'), may hold values from 0 to 60, as said below
- suffix_lengths: int32 [4, 32], P('fsdp', 'dp'), may hold values from 1 to 64, as said below
- cotangent: bfloat16 [4, 32, 64, 768], P('fsdp', 'dp'), may hold values from -6 to 6
- self_weights: float32 [2359296], P(('dp', 'fsdp'))
- self_moment: float32 [2359296], P(('dp', 'fsdp')), may hold values from -0.0048828125 to 0.0048828125
- self_second: float32 [2359296], P(('dp', 'fsdp')), may hold values from 1.05963814e-07 to 4.2385525e-07
- cross_weights: float32 [2359296], P(('dp', 'fsdp'))
- cross_moment: float32 [2359296], P(('dp', 'fsdp')), may hold values from -0.0048828125 to 0.0048828125
- cross_second: float32 [2359296], P(('dp', 'fsdp')), may hold values from 1.05963814e-07 to 4.2385525e-07
- feed_weights: float32 [4718592], P(('dp', 'fsdp'))
- feed_moment: float32 [4718592], P(('dp', 'fsdp')), may hold values from -0.0048828125 to 0.0048828125
- feed_second: float32 [4718592], P(('dp', 'fsdp')), may hold values from 1.05963814e-07 to 4.2385525e-07
- vectors: float32 [8448], replicated
- vector_moment: float32 [8448], replicated, may hold values from -0.015625 to 0.015625
- vector_second: float32 [8448], replicated, may hold values from 9.536743e-07 to 3.8146973e-06
Outputs:
- layer_output: float32 [4, 32, 64, 768], P('fsdp', 'dp')
- suffix_gradient: float32 [4, 32, 64, 768], P('fsdp', 'dp')
- memory_gradient: float32 [4, 32, 256, 768], P('fsdp', None, 'dp')
- self_gradient: float32 [2359296], P(('dp', 'fsdp'))
- self_momentum: float32 [2359296], P(('dp', 'fsdp'))
- self_variance: float32 [2359296], P(('dp', 'fsdp'))
- self_master: float32 [2359296], P(('dp', 'fsdp'))
- cross_gradient: float32 [2359296], P(('dp', 'fsdp'))
- cross_momentum: float32 [2359296], P(('dp', 'fsdp'))
- cross_variance: float32 [2359296], P(('dp', 'fsdp'))
- cross_master: float32 [2359296], P(('dp', 'fsdp'))
- feed_gradient: float32 [4718592], P(('dp', 'fsdp'))
- feed_momentum: float32 [4718592], P(('dp', 'fsdp'))
- feed_variance: float32 [4718592], P(('dp', 'fsdp'))
- feed_master: float32 [4718592], P(('dp', 'fsdp'))
- vector_gradient: float32 [8448], replicated
- vector_momentum: float32 [8448], replicated
- vector_variance: float32 [8448], replicated
- vector_master: float32 [8448], replicated
- tensor_norms: float32 [2, 18], replicated
- global_norm: float32 [], replicated
Inputs may be any that keep to these rules, and one draw needn't show every extreme that they name: The number of prefix text tokens of each example, zero for many; memory slots from 196 + prefix_lengths on are padding. The number of caption tokens of each example; slots from suffix_lengths on are padding.
All inputs are finite; a program needn't handle non-finite values.
Results may differ from a plain program's by a relative error of at most 0.014.
The roundings to bfloat16 on the way count: a program that leaves them out, or rounds other values in their place, can miss the bound.
Values may be sent and summed in bfloat16 or wider, within the bound.
A program may use at most 192 MiB of HBM per device.

v0:
```python
import jax
import jax.numpy as jnp
from jax import lax
from jax.sharding import PartitionSpec as P

D = 768
H = 12
HD = 64
FF = 3072
PATCH = 196
SUF = 64
EX_DEV = 4
MEMLEN = 256


beta_one = 0.5
beta_two = 0.55
step_count = 5
learn_rate = 0.5
decay_weight = 0.01
adam_eps = 1e-06
norm_eps = 1e-06
trust_eps = 1e-06
masked_score = -1e30


def layer_norm(values, norm_gain, norm_shift):
    centred = values - jnp.mean(values, axis=-1, keepdims=True)
    spread = jnp.mean(centred * centred, axis=-1, keepdims=True)
    return centred * lax.rsqrt(spread + norm_eps) * norm_gain + norm_shift


def gelu_tanh(values):
    return jax.nn.gelu(values, approximate=True)


def attend_forward(query_heads, key_heads, value_heads, allowed):
    score_scale = HD ** (-0.5)
    scores = (
        jnp.einsum("bqhe,bkhe->bhqk", query_heads, key_heads, preferred_element_type=jnp.float32)
        * score_scale
    )
    scores = jnp.where(allowed, scores, masked_score)
    attention = jax.nn.softmax(scores, axis=-1)
    totals = jax.nn.logsumexp(scores, axis=-1)
    mixed_rows = jnp.einsum(
        "bhqk,bkhe->bqhe",
        attention.astype(jnp.bfloat16),
        value_heads,
        preferred_element_type=jnp.float32,
    )
    return (mixed_rows, totals)


def attend_backward(query_heads, key_heads, value_heads, allowed, totals, mixed_grad):
    score_scale = HD ** (-0.5)
    scores = (
        jnp.einsum("bqhe,bkhe->bhqk", query_heads, key_heads, preferred_element_type=jnp.float32)
        * score_scale
    )
    scores = jnp.where(allowed, scores, masked_score)
    attention = jnp.exp(scores - totals[..., None])
    value_grad = jnp.einsum(
        "bhqk,bqhe->bkhe",
        attention.astype(jnp.bfloat16),
        mixed_grad,
        preferred_element_type=jnp.float32,
    )
    attention_grad = jnp.einsum(
        "bqhe,bkhe->bhqk", mixed_grad, value_heads, preferred_element_type=jnp.float32
    )
    score_grad = attention * (
        attention_grad - jnp.sum(attention * attention_grad, axis=-1, keepdims=True)
    )
    score_low = score_grad.astype(jnp.bfloat16)
    query_grad = (
        jnp.einsum("bhqk,bkhe->bqhe", score_low, key_heads, preferred_element_type=jnp.float32)
        * score_scale
    )
    key_grad = (
        jnp.einsum("bhqk,bqhe->bkhe", score_low, query_heads, preferred_element_type=jnp.float32)
        * score_scale
    )
    return (query_grad, key_grad, value_grad)


def lamb_step(weight, gradient, moment, second, clip_factor):
    clipped = clip_factor * gradient
    moment_new = beta_one * moment + (1.0 - beta_one) * clipped
    second_new = beta_two * second + (1.0 - beta_two) * clipped * clipped
    ratio = (
        moment_new
        / (1.0 - beta_one**step_count)
        / (jnp.sqrt(second_new / (1.0 - beta_two**step_count)) + adam_eps)
        + decay_weight * weight
    )
    return (moment_new, second_new, ratio)


def segment_sums(values, offset, segment_size, tensor_count):
    labels = (offset + jnp.arange(values.shape[0], dtype=jnp.int32)) // segment_size
    matches = labels[:, None] == jnp.arange(tensor_count, dtype=jnp.int32)[None, :]
    return jnp.sum(jnp.where(matches, values[:, None], 0.0), axis=0)


def segment_spread(factors, offset, length_here, segment_size):
    labels = (offset + jnp.arange(length_here, dtype=jnp.int32)) // segment_size
    matches = labels[:, None] == jnp.arange(factors.shape[0], dtype=jnp.int32)[None, :]
    return jnp.sum(jnp.where(matches, factors[None, :], 0.0), axis=1)


def shards(
    suffix,
    memory,
    prefix_lengths,
    suffix_lengths,
    cotangent,
    self_weights,
    self_moment,
    self_second,
    cross_weights,
    cross_moment,
    cross_second,
    feed_weights,
    feed_moment,
    feed_second,
    vectors,
    vector_moment,
    vector_second,
):
    row_count = EX_DEV * SUF
    attn_shard = self_weights.shape[0]
    feed_shard = feed_weights.shape[0]
    self_full, cross_full, feed_full = (
        lax.all_gather(self_weights.astype(jnp.bfloat16), ("dp", "fsdp"), axis=0, tiled=True),
        lax.all_gather(cross_weights.astype(jnp.bfloat16), ("dp", "fsdp"), axis=0, tiled=True),
        lax.all_gather(feed_weights.astype(jnp.bfloat16), ("dp", "fsdp"), axis=0, tiled=True),
    )
    self_mats = self_full.reshape(4, D, D)
    cross_mats = cross_full.reshape(4, D, D)
    up_mat = feed_full[: D * FF].reshape(D, FF)
    down_mat = feed_full[D * FF :].reshape(FF, D)
    vector_parts = [vectors[segment * D : (segment + 1) * D] for segment in range(7)]
    bias_up = vectors[7 * D :]
    own_memory = lax.all_to_all(memory, "dp", split_axis=1, concat_axis=2, tiled=True)
    memory_rows = own_memory.reshape(EX_DEV * MEMLEN, D)
    suffix_len = suffix_lengths[0]
    prefix_len = prefix_lengths[0]
    positions = jnp.arange(SUF, dtype=jnp.int32)
    causal = positions[:, None] >= positions[None, :]
    self_allowed = (
        causal[None, None, :, :] & (positions[None, :] < suffix_len[:, None])[:, None, None, :]
    )
    memory_pos = jnp.arange(MEMLEN, dtype=jnp.int32)
    cross_allowed = (memory_pos[None, :] < (PATCH + prefix_len)[:, None])[:, None, None, :]
    inputs = suffix.reshape(row_count, D).astype(jnp.float32)
    normed_one = layer_norm(inputs, vector_parts[0], vector_parts[1]).astype(jnp.bfloat16)
    self_qkv = jnp.einsum(
        "rd,jde->jre", normed_one, self_mats[0:3], preferred_element_type=jnp.float32
    ).astype(jnp.bfloat16)
    self_heads = self_qkv.reshape(3, EX_DEV, SUF, H, HD)
    mixed_one, totals_one = attend_forward(
        self_heads[0], self_heads[1], self_heads[2], self_allowed
    )
    mixed_one = mixed_one.reshape(row_count, D).astype(jnp.bfloat16)
    hidden_one = inputs + jnp.dot(mixed_one, self_mats[3], preferred_element_type=jnp.float32)
    normed_two = layer_norm(hidden_one, vector_parts[2], vector_parts[3]).astype(jnp.bfloat16)
    cross_query = jnp.dot(normed_two, cross_mats[0], preferred_element_type=jnp.float32).astype(
        jnp.bfloat16
    )
    cross_kv = jnp.einsum(
        "rd,jde->jre", memory_rows, cross_mats[1:3], preferred_element_type=jnp.float32
    ).astype(jnp.bfloat16)
    query_heads = cross_query.reshape(EX_DEV, SUF, H, HD)
    kv_heads = cross_kv.reshape(2, EX_DEV, MEMLEN, H, HD)
    mixed_two, totals_two = attend_forward(query_heads, kv_heads[0], kv_heads[1], cross_allowed)
    mixed_two = mixed_two.reshape(row_count, D).astype(jnp.bfloat16)
    hidden_two = hidden_one + jnp.dot(mixed_two, cross_mats[3], preferred_element_type=jnp.float32)
    normed_three = layer_norm(hidden_two, vector_parts[4], vector_parts[5]).astype(jnp.bfloat16)
    pre_act = jnp.dot(normed_three, up_mat, preferred_element_type=jnp.float32) + bias_up
    activated = gelu_tanh(pre_act).astype(jnp.bfloat16)
    layer_output = hidden_two + (
        jnp.dot(activated, down_mat, preferred_element_type=jnp.float32) + vector_parts[6]
    )
    valid_rows = (positions[None, :] < suffix_len[:, None]).astype(jnp.float32)
    seed_rows = (
        cotangent.reshape(EX_DEV, SUF, D).astype(jnp.float32) * valid_rows[:, :, None]
    ).reshape(row_count, D)
    seed_low = seed_rows.astype(jnp.bfloat16)
    bias_down_grad = jnp.sum(seed_low.astype(jnp.float32), axis=0)
    down_grad = jnp.einsum("rf,rd->fd", activated, seed_low, preferred_element_type=jnp.float32)
    activated_grad = jnp.einsum("rd,fd->rf", seed_low, down_mat, preferred_element_type=jnp.float32)
    _, gelu_back = jax.vjp(gelu_tanh, pre_act)
    pre_grad = gelu_back(activated_grad)[0].astype(jnp.bfloat16)
    bias_up_grad = jnp.sum(pre_grad.astype(jnp.float32), axis=0)
    up_grad = jnp.einsum("rd,rf->df", normed_three, pre_grad, preferred_element_type=jnp.float32)
    normed_three_grad = jnp.einsum(
        "rf,df->rd", pre_grad, up_mat, preferred_element_type=jnp.float32
    )
    _, norm_three_back = jax.vjp(layer_norm, hidden_two, vector_parts[4], vector_parts[5])
    through_three, gain_three_grad, shift_three_grad = norm_three_back(normed_three_grad)
    hidden_two_grad = seed_rows + through_three
    feed_flat = jnp.concatenate([up_grad.reshape(-1), down_grad.reshape(-1)])
    branch_two = hidden_two_grad.astype(jnp.bfloat16)
    cross_out_grad = jnp.einsum(
        "rd,re->de", mixed_two, branch_two, preferred_element_type=jnp.float32
    )
    mixed_two_grad = jnp.einsum(
        "re,de->rd", branch_two, cross_mats[3], preferred_element_type=jnp.float32
    ).astype(jnp.bfloat16)
    query_two_grad, key_two_grad, value_two_grad = attend_backward(
        query_heads,
        kv_heads[0],
        kv_heads[1],
        cross_allowed,
        totals_two,
        mixed_two_grad.reshape(EX_DEV, SUF, H, HD),
    )
    cross_query_grad = query_two_grad.reshape(row_count, D).astype(jnp.bfloat16)
    cross_kv_grad = (
        jnp.stack([key_two_grad, value_two_grad])
        .reshape(2, EX_DEV * MEMLEN, D)
        .astype(jnp.bfloat16)
    )
    query_weight_grad = jnp.einsum(
        "rd,re->de", normed_two, cross_query_grad, preferred_element_type=jnp.float32
    )
    kv_weight_grad = jnp.einsum(
        "rd,jre->jde", memory_rows, cross_kv_grad, preferred_element_type=jnp.float32
    )
    normed_two_grad = jnp.einsum(
        "re,de->rd", cross_query_grad, cross_mats[0], preferred_element_type=jnp.float32
    )
    memory_local_grad = jnp.einsum(
        "jre,jde->rd", cross_kv_grad, cross_mats[1:3], preferred_element_type=jnp.float32
    )
    memory_gradient = lax.all_to_all(
        memory_local_grad.reshape(1, EX_DEV, MEMLEN, D),
        "dp",
        split_axis=2,
        concat_axis=1,
        tiled=True,
    )
    _, norm_two_back = jax.vjp(layer_norm, hidden_one, vector_parts[2], vector_parts[3])
    through_two, gain_two_grad, shift_two_grad = norm_two_back(normed_two_grad)
    hidden_one_grad = hidden_two_grad + through_two
    cross_flat = jnp.concatenate(
        [query_weight_grad[None], kv_weight_grad, cross_out_grad[None]], axis=0
    ).reshape(-1)
    branch_one = hidden_one_grad.astype(jnp.bfloat16)
    self_out_grad = jnp.einsum(
        "rd,re->de", mixed_one, branch_one, preferred_element_type=jnp.float32
    )
    mixed_one_grad = jnp.einsum(
        "re,de->rd", branch_one, self_mats[3], preferred_element_type=jnp.float32
    ).astype(jnp.bfloat16)
    query_one_grad, key_one_grad, value_one_grad = attend_backward(
        self_heads[0],
        self_heads[1],
        self_heads[2],
        self_allowed,
        totals_one,
        mixed_one_grad.reshape(EX_DEV, SUF, H, HD),
    )
    self_qkv_grad = (
        jnp.stack([query_one_grad, key_one_grad, value_one_grad])
        .reshape(3, row_count, D)
        .astype(jnp.bfloat16)
    )
    qkv_weight_grad = jnp.einsum(
        "rd,jre->jde", normed_one, self_qkv_grad, preferred_element_type=jnp.float32
    )
    normed_one_grad = jnp.einsum(
        "jre,jde->rd", self_qkv_grad, self_mats[0:3], preferred_element_type=jnp.float32
    )
    _, norm_one_back = jax.vjp(layer_norm, inputs, vector_parts[0], vector_parts[1])
    through_one, gain_one_grad, shift_one_grad = norm_one_back(normed_one_grad)
    suffix_gradient = (hidden_one_grad + through_one).reshape(1, EX_DEV, SUF, D)
    self_flat = jnp.concatenate([qkv_weight_grad, self_out_grad[None]], axis=0).reshape(-1)
    owners = lax.axis_size(("dp", "fsdp"))
    joined = jnp.concatenate(
        [
            self_flat.reshape(owners, attn_shard),
            cross_flat.reshape(owners, attn_shard),
            feed_flat.reshape(owners, feed_shard),
        ],
        axis=1,
    ).reshape(-1)
    owned = lax.psum_scatter(joined, ("dp", "fsdp"), scatter_dimension=0, tiled=True)
    self_total = owned[:attn_shard]
    cross_total = owned[attn_shard : 2 * attn_shard]
    feed_total = owned[2 * attn_shard :]
    vector_partial = jnp.concatenate(
        [
            gain_one_grad,
            shift_one_grad,
            gain_two_grad,
            shift_two_grad,
            gain_three_grad,
            shift_three_grad,
            bias_down_grad,
            bias_up_grad,
        ]
    )
    shard_index = lax.axis_index(("dp", "fsdp"))
    attn_offset = shard_index * attn_shard
    feed_offset = shard_index * feed_shard
    grad_squares = jnp.concatenate(
        [
            segment_sums(self_total * self_total, attn_offset, D * D, 4),
            segment_sums(cross_total * cross_total, attn_offset, D * D, 4),
            segment_sums(feed_total * feed_total, feed_offset, D * FF, 2),
        ]
    )
    weight_squares = jnp.concatenate(
        [
            segment_sums(self_weights * self_weights, attn_offset, D * D, 4),
            segment_sums(cross_weights * cross_weights, attn_offset, D * D, 4),
            segment_sums(feed_weights * feed_weights, feed_offset, D * FF, 2),
        ]
    )
    vector_total, grad_summed, weight_summed = lax.psum(
        (vector_partial, grad_squares, weight_squares), ("dp", "fsdp")
    )
    squared_total = jnp.sum(grad_summed) + jnp.sum(vector_total * vector_total)
    global_norm = jnp.sqrt(squared_total)
    clip_factor = jnp.minimum(1.0, 1.0 / global_norm)
    self_momentum, self_variance, self_ratio = lamb_step(
        self_weights, self_total, self_moment, self_second, clip_factor
    )
    cross_momentum, cross_variance, cross_ratio = lamb_step(
        cross_weights, cross_total, cross_moment, cross_second, clip_factor
    )
    feed_momentum, feed_variance, feed_ratio = lamb_step(
        feed_weights, feed_total, feed_moment, feed_second, clip_factor
    )
    ratio_squares = jnp.concatenate(
        [
            segment_sums(self_ratio * self_ratio, attn_offset, D * D, 4),
            segment_sums(cross_ratio * cross_ratio, attn_offset, D * D, 4),
            segment_sums(feed_ratio * feed_ratio, feed_offset, D * FF, 2),
        ]
    )
    update_summed = lax.psum(ratio_squares, ("dp", "fsdp"))
    weight_norms = jnp.sqrt(weight_summed)
    ratio_norms = jnp.sqrt(update_summed)
    trust_ratio = weight_norms / (ratio_norms + trust_eps)
    self_master = (
        self_weights
        - learn_rate * segment_spread(trust_ratio[0:4], attn_offset, attn_shard, D * D) * self_ratio
    )
    cross_master = (
        cross_weights
        - learn_rate
        * segment_spread(trust_ratio[4:8], attn_offset, attn_shard, D * D)
        * cross_ratio
    )
    feed_master = (
        feed_weights
        - learn_rate
        * segment_spread(trust_ratio[8:10], feed_offset, feed_shard, D * FF)
        * feed_ratio
    )
    vector_momentum, vector_variance, vector_ratio = lamb_step(
        vectors, vector_total, vector_moment, vector_second, clip_factor
    )
    edges = [0, D, 2 * D, 3 * D, 4 * D, 5 * D, 6 * D, 7 * D, 7 * D + FF]
    vector_wn = []
    vector_rn = []
    new_pieces = []
    for segment in range(8):
        weight_part = vectors[edges[segment] : edges[segment + 1]]
        ratio_part = vector_ratio[edges[segment] : edges[segment + 1]]
        weight_norm = jnp.sqrt(jnp.sum(weight_part * weight_part))
        ratio_norm = jnp.sqrt(jnp.sum(ratio_part * ratio_part))
        piece_trust = weight_norm / (ratio_norm + trust_eps)
        vector_wn.append(weight_norm)
        vector_rn.append(ratio_norm)
        new_pieces.append(weight_part - learn_rate * piece_trust * ratio_part)
    vector_master = jnp.concatenate(new_pieces)
    tensor_norms = jnp.stack(
        [
            jnp.concatenate([weight_norms, jnp.stack(vector_wn)]),
            jnp.concatenate([ratio_norms, jnp.stack(vector_rn)]),
        ]
    )
    return (
        layer_output.reshape(1, EX_DEV, SUF, D),
        suffix_gradient,
        memory_gradient,
        self_total,
        self_momentum,
        self_variance,
        self_master,
        cross_total,
        cross_momentum,
        cross_variance,
        cross_master,
        feed_total,
        feed_momentum,
        feed_variance,
        feed_master,
        vector_total,
        vector_momentum,
        vector_variance,
        vector_master,
        tensor_norms,
        global_norm,
    )


def solution(mesh):
    return jax.shard_map(
        shards,
        mesh=mesh,
        in_specs=(
            P("fsdp", "dp", None, None),
            P("fsdp", None, "dp", None),
            P("fsdp", "dp"),
            P("fsdp", "dp"),
            P("fsdp", "dp", None, None),
            P(("dp", "fsdp")),
            P(("dp", "fsdp")),
            P(("dp", "fsdp")),
            P(("dp", "fsdp")),
            P(("dp", "fsdp")),
            P(("dp", "fsdp")),
            P(("dp", "fsdp")),
            P(("dp", "fsdp")),
            P(("dp", "fsdp")),
            P(),
            P(),
            P(),
        ),
        out_specs=(
            P("fsdp", "dp", None, None),
            P("fsdp", "dp", None, None),
            P("fsdp", None, "dp", None),
            P(("dp", "fsdp")),
            P(("dp", "fsdp")),
            P(("dp", "fsdp")),
            P(("dp", "fsdp")),
            P(("dp", "fsdp")),
            P(("dp", "fsdp")),
            P(("dp", "fsdp")),
            P(("dp", "fsdp")),
            P(("dp", "fsdp")),
            P(("dp", "fsdp")),
            P(("dp", "fsdp")),
            P(("dp", "fsdp")),
            P(),
            P(),
            P(),
            P(),
            P(),
            P(),
        ),
        check_vma=False,
    )
```

profile of v0, /device:TPU:0, one launch (start us, length us, event | category | flops | bytes accessed | tf_op | source)
XLA Modules:
  0.0 1262.3 jit_solution(2091022248354147053)
XLA Ops:
  10.8 7.4 all-to-all-start
  25.4 39.3 %all-to-all-done = bf16[1,32,32,768]{3,2,0,1:T(8,128)(2,1)S(1)} async-done(((bf16[1,32,32,768]{3,2,0,1:T(8,128)(2,1)}), bf16[1,32,32,768]{3,2,0,1:T(8,128)(2,1)S(1)}, u32[]{:S(2)}, u32[]{:S(2)}) %all-to-all-start) | async-done | bytes 1572896 | tf_op jit(solution)/shard_map/all_to_all | solution.py:145
  66.0 22.2 %all-gather.4.cloned.1.call-done = bf16[2359296]{0:T(1024)(128)(2,1)} async-done(((bf16[73728]{0:T(1024)(128)(2,1)}), bf16[2359296]{0:T(1024)(128)(2,1)}) %all-gather.4.cloned.1.call-update) | async-done | bytes 4718608 | tf_op jit(solution)/shard_map/all_gather | solution.py:135
  90.2 4.6 slice.203
  97.1 3.6 fusion.21
  110.9 43.2 %all-gather.6.cloned.1.call-done = bf16[2359296]{0:T(1024)(128)(2,1)} async-done(((bf16[73728]{0:T(1024)(128)(2,1)}), bf16[2359296]{0:T(1024)(128)(2,1)}) %all-gather.6.cloned.1.call-update) | async-done | bytes 4718608 | tf_op jit(solution)/shard_map/all_gather | solution.py:136
  154.2 2.8 fusion.81
  156.9 3.4 slice.218
  168.2 3.6 slice.210
  171.8 4.8 convert_bitcast_fusion
  177.0 2.4 squeeze.13
  179.4 2.3 squeeze.14
  181.7 2.6 fusion.88
  184.4 2.6 exponential_reduce_fusion
  192.2 2.2 fusion.89
  197.4 41.1 %all-gather.8.cloned.1.call-done = bf16[4718592]{0:T(1024)(128)(2,1)} async-done(((bf16[147456]{0:T(1024)(128)(2,1)}), bf16[4718592]{0:T(1024)(128)(2,1)}) %all-gather.8.cloned.1.call-update) | async-done | bytes 9437200 | tf_op jit(solution)/shard_map/all_gather | solution.py:137
  238.6 8.3 fusion.80
  246.9 8.2 slice.222
  255.1 9.3 slice.225
  264.5 3.9 fusion.90
  268.5 6.1 convert_reduce_fusion
  274.6 2.1 multiply_reduce_fusion.2
  280.2 2.4 reshape.496
  282.7 2.5 copy.212
  285.2 3.1 fusion.18
  296.6 2.1 multiply_reduce_fusion.3
  301.3 2.4 reshape.497
  303.8 2.6 copy.204
  306.4 2.1 multiply_reduce_fusion.1
  319.3 5.2 fusion.64
  324.5 2.4 copy.213
  326.9 3.8 stack.83
  330.7 3.8 copy.211
  334.5 3.9 stack.82
  339.9 2.6 reshape.488
  342.5 2.7 copy.236
  345.1 2.5 reshape.489
  349.3 2.7 reshape.490
  356.9 4.2 convolution_bitcast_fusion.1
  362.0 6.9 pad_maximum_fusion.1
  368.9 9.6 copy.222
  378.5 8.2 reshape_reshape.7
  389.3 2.4 convolution_bitcast_fusion
  391.7 4.5 pad_maximum_fusion
  396.1 9.7 copy.219
  405.8 8.2 reshape_reshape.6
  414.0 10.8 concatenate.44
  424.9 6.8 fusion.65
  431.7 10.6 concatenate.45
  442.3 30.2 %maximum_bitcast_fusion = f32[4,2304,8,128]{3,2,1,0:T(8,128)} fusion(f32[16,147456]{1,0:T(8,128)} %concatenate.45, f32[16,147456]{1,0:T(8,128)} %concatenate.44, f32[32,73728]{1,0:T(8,128)} %reshape_reshape.7, f32[32,73728]{1,0:T(8,128)} %reshape_reshape.6), kind=kLoop, calls=%fused_computation | loop fusion | flops 28311552 | bytes 75497472
  472.5 33.2 %copy.253 = f32[4,2304,8,128]{3,1,2,0:T(8,128)} copy(f32[4,2304,8,128]{3,2,1,0:T(8,128)} %maximum_bitcast_fusion) | data formatting | bytes 75497472
  513.4 3.2 reshape.486
  516.6 3.2 copy.214
  519.8 4.3 fusion.11
  524.2 3.7 copy.215
  527.9 4.3 all-to-all-start.1
  532.3 3.7 fusion.66
  548.1 572.5 %all-reduce.5.cloned.1.call-done = f32[9437184]{0:T(1024)} async-done(((f32[9437184]{0:T(1024)}), f32[9437184]{0:T(1024)}) %all-reduce.5.cloned.1.call-update) | async-done | bytes 37748752
  1127.9 2.2 copy.216
  1130.1 40.7 %all-reduce.2 = (f32[10]{0:T(128)S(1)}, f32[8448]{0:T(1024)S(1)}) all-reduce(f32[10]{0:T(128)S(1)} %pad_maximum_fusion.3, f32[8448]{0:T(1024)} %constant_dynamic-update-slice_fusion.7), channel_id=1, replica_groups=mesh['dp'=8,'fsdp'=4] {'dp','fsdp'}, use_global_device_ids=true, to_apply=%region_24.25 | all-reduce | flops 8458 | bytes 67664 | tf_op jit(solution)/shard_map/psum | solution.py:322
  1174.9 3.2 fusion.72
  1183.0 39.2 %all-reduce.1 = (f32[10]{0:T(128)S(1)}, f32[10]{0:T(128)S(1)}) all-reduce(f32[10]{0:T(128)S(1)} %pad_maximum_fusion.5, f32[10]{0:T(128)S(1)} %pad_maximum_fusion.4), channel_id=1, replica_groups=mesh['dp'=8,'fsdp'=4] {'dp','fsdp'}, use_global_device_ids=true, to_apply=%region_43.44 | all-reduce | flops 20 | bytes 160 | tf_op jit(solution)/shard_map/psum | solution.py:344
  1237.1 6.2 fusion.39
  1243.3 5.0 select_reduce_fusion
  (400 shorter events, 123.6 us)
Async XLA Ops:
  7.2 11.1 copy-start.40
  7.2 81.0 %all-gather.4.cloned.1.call-start = ((), (), s32[]{:S(2)}) async-start(), calls=%async_computation.2 | async-start | bytes 4866048 | tf_op jit(solution)/shard_map/all_gather | solution.py:135
  9.0 10.1 copy-start.6
  9.0 145.2 %all-gather.6.cloned.1.call-start = ((), (), s32[]{:S(2)}) async-start(), calls=%async_computation.3 | async-start | bytes 4866048 | tf_op jit(solution)/shard_map/all_gather | solution.py:136
  10.7 8.9 copy-start.125
  10.7 9.6 copy-start.126
  10.8 10.2 copy-start.76
  10.8 12.8 %copy-start.35 = (bf16[1,4,64,768]{3,2,1,0:T(8,128)(2,1)S(1)}, bf16[1,4,64,768]{3,2,1,0:T(8,128)(2,1)}, u32[]{:S(2)}) copy-start(bf16[1,4,64,768]{3,2,1,0:T(8,128)(2,1)} %param.21) | copy-start | bytes 1179652
  10.8 54.0 %all-to-all-start = ((bf16[1,32,32,768]{3,2,0,1:T(8,128)(2,1)}), bf16[1,32,32,768]{3,2,0,1:T(8,128)(2,1)S(1)}, u32[]{:S(2)}, u32[]{:S(2)}) async-start(bf16[1,32,32,768]{3,2,0,1:T(8,128)(2,1)} %bitcast.176), calls=%async_computation | async-start | bytes 3145728 | tf_op jit(solution)/shard_map/all_to_all | solution.py:145
  18.2 220.3 %all-gather.8.cloned.1.call-start = ((), (), s32[]{:S(2)}) async-start(), calls=%async_computation.4 | async-start | bytes 9732096 | tf_op jit(solution)/shard_map/all_gather | solution.py:137
  19.0 1101.6 %all-reduce.5.cloned.1.call-start = ((), (), s32[]{:S(2)}) async-start(), calls=%async_computation.5 | async-start | bytes 75497472
  19.3 46.7 %copy-start.93 = (f32[256]{0:T(256)}, f32[256]{0:T(256)S(1)}, u32[]{:S(2)}) copy-start(f32[256]{0:T(256)S(1)} %div.199) | copy-start | bytes 3076
  19.7 46.4 %copy-start.98 = (f32[256]{0:T(256)}, f32[256]{0:T(256)S(1)}, u32[]{:S(2)}) copy-start(f32[256]{0:T(256)S(1)} %rsqrt.33) | copy-start | bytes 3076
  20.2 45.8 %copy-start.91 = (f32[4,64]{1,0:T(4,128)}, f32[4,64]{1,0:T(4,128)S(1)}, u32[]{:S(2)}) copy-start(f32[4,64]{1,0:T(4,128)S(1)} %get-tuple-element.119) | copy-start | bytes 3076
  20.3 45.7 %copy-start.95 = (f32[256]{0:T(256)}, f32[256]{0:T(256)S(1)}, u32[]{:S(2)}) copy-start(f32[256]{0:T(256)S(1)} %reshape.482) | copy-start | bytes 3076
  22.8 43.2 %copy-start.87 = (f32[768]{0:T(1024)}, f32[768]{0:T(1024)S(1)}, u32[]{:S(2)}) copy-start(f32[768]{0:T(1024)S(1)} %get-tuple-element.113) | copy-start | bytes 9220
  22.8 140.8 %copy-start.103 = (f32[768]{0:T(1024)}, f32[768]{0:T(1024)S(1)}, u32[]{:S(2)}) copy-start(f32[768]{0:T(1024)S(1)} %get-tuple-element.110) | copy-start | bytes 9220
  97.1 65.1 %copy-start.15 = (bf16[768,768]{1,0:T(8,128)(2,1)}, bf16[768,768]{1,0:T(8,128)(2,1)S(1)}, u32[]{:S(2)}) copy-start(bf16[768,768]{1,0:T(8,128)(2,1)S(1)} %slice.208) | copy-start | bytes 3538948
  103.0 4.3 copy-start.85
  110.9 51.4 %copy-start.45 = (bf16[256,768]{0,1:T(8,128)(2,1)}, bf16[256,768]{0,1:T(8,128)(2,1)S(1)}, u32[]{:S(2)}) copy-start(bf16[256,768]{0,1:T(8,128)(2,1)S(1)} %convert_element_type.154) | copy-start | bytes 1179652
  156.9 5.3 copy-start.7
  184.3 4.4 copy-start.72
  192.1 54.7 %copy-start.47 = (bf16[256,768]{0,1:T(8,128)(2,1)}, bf16[256,768]{0,1:T(8,128)(2,1)S(1)}, u32[]{:S(2)}) copy-start(bf16[256,768]{0,1:T(8,128)(2,1)S(1)} %convert_element_type.163) | copy-start | bytes 1179652
  192.2 4.6 copy-start.73
  192.2 4.6 copy-start.84
  255.1 9.4 copy-start.44
  300.1 16.1 %copy-start.9 = (f32[256,768]{1,0:T(8,128)}, f32[256,768]{1,0:T(8,128)S(1)}, u32[]{:S(2)}) copy-start(f32[256,768]{1,0:T(8,128)S(1)} %add_add_fusion.4) | copy-start | bytes 2359300
  300.1 6.3 copy-start.1
  319.3 5.2 copy-start.34
  339.9 7.7 copy-start.52
  356.9 5.1 copy-start.19
  378.5 8.2 copy-start.61
  378.5 10.7 copy-start.57
  414.0 10.8 copy-start.39
  505.7 5.4 copy-start.92
  505.7 7.7 copy-start.3
  527.9 4.3 copy-start.8
  527.9 4.3 copy-start.88
  527.9 4.3 copy-start.94
  527.9 600.0 %all-to-all-start.1 = ((f32[1,4,256,768]{3,1,0,2:T(4,128)}), f32[1,4,256,768]{3,1,0,2:T(4,128)S(1)}, u32[]{:S(2)}, u32[]{:S(2)}) async-start(f32[1,4,256,768]{3,1,0,2:T(4,128)} %copy.215), calls=%async_computation.1 | async-start | bytes 6291456 | tf_op jit(solution)/shard_map/all_to_all | solution.py:237
  532.2 6.9 copy-start.123
  532.2 8.2 copy-start.122
  532.2 9.5 copy-start.121
  532.3 10.7 copy-start.120
  532.3 13.3 %copy-start.107 = (f32[3072]{0:T(1024)S(1)}, f32[3072]{0:T(1024)}, u32[]{:S(2)}) copy-start(f32[3072]{0:T(1024)} %get-tuple-element.74) | copy-start | bytes 36868
  532.3 14.7 %copy-start.10 = (f32[256,768]{1,0:T(8,128)S(1)}, f32[256,768]{1,0:T(8,128)}, u32[]{:S(2)}) copy-start(f32[256,768]{1,0:T(8,128)} %copy-done.9) | copy-start | bytes 2359300
  1120.6 5.9 copy-start.20
  1127.9 45.6 %copy-start.77 = (f32[8448]{0:T(1024)S(1)}, f32[8448]{0:T(1024)}, u32[]{:S(2)}) copy-start(f32[8448]{0:T(1024)} %param.31) | copy-start | bytes 101380
  1127.9 45.6 %copy-start.89 = (f32[8448]{0:T(1024)S(1)}, f32[8448]{0:T(1024)}, u32[]{:S(2)}) copy-start(f32[8448]{0:T(1024)} %param.32) | copy-start | bytes 101380
  1127.9 45.6 %copy-start.90 = (f32[8448]{0:T(1024)S(1)}, f32[8448]{0:T(1024)}, u32[]{:S(2)}) copy-start(f32[8448]{0:T(1024)} %param.33) | copy-start | bytes 101380
  1170.9 7.2 copy-start.83
  1174.8 4.7 copy-start.54
  1174.8 4.7 copy-start.55
  1174.8 4.7 copy-start.64
  1174.8 4.7 copy-start.65
  1174.9 4.7 copy-start.79
  1174.9 4.7 copy-start.80
  1174.9 4.7 copy-start.81
  1174.9 4.7 copy-start.82
  1179.6 48.4 %copy-start.78 = (f32[8448]{0:T(1024)S(1)}, f32[8448]{0:T(1024)}, u32[]{:S(2)}) copy-start(f32[8448]{0:T(1024)} %param.31) | copy-start | bytes 101380
  1179.6 57.5 %copy-start.14 = (f32[256,768]{1,0:T(8,128)S(1)}, f32[256,768]{1,0:T(8,128)}, u32[]{:S(2)}) copy-start(f32[256,768]{1,0:T(8,128)} %copy-done.11) | copy-start | bytes 2359300
  1237.1 13.4 %copy-start.41 = (f32[147456]{0:T(1024)S(1)}, f32[147456]{0:T(1024)}, u32[]{:S(2)}) copy-start(f32[147456]{0:T(1024)} %param.28) | copy-start | bytes 1769476
  1248.3 4.6 copy-start.67
  1248.3 5.4 copy-start.66
  (71 other events, 168.4 us)
Sparse Core Ops, SparseCore 0:
  11.5 76.6 all-gather.3
  91.7 62.4 all-gather.5
  157.6 80.8 all-gather.7
  505.8 614.7 all-reduce.4
where the time goes:
time: 1280 us; the launch traced here: 1260 us
  waiting for transfers between devices  718 us (56%)
  local copies, waits for them, and re-layouts  235 us (18%)
  other arithmetic  102 us (8%)
  matrix products  85.7 us (7%)
  blocking collectives  79.9 us (6%)
  between operations  29 us (2%)
    unnamed x5, waiting for transfers between devices  573 us
    unnamed x265, local copies, waits for them, and re-layouts  55.1 us
    all_gather x1, waiting for transfers between devices, shards(): lax.all_gather(cross_weights.astype(jnp.bfloat16), ('dp', 'fsdp'), axis=0...  43.2 us
    all_gather x1, waiting for transfers between devices, shards(): lax.all_gather(feed_weights.astype(jnp.bfloat16), ('dp', 'fsdp'), axis=0,...  41.1 us
    psum x1, blocking collectives, shards(): lax.psum((vector_partial, grad_squares, weight_squares), ('dp', 'fsdp'))  40.7 us
    unnamed x10, other arithmetic  39.3 us
    all_to_all x1, waiting for transfers between devices, shards(): lax.all_to_all(memory, 'dp', split_axis=1, concat_axis=2, tiled=True)  39.3 us
    psum x1, blocking collectives, shards(): update_summed = lax.psum(ratio_squares, ('dp', 'fsdp'))  39.2 us
  transfers between devices with their start and end apart: 6, of which 5 were waited for; matrix products, arithmetic and copies ran while one was open for 9% of the time, Pallas kernels for 0%

commit v1 on v0

--- a/solution.py
+++ b/solution.py
@@ -1,6 +1,8 @@
 import jax
 import jax.numpy as jnp
 from jax import lax
+from jax.experimental import pallas as pl
+from jax.experimental.pallas import tpu as pltpu
 from jax.sharding import PartitionSpec as P
 
 D = 768
@@ -409,9 +411,776 @@
     )
 
 
+BF = jnp.bfloat16
+F32 = jnp.float32
+MESH = pl.DeviceIdType.MESH
+NZ = 4
+
+
+def place():
+    dp, fs = lax.axis_index("dp"), lax.axis_index("fsdp")
+    return dp, fs, dp // 2, dp % 2, fs // 2, fs % 2
+
+
+def peer_id(z, y, x, c):
+    return (z * 2 + y, x * 2 + c)
+
+
+def greet(ids):
+    bar = pltpu.get_barrier_semaphore()
+    for where in ids:
+        pl.semaphore_signal(bar, inc=1, device_id=where, device_id_type=MESH)
+    pl.semaphore_wait(bar, len(ids))
+
+
+class Copies:
+    def __init__(self, send, recv, local):
+        self.send, self.recv, self.local = send, recv, local
+        self.remotes, self.locals = 0, 0
+        self.open = []
+
+    def remote(self, src, dst, where):
+        i = self.remotes
+        self.remotes += 1
+        cp = pltpu.make_async_remote_copy(
+            src_ref=src,
+            dst_ref=dst,
+            send_sem=self.send.at[i],
+            recv_sem=self.recv.at[i],
+            device_id=where,
+            device_id_type=MESH,
+        )
+        cp.start()
+        self.open.append(cp)
+        return cp
+
+    def here(self, src, dst):
+        cp = pltpu.make_async_copy(src, dst, self.local.at[self.locals])
+        self.locals += 1
+        cp.start()
+        return cp
+
+    def drain(self):
+        for cp in self.open:
+            cp.wait_send()
+
+
+def gather_kernel(
+    self_in, cross_in, feed_in, mem_in, self_out, cross_out, feed_out, mem_out, send, recv, local
+):
+    dp, fs, z, y, x, c = place()
+    ndp = mem_out.shape[1]
+    ex = mem_out.shape[0]
+    to_y, to_x, to_c = peer_id(z, 1 - y, x, c), peer_id(z, y, 1 - x, c), peer_id(z, y, x, 1 - c)
+    greet([((dp + k) % ndp, fs) for k in range(1, ndp)] + [to_x, to_c])
+    cp = Copies(send, recv, local)
+
+    chunks = []
+    for src, dst, js in (
+        (self_in, self_out, (0, 1)),
+        (cross_in, cross_out, (0, 1)),
+        (feed_in, feed_out, (0, 2)),
+        (feed_in, feed_out, (2, 2)),
+    ):
+        rows = src.shape[1]
+        cut = rows * 2 // 3
+        chunks.append((src, dst, pl.ds(*js), pl.ds(0, cut), pl.ds(cut, rows - cut)))
+
+    own = [cp.here(chunk[0].at[chunk[2]], chunk[1].at[z, y, x, c, chunk[2]]) for chunk in chunks]
+    own_mem = cp.here(mem_in.at[pl.ds(ex * dp, ex)], mem_out.at[:, dp])
+
+    zc, s2, s3, s4 = {}, {}, {}, {}
+
+    def send_z(t):
+        src, dst, js, r0, r1 = chunks[t]
+        for k in range(1, NZ):
+            zc[t, k] = cp.remote(
+                src.at[js], dst.at[z, y, x, c, js], peer_id((z + k) % NZ, y, x, c)
+            )
+
+    def send_2(t, k):
+        src, dst, js, r0, r1 = chunks[t]
+        zz = (z + NZ - k) % NZ
+        for part, rows, where in ((0, r0, to_y), (1, r1, to_x)):
+            here = src.at[js, rows] if k == 0 else dst.at[zz, y, x, c, js, rows]
+            s2[t, k, part] = cp.remote(here, dst.at[zz, y, x, c, js, rows], where)
+
+    def send_3(t):
+        src, dst, js, r0, r1 = chunks[t]
+        s3[t, 0] = cp.remote(
+            dst.at[:, :, x, c, js, r0], dst.at[:, :, x, c, js, r0], to_x
+        )
+        s3[t, 1] = cp.remote(
+            dst.at[:, y, :, c, js, r1], dst.at[:, y, :, c, js, r1], to_y
+        )
+
+    def send_4(t):
+        src, dst, js, r0, r1 = chunks[t]
+        s4[t] = cp.remote(dst.at[:, :, :, c, js], dst.at[:, :, :, c, js], to_c)
+
+    n = len(chunks)
+    for t in range(n):
+        send_z(t)
+        send_2(t, 0)
+    mem = [
+        cp.remote(
+            mem_in.at[pl.ds(ex * ((dp + k) % ndp), ex)],
+            mem_out.at[:, dp],
+            ((dp + k) % ndp, fs),
+        )
+        for k in range(1, ndp)
+    ]
+    for t in range(n + 2):
+        if t < n:
+            for k in range(1, NZ):
+                zc[t, k].wait_recv()
+                send_2(t, k)
+        if 1 <= t <= n:
+            own[t - 1].wait()
+            for k in range(NZ):
+                for part in (0, 1):
+                    s2[t - 1, k, part].wait_recv()
+            send_3(t - 1)
+        if t >= 2:
+            s3[t - 2, 0].wait_recv()
+            s3[t - 2, 1].wait_recv()
+            send_4(t - 2)
+    for t in range(n):
+        s4[t].wait_recv()
+    own_mem.wait()
+    for one in mem:
+        one.wait_recv()
+    cp.drain()
+
+
+def gather_all(self_in, cross_in, feed_in, mem_in, ndp):
+    any_space = pl.BlockSpec(memory_space=pl.ANY)
+    shards_of = lambda a: jax.ShapeDtypeStruct((NZ, 2, 2, 2) + a.shape, BF)
+    ex = mem_in.shape[0] // ndp
+    return pl.pallas_call(
+        gather_kernel,
+        out_shape=[
+            shards_of(self_in),
+            shards_of(cross_in),
+            shards_of(feed_in),
+            jax.ShapeDtypeStruct((ex, ndp) + mem_in.shape[1:], BF),
+        ],
+        in_specs=[any_space] * 4,
+        out_specs=[any_space] * 4,
+        scratch_shapes=[
+            pltpu.SemaphoreType.DMA((72,)),
+            pltpu.SemaphoreType.DMA((72,)),
+            pltpu.SemaphoreType.DMA((8,)),
+        ],
+        compiler_params=pltpu.CompilerParams(collective_id=1, has_side_effects=True),
+        name="gather_all",
+    )(self_in, cross_in, feed_in, mem_in)
+
+
+def squares(v):
+    rows, cols = v.shape
+    w = jnp.sum((v * v).reshape(rows // 8, 8, cols), axis=0)
+    total = w[:, 0:128]
+    for i in range(1, cols // 128):
+        total = total + w[:, i * 128 : (i + 1) * 128]
+    return total
+
+
+def sum_everywhere(cp, mine, slots_a, slots_b, dp, fs):
+    nfs, ndp = slots_a.shape[0], slots_b.shape[0]
+    slots_a[fs] = mine
+    got = [
+        cp.remote(slots_a.at[fs], slots_a.at[fs], (dp, (fs + k) % nfs)) for k in range(1, nfs)
+    ]
+    for one in got:
+        one.wait_recv()
+    total = slots_a[0]
+    for k in range(1, nfs):
+        total = total + slots_a[k]
+    slots_b[dp] = total
+    got = [
+        cp.remote(slots_b.at[dp], slots_b.at[dp], ((dp + k) % ndp, fs)) for k in range(1, ndp)
+    ]
+    for one in got:
+        one.wait_recv()
+    total = slots_b[0]
+    for k in range(1, ndp):
+        total = total + slots_b[k]
+    return total
+
+
+def scatter_kernel(
+    qkv_g, out_g, cq_g, ckv_g, co_g, up_g, dn_g, mem_g, vec,
+    self_t, cross_t, feed_t, mem_t, vec_t, sq_t,
+    send, recv, local,
+    acc_s, acc_c, acc_f0, acc_f1, r1_s, r1_c, r1_f0, r1_f1,
+    r2a_s, r2a_c, r2a_f0, r2a_f1, r2b_s, r2b_c, r2b_f0, r2b_f1,
+    r3a_s, r3a_c, r3a_f0, r3a_f1, r3b_s, r3b_c, r3b_f0, r3b_f1,
+    rz_s, rz_c, rz_f0, rz_f1,
+    v_send, v_recv, v_z, slots_a, slots_b,
+):
+    dp, fs, z, y, x, c = place()
+    ndp = mem_g.shape[1]
+    ex = mem_g.shape[0]
+    to_y, to_x, to_c = peer_id(z, 1 - y, x, c), peer_id(z, y, 1 - x, c), peer_id(z, y, x, 1 - c)
+    nfs = slots_a.shape[0]
+    greet(
+        [((dp + k) % ndp, fs) for k in range(1, ndp)] + [(dp, (fs + k) % nfs) for k in range(1, nfs)]
+    )
+    cp = Copies(send, recv, local)
+
+    def self_src(zz, j, cc):
+        return qkv_g.at[zz, :, :, cc] if zz < 3 else out_g.at[:, :, cc]
+
+    def cross_src(zz, j, cc):
+        if zz == 0:
+            return cq_g.at[:, :, cc]
+        return ckv_g.at[zz - 1, :, :, cc] if zz < 3 else co_g.at[:, :, cc]
+
+    def feed_src(first):
+        def src(zz, j, cc):
+            if zz < 2:
+                return up_g.at[first + j, zz, :, :, cc]
+            return dn_g.at[zz - 2, :, :, cc, first + j]
+
+        return src
+
+    chunks = (
+        (feed_src(0), acc_f0, r1_f0, r2a_f0, r2b_f0, r3a_f0, r3b_f0, rz_f0),
+        (feed_src(2), acc_f1, r1_f1, r2a_f1, r2b_f1, r3a_f1, r3b_f1, rz_f1),
+        (cross_src, acc_c, r1_c, r2a_c, r2b_c, r3a_c, r3b_c, rz_c),
+        (self_src, acc_s, r1_s, r2a_s, r2b_s, r3a_s, r3b_s, rz_s),
+    )
+    n = len(chunks)
+    sc, sl, s1, s2, sz = {}, {}, {}, {}, {}
+
+    vcp = cp.remote(vec, v_recv.at[0], to_c)
+    for t, (src, acc, r1, *_) in enumerate(chunks):
+        for zz in range(NZ):
+            for j in range(acc.shape[3]):
+                sc[t, zz, j] = cp.remote(src(zz, j, 1 - c), r1.at[zz, :, :, j], to_c)
+                sl[t, zz, j] = cp.here(src(zz, j, c), acc.at[zz, :, :, j])
+    own_mem = cp.here(mem_g.at[:, dp], mem_t.at[pl.ds(ex * dp, ex)])
+    mem = [
+        cp.remote(mem_g.at[:, (dp + k) % ndp], mem_t.at[pl.ds(ex * dp, ex)], ((dp + k) % ndp, fs))
+        for k in range(1, ndp)
+    ]
+
+    def cuts(acc):
+        rows = acc.shape[4]
+        cut = rows * 2 // 3
+        return pl.ds(0, cut), pl.ds(cut, rows - cut)
+
+    def add_c(acc, r1, fixed_y, fixed_x, rows):
+        def body(i, _):
+            zz, o = i // 2, i % 2
+            yy = o if fixed_y is None else fixed_y
+            xx = o if fixed_x is None else fixed_x
+            for j in range(acc.shape[3]):
+                acc[zz, yy, xx, j, rows] = acc[zz, yy, xx, j, rows] + r1[zz, yy, xx, j, rows]
+            return 0
+
+        lax.fori_loop(0, NZ * 2, body, 0)
+
+    def phase_c(t):
+        src, acc, r1, r2a, r2b, *_ = chunks[t]
+        r0, r1_rows = cuts(acc)
+        for zz in range(NZ):
+            for j in range(acc.shape[3]):
+                sc[t, zz, j].wait_recv()
+                sl[t, zz, j].wait()
+        add_c(acc, r1, None, 1 - x, r0)
+        s1[t, 0] = cp.remote(acc.at[:, :, 1 - x, :, r0], r2a, to_x)
+        add_c(acc, r1, 1 - y, None, r1_rows)
+        s1[t, 1] = cp.remote(acc.at[:, 1 - y, :, :, r1_rows], r2b, to_y)
+        add_c(acc, r1, None, x, r0)
+        add_c(acc, r1, y, None, r1_rows)
+
+    def phase_1(t):
+        src, acc, r1, r2a, r2b, r3a, r3b, rz = chunks[t]
+        r0, r1_rows = cuts(acc)
+
+        def body_a(yy):
+            def body(zz, _):
+                for j in range(acc.shape[3]):
+                    acc[zz, yy, x, j, r0] = acc[zz, yy, x, j, r0] + r2a[zz, yy, j]
+                return 0
+
+            return body
+
+        def body_b(xx):
+            def body(zz, _):
+                for j in range(acc.shape[3]):
+                    acc[zz, y, xx, j, r1_rows] = acc[zz, y, xx, j, r1_rows] + r2b[zz, xx, j]
+                return 0
+
+            return body
+
+        s1[t, 0].wait_recv()
+        lax.fori_loop(0, NZ, body_a(1 - y), 0)
+        s2[t, 0] = cp.remote(acc.at[:, 1 - y, x, :, r0], r3a, to_y)
+        s1[t, 1].wait_recv()
+        lax.fori_loop(0, NZ, body_b(1 - x), 0)
+        s2[t, 1] = cp.remote(acc.at[:, y, 1 - x, :, r1_rows], r3b, to_x)
+        lax.fori_loop(0, NZ, body_a(y), 0)
+        lax.fori_loop(0, NZ, body_b(x), 0)
+
+    def phase_2(t):
+        src, acc, r1, r2a, r2b, r3a, r3b, rz = chunks[t]
+        r0, r1_rows = cuts(acc)
+        s2[t, 0].wait_recv()
+        s2[t, 1].wait_recv()
+
+        def body(zz, _):
+            for j in range(acc.shape[3]):
+                acc[zz, y, x, j, r0] = acc[zz, y, x, j, r0] + r3a[zz, j]
+                acc[zz, y, x, j, r1_rows] = acc[zz, y, x, j, r1_rows] + r3b[zz, j]
+            return 0
+
+        lax.fori_loop(0, NZ, body, 0)
+        for k in range(1, NZ):
+            zt = (z + k) % NZ
+            sz[t, k] = cp.remote(acc.at[zt, y, x], rz.at[k - 1], peer_id(zt, y, x, c))
+
+    sums = []
+
+    def phase_z(t, out, first):
+        src, acc, r1, r2a, r2b, r3a, r3b, rz = chunks[t]
+        for k in range(1, NZ):
+            sz[t, k].wait_recv()
+        for j in range(acc.shape[3]):
+            total = acc[z, y, x, j].astype(F32)
+            for k in range(1, NZ):
+                total = total + rz[k - 1, j].astype(F32)
+            out[first + j] = total
+            sums.append(squares(total))
+
+    def vec_step(i):
+        nonlocal vcp
+        vcp.wait_recv()
+        if i < 3:
+            before = vec[...] if i == 0 else v_send[i - 1]
+            v_send[i] = before + v_recv[i]
+            if i < 2:
+                vcp = cp.remote(v_send.at[i], v_recv.at[i + 1], (to_x, to_y)[i])
+
+    for t in range(n + 3):
+        if t < n:
+            phase_c(t)
+        if t < 3:
+            vec_step(t)
+        if t == 2:
+            v_z[z] = v_send[2]
+            vz = [
+                cp.remote(v_send.at[2], v_z.at[z], peer_id((z + k) % NZ, y, x, c))
+                for k in range(1, NZ)
+            ]
+        if 1 <= t <= n:
+            phase_1(t - 1)
+        if 2 <= t <= n + 1:
+            phase_2(t - 2)
+        if t >= 3:
+            phase_z(t - 3, (feed_t, feed_t, cross_t, self_t)[t - 3], (0, 2, 0, 0)[t - 3])
+    for one in vz:
+        one.wait_recv()
+    vec_t[...] = (v_z[0] + v_z[1]) + (v_z[2] + v_z[3])
+    total = sums[0]
+    for one in sums[1:]:
+        total = total + one
+    sq_t[...] = sum_everywhere(cp, total, slots_a, slots_b, dp, fs)
+    own_mem.wait()
+    for one in mem:
+        one.wait_recv()
+    cp.drain()
+
+
+def scatter_all(grads, mem_g, vec, rows_a, rows_f, ndp, nfs):
+    any_space = pl.BlockSpec(memory_space=pl.ANY)
+    vmem = pl.BlockSpec(memory_space=pltpu.VMEM)
+    ex, _, pos, width = mem_g.shape
+    kinds = ((1, rows_a), (1, rows_a), (2, rows_f), (2, rows_f))
+    acc = [pltpu.VMEM((NZ, 2, 2, j, r, width), BF) for j, r in kinds]
+    r2a = [pltpu.VMEM((NZ, 2, j, r * 2 // 3, width), BF) for j, r in kinds]
+    r2b = [pltpu.VMEM((NZ, 2, j, r - r * 2 // 3, width), BF) for j, r in kinds]
+    r3a = [pltpu.VMEM((NZ, j, r * 2 // 3, width), BF) for j, r in kinds]
+    r3b = [pltpu.VMEM((NZ, j, r - r * 2 // 3, width), BF) for j, r in kinds]
+    rz = [pltpu.VMEM((NZ - 1, j, r, width), BF) for j, r in kinds]
+    return pl.pallas_call(
+        scatter_kernel,
+        out_shape=[
+            jax.ShapeDtypeStruct((1, rows_a, width), F32),
+            jax.ShapeDtypeStruct((1, rows_a, width), F32),
+            jax.ShapeDtypeStruct((4, rows_f, width), F32),
+            jax.ShapeDtypeStruct((ndp * ex, pos, width), BF),
+            jax.ShapeDtypeStruct(vec.shape, F32),
+            jax.ShapeDtypeStruct((8, 128), F32),
+        ],
+        in_specs=[any_space] * 8 + [vmem],
+        out_specs=[vmem, vmem, vmem, any_space, vmem, vmem],
+        scratch_shapes=[
+            pltpu.SemaphoreType.DMA((80,)),
+            pltpu.SemaphoreType.DMA((80,)),
+            pltpu.SemaphoreType.DMA((32,)),
+            *acc,
+            *acc,
+            *r2a,
+            *r2b,
+            *r3a,
+            *r3b,
+            *rz,
+            pltpu.VMEM((3,) + vec.shape, F32),
+            pltpu.VMEM((3,) + vec.shape, F32),
+            pltpu.VMEM((NZ,) + vec.shape, F32),
+            pltpu.VMEM((nfs, 8, 128), F32),
+            pltpu.VMEM((ndp, 8, 128), F32),
+        ],
+        compiler_params=pltpu.CompilerParams(
+            collective_id=2, has_side_effects=True, vmem_limit_bytes=58 << 20
+        ),
+        name="scatter_all",
+    )(*grads, mem_g, vec)
+
+
+def ratio_kernel(
+    gs, gc, gf, ws, wc, wf, ms, mc, mf, vs, vc, vf, clip, out, send, recv, local, slots_a, slots_b
+):
+    dp, fs, z, y, x, c = place()
+    nfs, ndp = slots_a.shape[0], slots_b.shape[0]
+    greet(
+        [((dp + k) % ndp, fs) for k in range(1, ndp)] + [(dp, (fs + k) % nfs) for k in range(1, nfs)]
+    )
+    cp = Copies(send, recv, local)
+    factor = clip[0:1, 0:1]
+    rows = lax.broadcasted_iota(jnp.int32, (32, 128), 0)
+    tile = jnp.zeros((32, 128), F32)
+    for g, w, m, v, row in (
+        (gs, ws, ms, vs, z),
+        (gc, wc, mc, vc, NZ + z),
+        (gf, wf, mf, vf, 2 * NZ + z // 2),
+    ):
+        ratio = lamb_step(w[...], g[...], m[...], v[...], factor)[2]
+        for first, a in ((0, ratio), (16, w[...])):
+            part = jnp.sum(a * a, axis=0, keepdims=True)
+            tile = tile + jnp.where(rows == first + row, part, 0.0)
+    out[...] = sum_everywhere(cp, tile, slots_a, slots_b, dp, fs)
+    cp.drain()
+
+
+def ratio_all(args, clip, ndp, nfs):
+    vmem = pl.BlockSpec(memory_space=pltpu.VMEM)
+    return pl.pallas_call(
+        ratio_kernel,
+        out_shape=jax.ShapeDtypeStruct((32, 128), F32),
+        in_specs=[vmem] * 13,
+        out_specs=vmem,
+        scratch_shapes=[
+            pltpu.SemaphoreType.DMA((16,)),
+            pltpu.SemaphoreType.DMA((16,)),
+            pltpu.SemaphoreType.DMA((1,)),
+            pltpu.VMEM((nfs, 32, 128), F32),
+            pltpu.VMEM((ndp, 32, 128), F32),
+        ],
+        compiler_params=pltpu.CompilerParams(
+            collective_id=3, has_side_effects=True, vmem_limit_bytes=40 << 20
+        ),
+        name="ratio_all",
+    )(*args, clip)
+
+
+def fast_shards(
+    suffix,
+    memory,
+    prefix_lengths,
+    suffix_lengths,
+    cotangent,
+    self_weights,
+    self_moment,
+    self_second,
+    cross_weights,
+    cross_moment,
+    cross_second,
+    feed_weights,
+    feed_moment,
+    feed_second,
+    vectors,
+    vector_moment,
+    vector_second,
+):
+    row_count = EX_DEV * SUF
+    ndp, nfs = lax.axis_size("dp"), lax.axis_size("fsdp")
+    owners = ndp * nfs
+    attn_shard, feed_shard = self_weights.shape[0], feed_weights.shape[0]
+    rows_a, rows_f = attn_shard // D, feed_shard // (4 * D)
+    shard_index = lax.axis_index(("dp", "fsdp"))
+    feed_low = feed_weights.astype(BF)
+    feed_in = jnp.where(
+        shard_index < owners // 2,
+        feed_low.reshape(rows_f, 4, D).transpose(1, 0, 2),
+        feed_low.reshape(4, rows_f, D),
+    )
+    self_full, cross_full, feed_full, own_memory = gather_all(
+        self_weights.astype(BF).reshape(1, rows_a, D),
+        cross_weights.astype(BF).reshape(1, rows_a, D),
+        feed_in,
+        memory[0],
+        ndp,
+    )
+    self_mats = self_full.reshape(4, D, D)
+    cross_mats = cross_full.reshape(4, D, D)
+    feed_full = feed_full.reshape(2, owners // 2, 4, rows_f, D)
+    up_mats = feed_full[0].transpose(1, 0, 2, 3).reshape(4, D, D)
+    down_mat = feed_full[1].reshape(FF, D)
+    memory_rows = own_memory.reshape(EX_DEV * MEMLEN, D)
+    vector_parts = [vectors[segment * D : (segment + 1) * D] for segment in range(7)]
+    bias_up = vectors[7 * D :]
+    suffix_len = suffix_lengths[0]
+    prefix_len = prefix_lengths[0]
+    positions = jnp.arange(SUF, dtype=jnp.int32)
+    causal = positions[:, None] >= positions[None, :]
+    self_allowed = (
+        causal[None, None, :, :] & (positions[None, :] < suffix_len[:, None])[:, None, None, :]
+    )
+    memory_pos = jnp.arange(MEMLEN, dtype=jnp.int32)
+    cross_allowed = (memory_pos[None, :] < (PATCH + prefix_len)[:, None])[:, None, None, :]
+    inputs = suffix.reshape(row_count, D).astype(jnp.float32)
+    normed_one = layer_norm(inputs, vector_parts[0], vector_parts[1]).astype(jnp.bfloat16)
+    self_qkv = jnp.einsum(
+        "rd,jde->jre", normed_one, self_mats[0:3], preferred_element_type=jnp.float32
+    ).astype(jnp.bfloat16)
+    self_heads = self_qkv.reshape(3, EX_DEV, SUF, H, HD)
+    mixed_one, totals_one = attend_forward(
+        self_heads[0], self_heads[1], self_heads[2], self_allowed
+    )
+    mixed_one = mixed_one.reshape(row_count, D).astype(jnp.bfloat16)
+    hidden_one = inputs + jnp.dot(mixed_one, self_mats[3], preferred_element_type=jnp.float32)
+    normed_two = layer_norm(hidden_one, vector_parts[2], vector_parts[3]).astype(jnp.bfloat16)
+    cross_query = jnp.dot(normed_two, cross_mats[0], preferred_element_type=jnp.float32).astype(
+        jnp.bfloat16
+    )
+    cross_kv = jnp.einsum(
+        "rd,jde->jre", memory_rows, cross_mats[1:3], preferred_element_type=jnp.float32
+    ).astype(jnp.bfloat16)
+    query_heads = cross_query.reshape(EX_DEV, SUF, H, HD)
+    kv_heads = cross_kv.reshape(2, EX_DEV, MEMLEN, H, HD)
+    mixed_two, totals_two = attend_forward(query_heads, kv_heads[0], kv_heads[1], cross_allowed)
+    mixed_two = mixed_two.reshape(row_count, D).astype(jnp.bfloat16)
+    hidden_two = hidden_one + jnp.dot(mixed_two, cross_mats[3], preferred_element_type=jnp.float32)
+    normed_three = layer_norm(hidden_two, vector_parts[4], vector_parts[5]).astype(jnp.bfloat16)
+    pre_act = (
+        jnp.einsum(
+            "rd,jde->jre", normed_three, up_mats, preferred_element_type=jnp.float32
+        )
+        + bias_up.reshape(4, 1, D)
+    )
+    activated = gelu_tanh(pre_act).astype(jnp.bfloat16)
+    layer_output = hidden_two + (
+        jnp.einsum(
+            "jre,jed->rd", activated, down_mat.reshape(4, D, D), preferred_element_type=jnp.float32
+        )
+        + vector_parts[6]
+    )
+    valid_rows = (positions[None, :] < suffix_len[:, None]).astype(jnp.float32)
+    seed_rows = (
+        cotangent.reshape(EX_DEV, SUF, D).astype(jnp.float32) * valid_rows[:, :, None]
+    ).reshape(row_count, D)
+    seed_low = seed_rows.astype(jnp.bfloat16)
+    bias_down_grad = jnp.sum(seed_low.astype(jnp.float32), axis=0)
+    down_grad = jnp.einsum(
+        "jre,rd->jed", activated, seed_low, preferred_element_type=jnp.float32
+    ).astype(BF)
+    activated_grad = jnp.einsum(
+        "rd,jed->jre", seed_low, down_mat.reshape(4, D, D), preferred_element_type=jnp.float32
+    )
+    _, gelu_back = jax.vjp(gelu_tanh, pre_act)
+    pre_grad = gelu_back(activated_grad)[0].astype(jnp.bfloat16)
+    bias_up_grad = jnp.sum(pre_grad.astype(jnp.float32), axis=1).reshape(FF)
+    up_grad = jnp.einsum(
+        "rd,jre->jde", normed_three, pre_grad, preferred_element_type=jnp.float32
+    ).astype(BF)
+    normed_three_grad = jnp.einsum(
+        "jre,jde->rd", pre_grad, up_mats, preferred_element_type=jnp.float32
+    )
+    _, norm_three_back = jax.vjp(layer_norm, hidden_two, vector_parts[4], vector_parts[5])
+    through_three, gain_three_grad, shift_three_grad = norm_three_back(normed_three_grad)
+    hidden_two_grad = seed_rows + through_three
+    branch_two = hidden_two_grad.astype(jnp.bfloat16)
+    cross_out_grad = jnp.einsum(
+        "rd,re->de", mixed_two, branch_two, preferred_element_type=jnp.float32
+    ).astype(BF)
+    mixed_two_grad = jnp.einsum(
+        "re,de->rd", branch_two, cross_mats[3], preferred_element_type=jnp.float32
+    ).astype(jnp.bfloat16)
+    query_two_grad, key_two_grad, value_two_grad = attend_backward(
+        query_heads,
+        kv_heads[0],
+        kv_heads[1],
+        cross_allowed,
+        totals_two,
+        mixed_two_grad.reshape(EX_DEV, SUF, H, HD),
+    )
+    cross_query_grad = query_two_grad.reshape(row_count, D).astype(jnp.bfloat16)
+    cross_kv_grad = (
+        jnp.stack([key_two_grad, value_two_grad])
+        .reshape(2, EX_DEV * MEMLEN, D)
+        .astype(jnp.bfloat16)
+    )
+    query_weight_grad = jnp.einsum(
+        "rd,re->de", normed_two, cross_query_grad, preferred_element_type=jnp.float32
+    ).astype(BF)
+    kv_weight_grad = jnp.einsum(
+        "rd,jre->jde", memory_rows, cross_kv_grad, preferred_element_type=jnp.float32
+    ).astype(BF)
+    normed_two_grad = jnp.einsum(
+        "re,de->rd", cross_query_grad, cross_mats[0], preferred_element_type=jnp.float32
+    )
+    memory_local_grad = jnp.einsum(
+        "jre,jde->rd", cross_kv_grad, cross_mats[1:3], preferred_element_type=jnp.float32
+    ).astype(BF)
+    _, norm_two_back = jax.vjp(layer_norm, hidden_one, vector_parts[2], vector_parts[3])
+    through_two, gain_two_grad, shift_two_grad = norm_two_back(normed_two_grad)
+    hidden_one_grad = hidden_two_grad + through_two
+    branch_one = hidden_one_grad.astype(jnp.bfloat16)
+    self_out_grad = jnp.einsum(
+        "rd,re->de", mixed_one, branch_one, preferred_element_type=jnp.float32
+    ).astype(BF)
+    mixed_one_grad = jnp.einsum(
+        "re,de->rd", branch_one, self_mats[3], preferred_element_type=jnp.float32
+    ).astype(jnp.bfloat16)
+    query_one_grad, key_one_grad, value_one_grad = attend_backward(
+        self_heads[0],
+        self_heads[1],
+        self_heads[2],
+        self_allowed,
+        totals_one,
+        mixed_one_grad.reshape(EX_DEV, SUF, H, HD),
+    )
+    self_qkv_grad = (
+        jnp.stack([query_one_grad, key_one_grad, value_one_grad])
+        .reshape(3, row_count, D)
+        .astype(jnp.bfloat16)
+    )
+    qkv_weight_grad = jnp.einsum(
+        "rd,jre->jde", normed_one, self_qkv_grad, preferred_element_type=jnp.float32
+    ).astype(BF)
+    normed_one_grad = jnp.einsum(
+        "jre,jde->rd", self_qkv_grad, self_mats[0:3], preferred_element_type=jnp.float32
+    )
+    _, norm_one_back = jax.vjp(layer_norm, inputs, vector_parts[0], vector_parts[1])
+    through_one, gain_one_grad, shift_one_grad = norm_one_back(normed_one_grad)
+    suffix_gradient = (hidden_one_grad + through_one).reshape(1, EX_DEV, SUF, D)
+    vector_partial = jnp.concatenate(
+        [
+            gain_one_grad,
+            shift_one_grad,
+            gain_two_grad,
+            shift_two_grad,
+            gain_three_grad,
+            shift_three_grad,
+            bias_down_grad,
+            bias_up_grad,
+        ]
+    )
+    vec_rows = vectors.shape[0] // 128
+    vec_pad = (vec_rows + 7) // 8 * 8
+    vector_in = jnp.pad(vector_partial.reshape(vec_rows, 128), ((0, vec_pad - vec_rows), (0, 0)))
+    split = (2, 2, 2)
+    self_total, cross_total, feed_total, memory_back, vec_sum, squared = scatter_all(
+        (
+            qkv_weight_grad.reshape((3,) + split + (rows_a, D)),
+            self_out_grad.reshape(split + (rows_a, D)),
+            query_weight_grad.reshape(split + (rows_a, D)),
+            kv_weight_grad.reshape((2,) + split + (rows_a, D)),
+            cross_out_grad.reshape(split + (rows_a, D)),
+            up_grad.reshape((4, 2) + split + (rows_f, D)),
+            down_grad.reshape((2,) + split + (4, rows_f, D)),
+        ),
+        memory_local_grad.reshape(EX_DEV, ndp, MEMLEN // ndp, D),
+        vector_in,
+        rows_a,
+        rows_f,
+        ndp,
+        nfs,
+    )
+    memory_gradient = memory_back.astype(F32)[None]
+    self_total = self_total.reshape(-1)
+    cross_total = cross_total.reshape(-1)
+    feed_total = jnp.where(
+        shard_index < owners // 2, feed_total.transpose(1, 0, 2).reshape(-1), feed_total.reshape(-1)
+    )
+    vector_total = vec_sum[:vec_rows].reshape(-1)
+    squared_total = jnp.sum(squared) + jnp.sum(vector_total * vector_total)
+    global_norm = jnp.sqrt(squared_total)
+    clip_factor = jnp.minimum(1.0, 1.0 / global_norm)
+    flat = lambda *group: [a.reshape(-1, 128) for a in group]
+    sums = ratio_all(
+        flat(
+            self_total, cross_total, feed_total,
+            self_weights, cross_weights, feed_weights,
+            self_moment, cross_moment, feed_moment,
+            self_second, cross_second, feed_second,
+        ),
+        jnp.broadcast_to(clip_factor, (8, 128)),
+        ndp,
+        nfs,
+    )
+    norms = jnp.sqrt(jnp.sum(sums, axis=1))
+    ratio_norms, weight_norms = norms[0:10], norms[16:26]
+    trust_ratio = weight_norms / (ratio_norms + trust_eps)
+    z = shard_index // 8
+    new = []
+    for weights, total, moment, second, row in (
+        (self_weights, self_total, self_moment, self_second, z),
+        (cross_weights, cross_total, cross_moment, cross_second, 4 + z),
+        (feed_weights, feed_total, feed_moment, feed_second, 8 + z // 2),
+    ):
+        momentum, variance, ratio = lamb_step(weights, total, moment, second, clip_factor)
+        new += [total, momentum, variance, weights - learn_rate * trust_ratio[row] * ratio]
+    vector_momentum, vector_variance, vector_ratio = lamb_step(
+        vectors, vector_total, vector_moment, vector_second, clip_factor
+    )
+    edges = [0, D, 2 * D, 3 * D, 4 * D, 5 * D, 6 * D, 7 * D, 7 * D + FF]
+    vector_wn = []
+    vector_rn = []
+    new_pieces = []
+    for segment in range(8):
+        weight_part = vectors[edges[segment] : edges[segment + 1]]
+        ratio_part = vector_ratio[edges[segment] : edges[segment + 1]]
+        weight_norm = jnp.sqrt(jnp.sum(weight_part * weight_part))
+        ratio_norm = jnp.sqrt(jnp.sum(ratio_part * ratio_part))
+        piece_trust = weight_norm / (ratio_norm + trust_eps)
+        vector_wn.append(weight_norm)
+        vector_rn.append(ratio_norm)
+        new_pieces.append(weight_part - learn_rate * piece_trust * ratio_part)
+    vector_master = jnp.concatenate(new_pieces)
+    tensor_norms = jnp.stack(
+        [
+            jnp.concatenate([weight_norms, jnp.stack(vector_wn)]),
+            jnp.concatenate([ratio_norms, jnp.stack(vector_rn)]),
+        ]
+    )
+    return (
+        layer_output.reshape(1, EX_DEV, SUF, D),
+        suffix_gradient,
+        memory_gradient,
+        *new,
+        vector_total,
+        vector_momentum,
+        vector_variance,
+        vector_master,
+        tensor_norms,
+        global_norm,
+    )
+
+
+def pick(mesh):
+    if mesh.shape["dp"] == 8 and mesh.shape["fsdp"] == 4:
+        return fast_shards
+    return shards
+
+
 def solution(mesh):
     return jax.shard_map(
-        shards,
+        pick(mesh),
         mesh=mesh,
         in_specs=(
             P("fsdp", "dp", None, None),

time: 1280 us -> 546 us (0.43)
  waiting for transfers between devices: 718 us -> 0 us
  Pallas kernels: 0 us -> 269 us
  local copies, waits for them, and re-layouts: 235 us -> 110 us
  blocking collectives: 79.9 us -> 0 us
  other arithmetic: 102 us -> 57 us
    unnamed x5 -> x0, waiting for transfers between devices: 573 us -> none
    pallas_call x0 -> x3, Pallas kernels: none -> 269 us  [the longest x1 130 us: gather_all(): pl.pallas_call(gather_kernel, out_shape=[shards_of(self_in), shards_of(cr...]
    all_gather x3 -> x0, waiting for transfers between devices: 107 us -> none  [the longest x1 43.2 us: shards(): lax.all_gather(cross_weights.astype(jnp.bfloat16), ('dp', 'fsdp'), axis=0...]
    psum x2 -> x0, blocking collectives: 79.9 us -> none  [the longest x1 40.7 us: shards(): lax.psum((vector_partial, grad_squares, weight_squares), ('dp', 'fsdp'))]
    concatenate x7 -> x3, local copies, waits for them, and re-layouts: 42.3 us -> 0.18 us  [the longest x1 0.08 us: fast_shards(): jnp.concatenate([ratio_norms, jnp.stack(vector_rn)])]
    unnamed x265 -> x231, local copies, waits for them, and re-layouts: 55.1 us -> 13.7 us
    all_to_all x2 -> x0, waiting for transfers between devices: 39.3 us -> none  [the longest x1 39.3 us: shards(): lax.all_to_all(memory, 'dp', split_axis=1, concat_axis=2, tiled=True)]
    slice x19 -> x8, local copies, waits for them, and re-layouts: 51.9 us -> 20.2 us  [the longest x1 8.46 us: fast_shards(): up_mats = feed_full[0].transpose(1, 0, 2, 3).reshape(4, D, D)]
  transfers between devices with their start and end apart: 6 -> 0, of which waited for: 5 -> 0; matrix products, arithmetic and copies ran while one was open for 9% -> 0% of each run, Pallas kernels for 0% -> 0%
where the time goes in v1:
time: 546 us; the launch traced here: 540 us
  Pallas kernels  269 us (49%)
  local copies, waits for them, and re-layouts  110 us (20%)
  matrix products  85.8 us (16%)
  other arithmetic  57 us (10%)
  between operations  17.9 us (3%)
    pallas_call x1, Pallas kernels, gather_all(): pl.pallas_call(gather_kernel, out_shape=[shards_of(self_in), shards_of(cr...  130 us
    pallas_call x1, Pallas kernels, scatter_all(): pl.pallas_call(scatter_kernel, out_shape=[jax.ShapeDtypeStruct((1, rows_a...  128 us
    another operation x7, local copies, waits for them, and re-layouts, fast_shards(): jnp.stack([query_one_grad, key_one_grad, value_one_grad])  15.2 us
    unnamed x231, local copies, waits for them, and re-layouts  13.7 us
    pallas_call x1, Pallas kernels, ratio_all(): pl.pallas_call(ratio_kernel, out_shape=jax.ShapeDtypeStruct((32, 128), F3...  11 us

profile of v1, /device:TPU:0, one launch (start us, length us, event | category | flops | bytes accessed | tf_op | source)
XLA Modules:
  0.0 539.9 jit_solution(7978185199530518499)
XLA Ops:
  6.5 129.7 %gather_all.1 = (bf16[4,2,2,2,1,96,768]{6,5,4,3,2,1,0:T(8,128)(2,1)}, bf16[4,2,2,2,1,96,768]{6,5,4,3,2,1,0:T(8,128)(2,1)}, bf16[4,2,2,2,4,48,768]{6,5,4,3,2,1,0:T(8,128)(2,1)}, bf16[4,8,32,768]{3,2,1,0:T(8,128)(2,1)}) custom-call(bf16[1,96,768]{2,1,0:T(8,128)(2,1)} %reshape.510.self_in, bf16[1,96,768]{2,1,0:T(8,128)(2,1)} %reshape.511.cross_in, ...), custom_call_target="tpu_custom_call" | custom-call | tf_op jit(solution)/shard_map/gather_all/pallas_call | solution.py:560
  136.2 2.4 slice.137
  138.6 1.7 multiply_reduce_fusion.15
  153.0 3.1 fusion.83
  158.4 1.6 copy.107
  159.9 2.0 slice.145
  162.0 2.9 convert_bitcast_fusion
  166.4 2.4 squeeze.49
  168.8 2.6 fusion.90
  172.1 2.6 exponential_reduce_fusion
  174.7 4.4 squeeze.47
  179.1 2.6 fusion.38
  181.7 1.5 copy.81
  183.2 2.5 convert_element_type.217
  185.7 3.6 fusion.91
  189.2 8.5 %fusion.82 = (bf16[2,2,2,2,4,48,768]{6,5,4,3,2,1,0:T(8,128)(2,1)}, bf16[2,2,2,2,4,48,768]{6,5,4,3,2,1,0:T(8,128)(2,1)}) fusion(bf16[4,2,2,2,4,48,768]{6,5,4,3,2,1,0:T(8,128)(2,1)} %get-tuple-element.34), kind=kLoop, calls=%fused_computation.215 | loop fusion | bytes 18874368 | tf_op jit(solution)/shard_map/slice | solution.py:931
  203.9 2.8 copy.82
  206.7 3.2 fusion.70
  209.9 1.9 multiply_reduce_fusion.13
  213.2 1.9 convert_reduce_fusion.1
  215.1 7.6 %convert_reduce_fusion = (f32[4,768]{1,0:T(4,128)}, bf16[4,256,768]{2,1,0:T(8,128)(2,1)S(1)}) fusion(f32[4,768,256]{1,2,0:T(8,128)} %fusion.70, f32[4,768]{1,0:T(4,128)} %slice.157, bf16[4,768,768]{2,1,0:T(8,128)(2,1)} %bitcast.263, bf16[256,768,1]{1,0,2:T(8,128)(2,1)S(1)} %bitcast.276), kind=kOutput, calls=%fused_computation.18 | convolution fusion | flops 1226044416 | bytes 9854976 | tf_op jit(solution)/shard_map/rd,jed->jre/dot_general | solution.py:991
  222.7 2.1 multiply_reduce_fusion.2
  229.0 2.4 reshape.567
  231.4 2.5 copy.109
  233.9 3.1 multiply_reduce_fusion
  240.9 2.2 copy.88
  243.2 2.5 convert_element_type.234
  245.7 3.0 multiply_reduce_fusion.3
  252.3 2.5 reshape.568
  254.8 2.5 copy.100
  257.3 2.5 multiply_reduce_fusion.1
  261.8 1.6 copy.131
  263.4 2.5 reshape.563
  265.9 1.8 constant_dynamic-update-slice_fusion.2
  267.7 1.9 fusion.37
  269.6 1.5 copy.132
  271.2 2.5 reshape.564
  273.7 1.8 constant_dynamic-update-slice_fusion.1
  275.5 3.1 fusion.32
  278.5 2.6 copy.133
  281.1 2.7 reshape.565
  283.8 1.8 constant_dynamic-update-slice_fusion
  286.9 4.9 fusion.75
  293.9 2.2 multiply_reduce_fusion.4
  296.0 2.7 add_convert_fusion
  298.7 2.9 convolution_convert_fusion.2
  301.7 1.5 convolution_convert_fusion.6
  303.2 1.7 convolution_convert_fusion.5
  308.0 1.6 copy.112
  309.6 2.0 fusion.19
  314.0 2.0 copy.111
  316.0 6.1 %fusion.15 = bf16[2,768,768]{1,2,0:T(8,128)(2,1)} fusion(bf16[1024,768,1]{1,0,2:T(8,128)(2,1)} %bitcast.282, bf16[1,1024,768]{2,1,0:T(8,128)(2,1)S(1)} %copy-done.51, bf16[1,1024,768]{2,1,0:T(8,128)(2,1)} %copy.111), kind=kOutput, calls=%fused_computation.35 | convolution fusion | flops 2418671616 | bytes 7077888 | tf_op jit(solution)/shard_map/rd,jre->jde/dot_general | solution.py:1030
  322.1 1.6 convolution_convert_fusion.4
  323.7 3.7 convolution_convert_fusion.1
  327.5 4.5 convolution_convert_fusion
  332.1 3.8 bitcast_convert_fusion
  336.7 128.1 %scatter_all.1 = (f32[1,96,768]{2,1,0:T(8,128)}, f32[1,96,768]{2,1,0:T(8,128)}, f32[4,48,768]{2,1,0:T(8,128)}, bf16[32,32,768]{2,1,0:T(8,128)(2,1)}, f32[72,128]{1,0:T(8,128)}, /*index=5*/f32[8,128]{1,0:T(8,128)}) custom-call(bf16[3,2,2,2,96,768]{5,4,3,2,1,0:T(8,128)(2,1)} %bitcast.254, bf16[2,2,2,96,768]{4,3,2,1,0:T(8,128)(2,1)} %bitcast.260, ...), custom_call_target="tpu_custom_call" | custom-call | tf_op jit(solution)/shard_map/scatter_all/pallas_call | solution.py:808
  489.8 6.3 %fusion.42 = f32[256,768]{1,0:T(8,128)} fusion(f32[256,768]{1,0:T(8,128)S(1)} %copy-done.18, bf16[4,768,768]{2,1,0:T(8,128)(2,1)} %bitcast.264, f32[768]{0:T(1024)S(1)} %get-tuple-element.103, f32[4,768,256]{1,2,0:T(8,128)} %fusion.70, f32[4,768]{1,0:T(4,128)S(1)} %copy-done.89), kind=kOutput, calls=%fused_computation.78 | convolution fusion | flops 1216217088 | bytes 9452544 | tf_op jit(solution)/shard_map/jre,jed->rd/dot_general | solution.py:977
  496.2 2.0 bitcast_convert_fusion.1
  501.7 2.3 reshape.532
  504.0 1.9 reshape.533
  509.1 11.0 %ratio_all.1 = f32[32,128]{1,0:T(8,128)S(1)} custom-call(f32[576,128]{1,0:T(8,128)S(1)} %copy-done.9, f32[576,128]{1,0:T(8,128)S(1)} %copy-done.10, f32[1152,128]{1,0:T(8,128)S(1)} %broadcast_select_fusion.1.gf, f32[576,128]{1,0:T(8,128)S(1)} %bitcast.240, f32[576,128]{1,0:T(8,128)S(1)} %bitcast.241, f32[1152,128]{1,0:T(8,128)S(1)} %bitcast.238, ...), custom_call_target="tpu_custom_call" | custom-call | tf_op jit(solution)/shard_map/ratio_all/pallas_call | solution.py:871
  522.7 1.7 reshape.543
  525.1 2.5 multiply_subtract_fusion.1
  (335 shorter events, 84.5 us)
Async XLA Ops:
  136.2 4.1 copy-start.20
  138.6 4.2 copy-start.34
  144.1 4.1 copy-start.42
  144.5 3.7 copy-start.44
  144.8 3.4 copy-start.43
  149.9 3.1 copy-start.35
  153.0 3.4 copy-start.13
  153.0 4.1 copy-start.85
  156.3 3.6 copy-start.98
  202.5 4.2 copy-start.76
  206.7 3.2 copy-start.19
  213.2 9.5 %slice-start = ((s8[4718592]{0:T(1024)(128)(4,1)}), s8[4194304]{0:T(1024)(128)(4,1)S(1)}, s32[]{:S(2)}) async-start(s8[4718592]{0:T(1024)(128)(4,1)} %bitcast.248), calls=%async_computation | async-start | bytes 8388608
  215.1 7.6 %copy-start.17 = (f32[256,768]{1,0:T(8,128)S(1)}, f32[256,768]{1,0:T(8,128)}, u32[]{:S(2)}) copy-start(f32[256,768]{1,0:T(8,128)} %get-tuple-element.129) | copy-start | bytes 2359300
  215.1 7.6 %slice-start.1 = ((s8[4718592]{0:T(1024)(128)(4,1)}), s8[524288]{0:T(1024)(128)(4,1)S(1)}, s32[]{:S(2)}) async-start(s8[4718592]{0:T(1024)(128)(4,1)} %bitcast.248), calls=%async_computation.1 | async-start | bytes 1048576
  215.1 7.6 %copy-start.77 = (f32[256]{0:T(256)S(1)}, f32[256]{0:T(256)}, u32[]{:S(2)}) copy-start(f32[256]{0:T(256)} %copy-done.76) | copy-start | bytes 3076
  215.1 7.6 %copy-start.83 = (f32[256]{0:T(256)S(1)}, f32[256]{0:T(256)}, u32[]{:S(2)}) copy-start(f32[256]{0:T(256)} %copy-done.82) | copy-start | bytes 3076
  233.9 3.1 copy-start.61
  245.7 3.1 copy-start.99
  245.7 3.1 copy-start.14
  245.7 3.1 copy-start.80
  245.7 3.1 copy-start.96
  245.7 3.5 copy-start.29
  245.7 3.5 copy-start.38
  245.7 3.5 copy-start.92
  245.7 3.5 copy-start.94
  293.1 5.6 %copy-start.50 = (bf16[3,256,768]{2,1,0:T(8,128)(2,1)S(1)}, bf16[3,256,768]{2,1,0:T(8,128)(2,1)}, u32[]{:S(2)}) copy-start(bf16[3,256,768]{2,1,0:T(8,128)(2,1)} %constant_dynamic-update-slice_fusion) | copy-start | bytes 3538948
  301.6 3.3 copy-start.27
  301.6 3.3 copy-start.62
  316.0 6.2 %copy-start.39 = (bf16[256,768]{0,1:T(8,128)(2,1)S(1)}, bf16[256,768]{0,1:T(8,128)(2,1)}, u32[]{:S(2)}) copy-start(bf16[256,768]{0,1:T(8,128)(2,1)} %convert_element_type.217) | copy-start | bytes 1179652
  316.0 6.2 %copy-start.41 = (bf16[256,768]{1,0:T(8,128)(2,1)S(1)}, bf16[256,768]{1,0:T(8,128)(2,1)}, u32[]{:S(2)}) copy-start(bf16[256,768]{1,0:T(8,128)(2,1)} %copy-done.40) | copy-start | bytes 1179652
  316.0 7.7 %copy-start.55 = (bf16[4,256,768]{2,1,0:T(8,128)(2,1)S(1)}, bf16[4,256,768]{2,1,0:T(8,128)(2,1)}, u32[]{:S(2)}) copy-start(bf16[4,256,768]{2,1,0:T(8,128)(2,1)} %copy-done.54) | copy-start | bytes 4718596
  316.0 7.7 %copy-start.78 = (f32[256]{0:T(256)S(1)}, f32[256]{0:T(256)}, u32[]{:S(2)}) copy-start(f32[256]{0:T(256)} %copy-done.76) | copy-start | bytes 3076
  316.0 7.7 %copy-start.84 = (f32[256]{0:T(256)S(1)}, f32[256]{0:T(256)}, u32[]{:S(2)}) copy-start(f32[256]{0:T(256)} %copy-done.82) | copy-start | bytes 3076
  323.7 3.8 copy-start.46
  323.7 3.8 copy-start.65
  323.7 3.8 copy-start.89
  327.5 4.6 copy-start.48
  327.5 4.5 copy-start.52
  327.5 4.5 copy-start.53
  332.0 3.9 copy-start.88
  332.1 3.9 copy-start.106
  332.1 3.9 copy-start.105
  332.1 3.9 copy-start.104
  332.1 3.9 copy-start.103
  332.1 3.9 copy-start.102
  332.1 3.9 copy-start.87
  332.1 3.9 copy-start.90
  336.7 132.2 %copy-start.67 = (f32[8448]{0:T(1024)S(1)}, f32[8448]{0:T(1024)}, u32[]{:S(2)}) copy-start(f32[8448]{0:T(1024)} %param.31) | copy-start | bytes 101380
  336.7 132.2 %copy-start.70 = (f32[8448]{0:T(1024)S(1)}, f32[8448]{0:T(1024)}, u32[]{:S(2)}) copy-start(f32[8448]{0:T(1024)} %param.32) | copy-start | bytes 101380
  336.7 132.2 %copy-start.74 = (f32[8448]{0:T(1024)S(1)}, f32[8448]{0:T(1024)}, u32[]{:S(2)}) copy-start(f32[8448]{0:T(1024)} %param.33) | copy-start | bytes 101380
  470.4 25.8 %copy-start.68 = (f32[8448]{0:T(1024)}, f32[8448]{0:T(1024)S(1)}, u32[]{:S(2)}) copy-start(f32[8448]{0:T(1024)S(1)} %get-tuple-element.69) | copy-start | bytes 101380
  489.8 6.3 %copy-start.56 = (bf16[32,32,768]{2,1,0:T(8,128)(2,1)S(1)}, bf16[32,32,768]{2,1,0:T(8,128)(2,1)}, u32[]{:S(2)}) copy-start(bf16[32,32,768]{2,1,0:T(8,128)(2,1)} %get-tuple-element.35) | copy-start | bytes 4718596
  496.2 3.5 copy-start.58
  496.2 4.3 copy-start.33
  501.7 5.4 %copy-start = (f32[147456]{0:T(1024)S(1)}, f32[147456]{0:T(1024)}, u32[]{:S(2)}) copy-start(f32[147456]{0:T(1024)} %param.28) | copy-start | bytes 1769476
  501.7 5.4 %copy-start.1 = (f32[147456]{0:T(1024)S(1)}, f32[147456]{0:T(1024)}, u32[]{:S(2)}) copy-start(f32[147456]{0:T(1024)} %param.29) | copy-start | bytes 1769476
  501.7 5.4 %copy-start.2 = (f32[73728]{0:T(1024)S(1)}, f32[73728]{0:T(1024)}, u32[]{:S(2)}) copy-start(f32[73728]{0:T(1024)} %param.22) | copy-start | bytes 884740
  501.7 5.4 %copy-start.3 = (f32[73728]{0:T(1024)S(1)}, f32[73728]{0:T(1024)}, u32[]{:S(2)}) copy-start(f32[73728]{0:T(1024)} %param.25) | copy-start | bytes 884740
  501.7 5.4 %copy-start.4 = (f32[147456]{0:T(1024)S(1)}, f32[147456]{0:T(1024)}, u32[]{:S(2)}) copy-start(f32[147456]{0:T(1024)} %param.30) | copy-start | bytes 1769476
  501.7 5.4 %copy-start.5 = (f32[73728]{0:T(1024)S(1)}, f32[73728]{0:T(1024)}, u32[]{:S(2)}) copy-start(f32[73728]{0:T(1024)} %param.23) | copy-start | bytes 884740
  501.7 5.4 %copy-start.6 = (f32[73728]{0:T(1024)S(1)}, f32[73728]{0:T(1024)}, u32[]{:S(2)}) copy-start(f32[73728]{0:T(1024)} %param.26) | copy-start | bytes 884740
  501.7 5.4 %copy-start.7 = (f32[73728]{0:T(1024)S(1)}, f32[73728]{0:T(1024)}, u32[]{:S(2)}) copy-start(f32[73728]{0:T(1024)} %param.24) | copy-start | bytes 884740
  501.7 5.4 %copy-start.8 = (f32[73728]{0:T(1024)S(1)}, f32[73728]{0:T(1024)}, u32[]{:S(2)}) copy-start(f32[73728]{0:T(1024)} %param.27) | copy-start | bytes 884740
  532.1 6.5 %copy-start.49 = (f32[147456]{0:T(1024)}, f32[147456]{0:T(1024)S(1)}, u32[]{:S(2)}) copy-start(f32[147456]{0:T(1024)S(1)} %get-tuple-element.74) | copy-start | bytes 1769476
  (47 other events, 89.7 us)

commit v2 on v1

--- a/solution.py
+++ b/solution.py
@@ -887,6 +887,289 @@
     )(*args, clip)
 
 
+def dot_nn(a, b):
+    return lax.dot_general(a, b, (((1,), (0,)), ((), ())), preferred_element_type=F32)
+
+
+def dot_nt(a, b):
+    return lax.dot_general(a, b, (((1,), (1,)), ((), ())), preferred_element_type=F32)
+
+
+def dot_tn(a, b):
+    return lax.dot_general(a, b, (((0,), (0,)), ((), ())), preferred_element_type=F32)
+
+
+def norm_parts(values):
+    centred = values - jnp.mean(values, axis=-1, keepdims=True)
+    scale = lax.rsqrt(jnp.mean(centred * centred, axis=-1, keepdims=True) + norm_eps)
+    return centred * scale, scale
+
+
+def norm_back(unit, scale, gain, grad):
+    e = grad * gain
+    return scale * (
+        e
+        - jnp.mean(e, axis=-1, keepdims=True)
+        - unit * jnp.mean(e * unit, axis=-1, keepdims=True)
+    )
+
+
+def column_sum(values):
+    return jnp.sum(values, axis=0, keepdims=True)
+
+
+def split_heads(pair):
+    low = lax.broadcasted_iota(jnp.int32, pair.shape, 1) < HD
+    zero = jnp.zeros_like(pair)
+    return jnp.concatenate([jnp.where(low, pair, zero), jnp.where(low, zero, pair)], axis=0)
+
+
+def join_heads(stacked):
+    rows = stacked.shape[0] // 2
+    low = lax.broadcasted_iota(jnp.int32, (rows, 2 * HD), 1) < HD
+    return jnp.where(low, stacked[:rows], stacked[rows:])
+
+
+def soft_rows(scores, allowed):
+    scores = jnp.where(allowed, scores * HD ** (-0.5), masked_score)
+    top = jnp.max(scores, axis=-1, keepdims=True)
+    p = jnp.exp(scores - top)
+    return p / jnp.sum(p, axis=-1, keepdims=True)
+
+
+def self_mask(lens):
+    shape = (2 * SUF, SUF)
+    query = lax.broadcasted_iota(jnp.int32, shape, 0) % SUF
+    key = lax.broadcasted_iota(jnp.int32, shape, 1)
+    return (key <= query) & (key < lens[0:1, 0:SUF])
+
+
+def cross_mask(lens):
+    key = lax.broadcasted_iota(jnp.int32, (2 * SUF, MEMLEN), 1)
+    seen = jnp.concatenate([lens[0:1]] * (MEMLEN // 128), axis=1)
+    return key < PATCH + seen
+
+
+PAIRS = H // 2
+
+
+def attend(mask_of, lens, q_ref, k_ref, v_ref, o_ref, p_ref, key_rows):
+    def body(ex, _):
+        allowed = mask_of(lens[ex])
+        rows = pl.ds(pl.multiple_of(ex * SUF, SUF), SUF)
+        keys = pl.ds(pl.multiple_of(ex * key_rows, key_rows), key_rows)
+        for pair in range(PAIRS):
+            lanes = pl.ds(pair * 2 * HD, 2 * HD)
+            p = soft_rows(dot_nt(split_heads(q_ref[rows, lanes]), k_ref[keys, lanes]), allowed)
+            p_ref[ex * PAIRS + pair] = p
+            o_ref[rows, lanes] = join_heads(dot_nn(p.astype(BF), v_ref[keys, lanes])).astype(BF)
+        return 0
+
+    lax.fori_loop(0, EX_DEV, body, 0)
+
+
+def attend_back(q_ref, k_ref, v_ref, p_ref, do_ref, dq_ref, dk_ref, dv_ref, key_rows):
+    scale = HD ** (-0.5)
+
+    def body(ex, _):
+        rows = pl.ds(pl.multiple_of(ex * SUF, SUF), SUF)
+        keys = pl.ds(pl.multiple_of(ex * key_rows, key_rows), key_rows)
+        for pair in range(PAIRS):
+            lanes = pl.ds(pair * 2 * HD, 2 * HD)
+            p = p_ref[ex * PAIRS + pair]
+            d_out = split_heads(do_ref[rows, lanes])
+            dv_ref[keys, lanes] = dot_tn(p.astype(BF), d_out).astype(BF)
+            dp = dot_nt(d_out, v_ref[keys, lanes])
+            ds = (p * (dp - jnp.sum(p * dp, axis=-1, keepdims=True))).astype(BF)
+            dq_ref[rows, lanes] = (join_heads(dot_nn(ds, k_ref[keys, lanes])) * scale).astype(BF)
+            dk_ref[keys, lanes] = (
+                dot_tn(ds, split_heads(q_ref[rows, lanes])) * scale
+            ).astype(BF)
+        return 0
+
+    lax.fori_loop(0, EX_DEV, body, 0)
+
+
+def gelu_parts(u):
+    rate = (2.0 / jnp.pi) ** 0.5
+    square = u * u
+    t = jnp.tanh(rate * (u + 0.044715 * u * square))
+    half = 0.5 * (1.0 + t)
+    slope = half + 0.5 * u * (1.0 - t * t) * (rate * (1.0 + 3 * 0.044715 * square))
+    return u * half, slope
+
+
+def layer_kernel(
+    x_ref, cot_ref, vec_ref, slen_ref, plen_ref, self_h, cross_h, up_h, dn_h, mem_h,
+    out_ref, sg_ref, vecg_ref, qkv_g, wo_g, cq_g, ckv_g, co_g, up_g, dn_g, mem_g,
+    sw, cw, uw, dw, mem, ring, dmem, a1, q1, k1, v1, o1, a2, q2, o2, a3, k2, v2,
+    db, dq, dk1, dv1, dk2, dv2, e3, z_ref, slope, unit1, unit2, unit3, h1, h2, dh, ps, pc,
+    loads, stores, mem_sem,
+):
+    sources = (
+        [(self_h.at[i], sw.at[i]) for i in range(4)]
+        + [(mem_h, mem)]
+        + [(cross_h.at[i], cw.at[i]) for i in range(4)]
+        + [(up_h.at[pl.ds(0, uw.shape[1]), j], uw.at[j]) for j in range(4)]
+        + [(dn_h.at[4 + j], dw.at[j]) for j in range(4)]
+    )
+    fetched = []
+    for i, (src, dst) in enumerate(sources):
+        fetched.append(pltpu.make_async_copy(src, dst, loads.at[i]))
+        fetched[-1].start()
+    self_ok, mem_ok, cross_ok = fetched[0:4], fetched[4], fetched[5:9]
+    up_ok, dn_ok = fetched[9:13], fetched[13:17]
+
+    depth = ring.shape[0]
+    pending = []
+
+    def give(value, dst):
+        slot = len(pending) % depth
+        if len(pending) >= depth:
+            pending[-depth].wait()
+        ring[slot] = value.astype(BF)
+        pending.append(pltpu.make_async_copy(ring.at[slot], dst, stores.at[slot]))
+        pending[-1].start()
+
+    def row(i):
+        return vec_ref[i : i + 1, :]
+
+    g1, b1, g2, b2, g3, b3, bdn = [row(i) for i in range(7)]
+
+    x = x_ref[...].astype(F32)
+    unit, r1 = norm_parts(x)
+    unit1[...] = unit
+    a1[...] = (unit * g1 + b1).astype(BF)
+    for i, ref in enumerate((q1, k1, v1)):
+        self_ok[i].wait()
+        ref[...] = dot_nn(a1[...], sw[i]).astype(BF)
+    attend(self_mask, slen_ref, q1, k1, v1, o1, ps, SUF)
+    self_ok[3].wait()
+    h1[...] = x_ref[...].astype(F32) + dot_nn(o1[...], sw[3])
+
+    unit, r2 = norm_parts(h1[...])
+    unit2[...] = unit
+    a2[...] = (unit * g2 + b2).astype(BF)
+    cross_ok[0].wait()
+    q2[...] = dot_nn(a2[...], cw[0]).astype(BF)
+    mem_ok.wait()
+    for i, ref in ((1, k2), (2, v2)):
+        cross_ok[i].wait()
+        ref[...] = dot_nn(mem[...], cw[i]).astype(BF)
+    attend(cross_mask, plen_ref, q2, k2, v2, o2, pc, MEMLEN)
+    cross_ok[3].wait()
+    h2[...] = h1[...] + dot_nn(o2[...], cw[3])
+
+    unit, r3 = norm_parts(h2[...])
+    unit3[...] = unit
+    a3[...] = (unit * g3 + b3).astype(BF)
+    out_ref[...] = h2[...] + bdn
+    ones = lax.broadcasted_iota(jnp.int32, (SUF, D), 0)
+    for ex in range(EX_DEV):
+        rows = pl.ds(ex * SUF, SUF)
+        length = jnp.concatenate([slen_ref[ex, 0:1]] * (D // 128), axis=1)
+        seed = cot_ref[rows].astype(F32) * (ones < length).astype(F32)
+        dh[rows] = seed
+        e3[rows] = seed.astype(BF)
+    vecg_ref[6:7] = column_sum(e3[...].astype(F32))
+    width = uw.shape[1] * uw.shape[2]
+    for j in range(4):
+        up_ok[j].wait()
+        dn_ok[j].wait()
+        u = dot_nn(a3[...], uw[j].reshape(width, D)) + row(7 + j)
+        act, bend = gelu_parts(u)
+        z_ref[...] = act.astype(BF)
+        slope[...] = bend
+        out_ref[...] += dot_nn(z_ref[...], dw[j])
+        give(dot_tn(z_ref[...], e3[...]), dn_g.at[j])
+        db[...] = (dot_nt(e3[...], dw[j]) * slope[...]).astype(BF)
+        vecg_ref[7 + j : 8 + j] = column_sum(db[...].astype(F32))
+        give(dot_tn(a3[...], db[...]), up_g.at[j])
+        part = dot_nt(db[...], uw[j].reshape(width, D))
+        if j == 0:
+            h2[...] = part
+        else:
+            h2[...] += part
+
+    grad = h2[...]
+    vecg_ref[4:5] = column_sum(grad * unit3[...])
+    vecg_ref[5:6] = column_sum(grad)
+    dh[...] += norm_back(unit3[...], r3, g3, grad)
+    db[...] = dh[...].astype(BF)
+    give(dot_tn(o2[...], db[...]), co_g)
+    e3[...] = dot_nt(db[...], cw[3]).astype(BF)
+    attend_back(q2, k2, v2, pc, e3, dq, dk2, dv2, MEMLEN)
+    give(dot_tn(a2[...], dq[...]), cq_g)
+    give(dot_tn(mem[...], dk2[...]), ckv_g.at[0])
+    give(dot_tn(mem[...], dv2[...]), ckv_g.at[1])
+    outs = []
+    for ex in range(EX_DEV):
+        keys = pl.ds(ex * MEMLEN, MEMLEN)
+        dmem[ex] = (dot_nt(dk2[keys], cw[1]) + dot_nt(dv2[keys], cw[2])).astype(BF)
+        outs.append(pltpu.make_async_copy(dmem.at[ex], mem_g.at[ex], mem_sem.at[ex]))
+        outs[-1].start()
+    grad = dot_nt(dq[...], cw[0])
+    vecg_ref[2:3] = column_sum(grad * unit2[...])
+    vecg_ref[3:4] = column_sum(grad)
+    dh[...] += norm_back(unit2[...], r2, g2, grad)
+    db[...] = dh[...].astype(BF)
+    give(dot_tn(o1[...], db[...]), wo_g)
+    e3[...] = dot_nt(db[...], sw[3]).astype(BF)
+    attend_back(q1, k1, v1, ps, e3, dq, dk1, dv1, SUF)
+    for i, ref in enumerate((dq, dk1, dv1)):
+        give(dot_tn(a1[...], ref[...]), qkv_g.at[i])
+    grad = dot_nt(dq[...], sw[0]) + dot_nt(dk1[...], sw[1]) + dot_nt(dv1[...], sw[2])
+    vecg_ref[0:1] = column_sum(grad * unit1[...])
+    vecg_ref[1:2] = column_sum(grad)
+    sg_ref[...] = dh[...] + norm_back(unit1[...], r1, g1, grad)
+    for one in outs + pending[-depth:]:
+        one.wait()
+
+
+def layer_all(x, cot, vec, slen, plen, self_mats, cross_mats, up_view, dn_view, mem_rows):
+    anywhere = pl.BlockSpec(memory_space=pl.ANY)
+    vmem = pl.BlockSpec(memory_space=pltpu.VMEM)
+    rows, mem_count = x.shape[0], mem_rows.shape[0]
+    mats = lambda n: pltpu.VMEM((n, D, D), BF)
+    low = pltpu.VMEM((rows, D), BF)
+    wide = pltpu.VMEM((rows, D), F32)
+    mem_low = pltpu.VMEM((mem_count, D), BF)
+    shape = lambda *dims, dtype=BF: jax.ShapeDtypeStruct(dims, dtype)
+    half = up_view.shape[0] // 2
+    return pl.pallas_call(
+        layer_kernel,
+        out_shape=[
+            shape(rows, D, dtype=F32),
+            shape(rows, D, dtype=F32),
+            shape(*vec.shape, dtype=F32),
+            shape(3, D, D),
+            shape(D, D),
+            shape(D, D),
+            shape(2, D, D),
+            shape(D, D),
+            shape(4, D, D),
+            shape(4, D, D),
+            shape(EX_DEV, MEMLEN, D),
+        ],
+        in_specs=[vmem] * 5 + [anywhere] * 5,
+        out_specs=[vmem] * 3 + [anywhere] * 8,
+        scratch_shapes=[
+            mats(4), mats(4), pltpu.VMEM((4, half) + up_view.shape[2:], BF), mats(4),
+            mem_low, mats(4), pltpu.VMEM((EX_DEV, MEMLEN, D), BF),
+            low, low, low, low, low, low, low, low, low, mem_low, mem_low,
+            low, low, low, low, mem_low, mem_low, low, low,
+            wide, wide, wide, wide, wide, wide, wide,
+            pltpu.VMEM((EX_DEV * PAIRS, 2 * SUF, SUF), F32),
+            pltpu.VMEM((EX_DEV * PAIRS, 2 * SUF, MEMLEN), F32),
+            pltpu.SemaphoreType.DMA((17,)),
+            pltpu.SemaphoreType.DMA((4,)),
+            pltpu.SemaphoreType.DMA((EX_DEV,)),
+        ],
+        compiler_params=pltpu.CompilerParams(vmem_limit_bytes=60 << 20),
+        name="layer_all",
+    )(x, cot, vec, slen, plen, self_mats, cross_mats, up_view, dn_view, mem_rows)
+
+
 def fast_shards(
     suffix,
     memory,
@@ -925,160 +1208,21 @@
         memory[0],
         ndp,
     )
-    self_mats = self_full.reshape(4, D, D)
-    cross_mats = cross_full.reshape(4, D, D)
-    feed_full = feed_full.reshape(2, owners // 2, 4, rows_f, D)
-    up_mats = feed_full[0].transpose(1, 0, 2, 3).reshape(4, D, D)
-    down_mat = feed_full[1].reshape(FF, D)
-    memory_rows = own_memory.reshape(EX_DEV * MEMLEN, D)
-    vector_parts = [vectors[segment * D : (segment + 1) * D] for segment in range(7)]
-    bias_up = vectors[7 * D :]
-    suffix_len = suffix_lengths[0]
-    prefix_len = prefix_lengths[0]
-    positions = jnp.arange(SUF, dtype=jnp.int32)
-    causal = positions[:, None] >= positions[None, :]
-    self_allowed = (
-        causal[None, None, :, :] & (positions[None, :] < suffix_len[:, None])[:, None, None, :]
-    )
-    memory_pos = jnp.arange(MEMLEN, dtype=jnp.int32)
-    cross_allowed = (memory_pos[None, :] < (PATCH + prefix_len)[:, None])[:, None, None, :]
-    inputs = suffix.reshape(row_count, D).astype(jnp.float32)
-    normed_one = layer_norm(inputs, vector_parts[0], vector_parts[1]).astype(jnp.bfloat16)
-    self_qkv = jnp.einsum(
-        "rd,jde->jre", normed_one, self_mats[0:3], preferred_element_type=jnp.float32
-    ).astype(jnp.bfloat16)
-    self_heads = self_qkv.reshape(3, EX_DEV, SUF, H, HD)
-    mixed_one, totals_one = attend_forward(
-        self_heads[0], self_heads[1], self_heads[2], self_allowed
-    )
-    mixed_one = mixed_one.reshape(row_count, D).astype(jnp.bfloat16)
-    hidden_one = inputs + jnp.dot(mixed_one, self_mats[3], preferred_element_type=jnp.float32)
-    normed_two = layer_norm(hidden_one, vector_parts[2], vector_parts[3]).astype(jnp.bfloat16)
-    cross_query = jnp.dot(normed_two, cross_mats[0], preferred_element_type=jnp.float32).astype(
-        jnp.bfloat16
-    )
-    cross_kv = jnp.einsum(
-        "rd,jde->jre", memory_rows, cross_mats[1:3], preferred_element_type=jnp.float32
-    ).astype(jnp.bfloat16)
-    query_heads = cross_query.reshape(EX_DEV, SUF, H, HD)
-    kv_heads = cross_kv.reshape(2, EX_DEV, MEMLEN, H, HD)
-    mixed_two, totals_two = attend_forward(query_heads, kv_heads[0], kv_heads[1], cross_allowed)
-    mixed_two = mixed_two.reshape(row_count, D).astype(jnp.bfloat16)
-    hidden_two = hidden_one + jnp.dot(mixed_two, cross_mats[3], preferred_element_type=jnp.float32)
-    normed_three = layer_norm(hidden_two, vector_parts[4], vector_parts[5]).astype(jnp.bfloat16)
-    pre_act = (
-        jnp.einsum(
-            "rd,jde->jre", normed_three, up_mats, preferred_element_type=jnp.float32
-        )
-        + bias_up.reshape(4, 1, D)
-    )
-    activated = gelu_tanh(pre_act).astype(jnp.bfloat16)
-    layer_output = hidden_two + (
-        jnp.einsum(
-            "jre,jed->rd", activated, down_mat.reshape(4, D, D), preferred_element_type=jnp.float32
-        )
-        + vector_parts[6]
-    )
-    valid_rows = (positions[None, :] < suffix_len[:, None]).astype(jnp.float32)
-    seed_rows = (
-        cotangent.reshape(EX_DEV, SUF, D).astype(jnp.float32) * valid_rows[:, :, None]
-    ).reshape(row_count, D)
-    seed_low = seed_rows.astype(jnp.bfloat16)
-    bias_down_grad = jnp.sum(seed_low.astype(jnp.float32), axis=0)
-    down_grad = jnp.einsum(
-        "jre,rd->jed", activated, seed_low, preferred_element_type=jnp.float32
-    ).astype(BF)
-    activated_grad = jnp.einsum(
-        "rd,jed->jre", seed_low, down_mat.reshape(4, D, D), preferred_element_type=jnp.float32
-    )
-    _, gelu_back = jax.vjp(gelu_tanh, pre_act)
-    pre_grad = gelu_back(activated_grad)[0].astype(jnp.bfloat16)
-    bias_up_grad = jnp.sum(pre_grad.astype(jnp.float32), axis=1).reshape(FF)
-    up_grad = jnp.einsum(
-        "rd,jre->jde", normed_three, pre_grad, preferred_element_type=jnp.float32
-    ).astype(BF)
-    normed_three_grad = jnp.einsum(
-        "jre,jde->rd", pre_grad, up_mats, preferred_element_type=jnp.float32
-    )
-    _, norm_three_back = jax.vjp(layer_norm, hidden_two, vector_parts[4], vector_parts[5])
-    through_three, gain_three_grad, shift_three_grad = norm_three_back(normed_three_grad)
-    hidden_two_grad = seed_rows + through_three
-    branch_two = hidden_two_grad.astype(jnp.bfloat16)
-    cross_out_grad = jnp.einsum(
-        "rd,re->de", mixed_two, branch_two, preferred_element_type=jnp.float32
-    ).astype(BF)
-    mixed_two_grad = jnp.einsum(
-        "re,de->rd", branch_two, cross_mats[3], preferred_element_type=jnp.float32
-    ).astype(jnp.bfloat16)
-    query_two_grad, key_two_grad, value_two_grad = attend_backward(
-        query_heads,
-        kv_heads[0],
-        kv_heads[1],
-        cross_allowed,
-        totals_two,
-        mixed_two_grad.reshape(EX_DEV, SUF, H, HD),
-    )
-    cross_query_grad = query_two_grad.reshape(row_count, D).astype(jnp.bfloat16)
-    cross_kv_grad = (
-        jnp.stack([key_two_grad, value_two_grad])
-        .reshape(2, EX_DEV * MEMLEN, D)
-        .astype(jnp.bfloat16)
-    )
-    query_weight_grad = jnp.einsum(
-        "rd,re->de", normed_two, cross_query_grad, preferred_element_type=jnp.float32
-    ).astype(BF)
-    kv_weight_grad = jnp.einsum(
-        "rd,jre->jde", memory_rows, cross_kv_grad, preferred_element_type=jnp.float32
-    ).astype(BF)
-    normed_two_grad = jnp.einsum(
-        "re,de->rd", cross_query_grad, cross_mats[0], preferred_element_type=jnp.float32
-    )
-    memory_local_grad = jnp.einsum(
-        "jre,jde->rd", cross_kv_grad, cross_mats[1:3], preferred_element_type=jnp.float32
-    ).astype(BF)
-    _, norm_two_back = jax.vjp(layer_norm, hidden_one, vector_parts[2], vector_parts[3])
-    through_two, gain_two_grad, shift_two_grad = norm_two_back(normed_two_grad)
-    hidden_one_grad = hidden_two_grad + through_two
-    branch_one = hidden_one_grad.astype(jnp.bfloat16)
-    self_out_grad = jnp.einsum(
-        "rd,re->de", mixed_one, branch_one, preferred_element_type=jnp.float32
-    ).astype(BF)
-    mixed_one_grad = jnp.einsum(
-        "re,de->rd", branch_one, self_mats[3], preferred_element_type=jnp.float32
-    ).astype(jnp.bfloat16)
-    query_one_grad, key_one_grad, value_one_grad = attend_backward(
-        self_heads[0],
-        self_heads[1],
-        self_heads[2],
-        self_allowed,
-        totals_one,
-        mixed_one_grad.reshape(EX_DEV, SUF, H, HD),
-    )
-    self_qkv_grad = (
-        jnp.stack([query_one_grad, key_one_grad, value_one_grad])
-        .reshape(3, row_count, D)
-        .astype(jnp.bfloat16)
-    )
-    qkv_weight_grad = jnp.einsum(
-        "rd,jre->jde", normed_one, self_qkv_grad, preferred_element_type=jnp.float32
-    ).astype(BF)
-    normed_one_grad = jnp.einsum(
-        "jre,jde->rd", self_qkv_grad, self_mats[0:3], preferred_element_type=jnp.float32
-    )
-    _, norm_one_back = jax.vjp(layer_norm, inputs, vector_parts[0], vector_parts[1])
-    through_one, gain_one_grad, shift_one_grad = norm_one_back(normed_one_grad)
-    suffix_gradient = (hidden_one_grad + through_one).reshape(1, EX_DEV, SUF, D)
-    vector_partial = jnp.concatenate(
-        [
-            gain_one_grad,
-            shift_one_grad,
-            gain_two_grad,
-            shift_two_grad,
-            gain_three_grad,
-            shift_three_grad,
-            bias_down_grad,
-            bias_up_grad,
-        ]
+    lens = lambda a: jnp.broadcast_to(a[0][:, None, None], (EX_DEV, 8, 128))
+    (
+        layer_output, suffix_gradient, vector_partial,
+        qkv_g, wo_g, cq_g, ckv_g, co_g, up_g, dn_g, mem_g,
+    ) = layer_all(
+        suffix.reshape(row_count, D),
+        cotangent.reshape(row_count, D),
+        vectors.reshape(-1, D),
+        lens(suffix_lengths),
+        lens(prefix_lengths),
+        self_full.reshape(4, D, D),
+        cross_full.reshape(4, D, D),
+        feed_full.reshape(owners, 4, rows_f, D),
+        feed_full.reshape(8, D, D),
+        own_memory.reshape(EX_DEV * MEMLEN, D),
     )
     vec_rows = vectors.shape[0] // 128
     vec_pad = (vec_rows + 7) // 8 * 8
@@ -1086,15 +1230,15 @@
     split = (2, 2, 2)
     self_total, cross_total, feed_total, memory_back, vec_sum, squared = scatter_all(
         (
-            qkv_weight_grad.reshape((3,) + split + (rows_a, D)),
-            self_out_grad.reshape(split + (rows_a, D)),
-            query_weight_grad.reshape(split + (rows_a, D)),
-            kv_weight_grad.reshape((2,) + split + (rows_a, D)),
-            cross_out_grad.reshape(split + (rows_a, D)),
-            up_grad.reshape((4, 2) + split + (rows_f, D)),
-            down_grad.reshape((2,) + split + (4, rows_f, D)),
+            qkv_g.reshape((3,) + split + (rows_a, D)),
+            wo_g.reshape(split + (rows_a, D)),
+            cq_g.reshape(split + (rows_a, D)),
+            ckv_g.reshape((2,) + split + (rows_a, D)),
+            co_g.reshape(split + (rows_a, D)),
+            up_g.reshape((4, 2) + split + (rows_f, D)),
+            dn_g.reshape((2,) + split + (4, rows_f, D)),
         ),
-        memory_local_grad.reshape(EX_DEV, ndp, MEMLEN // ndp, D),
+        mem_g.reshape(EX_DEV, ndp, MEMLEN // ndp, D),
         vector_in,
         rows_a,
         rows_f,
@@ -1160,7 +1304,7 @@
     )
     return (
         layer_output.reshape(1, EX_DEV, SUF, D),
-        suffix_gradient,
+        suffix_gradient.reshape(1, EX_DEV, SUF, D),
         memory_gradient,
         *new,
         vector_total,

time: 546 us -> 402 us (0.74)
  local copies, waits for them, and re-layouts: 110 us -> 24 us
  matrix products: 85.8 us -> 0 us
  Pallas kernels: 269 us -> 328 us
  other arithmetic: 57 us -> 25 us
    dot_general x33 -> x0, matrix products: 85.8 us -> none  [the longest x1 7.6 us: fast_shards(): jnp.einsum('rd,jed->jre', seed_low, down_mat.reshape(4, D, D), preferred_...]
    pallas_call x0 -> x1, Pallas kernels: none -> 59 us  [layer_all(): pl.pallas_call(layer_kernel, out_shape=[shape(rows, D, dtype=F32), shape(...]
    another operation x11 -> x0, local copies, waits for them, and re-layouts: 21 us -> none  [the longest x7 15.2 us: fast_shards(): jnp.stack([query_one_grad, key_one_grad, value_one_grad])]
    slice x8 -> x0, local copies, waits for them, and re-layouts: 20.2 us -> none  [the longest x1 8.46 us: fast_shards(): up_mats = feed_full[0].transpose(1, 0, 2, 3).reshape(4, D, D)]
    convert_element_type x7 -> x0, local copies, waits for them, and re-layouts: 11.1 us -> none  [the longest x2 4.72 us: fast_shards(): cross_query_grad = query_two_grad.reshape(row_count, D).astype(jnp.bfloat16)]
    reshape x7 -> x2, local copies, waits for them, and re-layouts: 12.2 us -> 1.43 us  [the longest x1 0.81 us: fast_shards(): vector_partial.reshape(vec_rows, 128)]
    reduce_sum x10 -> x0, other arithmetic: 10.6 us -> none  [the longest x2 3.96 us: attend_forward(): totals = jax.nn.logsumexp(scores, axis=-1)]
    squeeze x6 -> x0, local copies, waits for them, and re-layouts: 8.58 us -> none  [the longest x1 4.36 us: fast_shards(): kv_heads[1]]
where the time goes in v2:
time: 402 us; the launch traced here: 394 us
  Pallas kernels  328 us (82%)
  other arithmetic  25 us (6%)
  local copies, waits for them, and re-layouts  24 us (6%)
  between operations  17.3 us (4%)
    pallas_call x1, Pallas kernels, gather_all(): pl.pallas_call(gather_kernel, out_shape=[shards_of(self_in), shards_of(cr...  130 us
    pallas_call x1, Pallas kernels, scatter_all(): pl.pallas_call(scatter_kernel, out_shape=[jax.ShapeDtypeStruct((1, rows_a...  128 us
    pallas_call x1, Pallas kernels, layer_all(): pl.pallas_call(layer_kernel, out_shape=[shape(rows, D, dtype=F32), shape(...  59 us
    pallas_call x1, Pallas kernels, ratio_all(): pl.pallas_call(ratio_kernel, out_shape=jax.ShapeDtypeStruct((32, 128), F3...  11 us

profile of v2, /device:TPU:0, one launch (start us, length us, event | category | flops | bytes accessed | tf_op | source)
XLA Modules:
  0.0 394.2 jit_solution(1373766941229514290)
XLA Ops:
  0.7 1.2 convert_element_type.14
  1.8 0.1 reshape.173
  2.0 0.3 reshape.174
  2.3 0.0 copy-start.25
  2.3 0.0 copy-start.26
  2.3 0.8 bitcast_select_fusion.feed_in
  3.1 0.8 reshape.171.self_in
  3.9 0.8 reshape.172.cross_in
  4.7 129.7 %gather_all.1 = (bf16[4,2,2,2,1,96,768]{6,5,4,3,2,1,0:T(8,128)(2,1)}, bf16[4,2,2,2,1,96,768]{6,5,4,3,2,1,0:T(8,128)(2,1)}, bf16[4,2,2,2,4,48,768]{6,5,4,3,2,1,0:T(8,128)(2,1)}, bf16[4,8,32,768]{3,2,1,0:T(8,128)(2,1)}) custom-call(bf16[1,96,768]{2,1,0:T(8,128)(2,1)} %reshape.171.self_in, bf16[1,96,768]{2,1,0:T(8,128)(2,1)} %reshape.172.cross_in, ...), custom_call_target="tpu_custom_call" | custom-call | tf_op jit(solution)/shard_map/gather_all/pallas_call | solution.py:560
  134.4 0.6 reshape.170.vec_ref
  135.1 0.7 broadcast_in_dim.24.slen_ref
  135.7 0.7 broadcast_in_dim.26.plen_ref
  136.4 59.0 %layer_all.1 = (f32[256,768]{1,0:T(8,128)}, f32[256,768]{1,0:T(8,128)}, f32[11,768]{1,0:T(8,128)}, bf16[3,768,768]{2,1,0:T(8,128)(2,1)}, bf16[768,768]{1,0:T(8,1...) custom-call(bf16[256,768]{1,0:T(8,128)(2,1)} %bitcast.83, ...), custom_call_target="tpu_custom_call" | custom-call | tf_op jit(solution)/shard_map/layer_all/pallas_call | solution.py:1139
  195.4 0.8 reshape.190
  196.2 0.6 pad.4.vec
  196.8 128.2 %scatter_all.1 = (f32[1,96,768]{2,1,0:T(8,128)}, f32[1,96,768]{2,1,0:T(8,128)}, f32[4,48,768]{2,1,0:T(8,128)}, bf16[32,32,768]{2,1,0:T(8,128)(2,1)}, f32[72,128]{1,0:T(8,128)}, /*index=5*/f32[8,128]{1,0:T(8,128)}) custom-call(bf16[3,2,2,2,96,768]{5,4,3,2,1,0:T(8,128)(2,1)} %bitcast.75, bf16[2,2,2,96,768]{4,3,2,1,0:T(8,128)(2,1)} %bitcast.80, ...), custom_call_target="tpu_custom_call" | custom-call | tf_op jit(solution)/shard_map/scatter_all/pallas_call | solution.py:808
  325.0 1.4 multiply_reduce_fusion
  326.4 1.3 reduce_sum.171
  329.1 1.4 multiply_add_fusion.3
  330.5 0.6 multiply_reduce_fusion.3
  336.0 0.6 multiply_reduce_fusion.1
  337.3 0.6 broadcast_in_dim.29.clip
  337.9 1.4 copy.40
  339.3 0.0 copy-start.15
  339.3 0.8 copy-done.15
  340.1 1.1 reshape.192
  341.2 0.0 copy-start.6
  341.2 0.9 reshape.193
  342.1 1.2 broadcast_select_fusion.1.gf
  343.3 1.7 reshape_reshape.6.gs
  345.0 1.7 reshape_reshape.7.gc
  346.7 1.0 copy-done.7
  347.6 1.0 copy-done.9
  348.6 1.0 copy-done.11
  349.6 1.0 copy-done.12
  350.5 0.7 copy-done.13
  351.2 11.0 %ratio_all.1 = f32[32,128]{1,0:T(8,128)S(1)} custom-call(f32[576,128]{1,0:T(8,128)S(1)} %copy-done.11, f32[576,128]{1,0:T(8,128)S(1)} %copy-done.12, f32[1152,128]{1,0:T(8,128)S(1)} %broadcast_select_fusion.1.gf, f32[576,128]{1,0:T(8,128)S(1)} %bitcast.61, f32[576,128]{1,0:T(8,128)S(1)} %bitcast.62, f32[1152,128]{1,0:T(8,128)S(1)} %bitcast.59, ...), custom_call_target="tpu_custom_call" | custom-call | tf_op jit(solution)/shard_map/ratio_all/pallas_call | solution.py:871
  362.2 0.1 reduce_sum.173
  362.4 0.1 fusion.8
  362.4 0.1 concatenate.11
  362.5 1.4 multiply_reduce_fusion.4
  368.8 1.3 multiply_reduce_fusion.2
  370.8 0.1 concatenate.10
  370.9 0.6 pad_maximum_fusion
  371.5 0.7 constant_dynamic-update-slice_fusion.6
  372.3 0.7 constant_dynamic-update-slice_fusion.5
  373.1 0.7 constant_dynamic-update-slice_fusion.4
  373.8 0.7 constant_dynamic-update-slice_fusion.3
  374.6 0.7 constant_dynamic-update-slice_fusion.2
  375.4 0.7 constant_dynamic-update-slice_fusion.1
  376.1 0.7 constant_dynamic-update-slice_fusion
  376.9 0.7 subtract_dynamic-update-slice_fusion
  377.7 1.4 broadcast_multiply_fusion.3
  379.1 0.6 fusion.9
  380.4 1.3 reshape.204
  381.7 1.9 reshape.205
  383.6 1.4 multiply_subtract_fusion
  385.0 0.9 broadcast_multiply_fusion
  385.9 0.1 copy-done.16
  387.3 1.0 reshape.191
  388.3 0.0 copy-start.18
  388.4 1.5 multiply_subtract_fusion.1
  389.9 0.7 copy-done.17
  390.6 2.0 bitcast_convert_fusion
  (48 shorter events, 0.2 us)
Async XLA Ops:
  0.7 2.4 copy-start.2
  0.7 3.2 copy-start.3
  2.2 132.2 %copy-start.21 = (f32[8448]{0:T(1024)S(1)}, f32[8448]{0:T(1024)}, u32[]{:S(2)}) copy-start(f32[8448]{0:T(1024)} %param.31) | copy-start | bytes 101380
  2.3 132.8 %copy-start.25 = (s32[1,4]{1,0:T(1,128)S(1)}, s32[1,4]{1,0:T(1,128)}, u32[]{:S(2)}) copy-start(s32[1,4]{1,0:T(1,128)} %param.20) | copy-start | bytes 52
  2.3 133.5 %copy-start.26 = (s32[1,4]{1,0:T(1,128)S(1)}, s32[1,4]{1,0:T(1,128)}, u32[]{:S(2)}) copy-start(s32[1,4]{1,0:T(1,128)} %param.19) | copy-start | bytes 52
  196.8 132.3 %copy-start.23 = (f32[8448]{0:T(1024)S(1)}, f32[8448]{0:T(1024)}, u32[]{:S(2)}) copy-start(f32[8448]{0:T(1024)} %param.32) | copy-start | bytes 101380
  196.8 132.3 %copy-start.24 = (f32[8448]{0:T(1024)S(1)}, f32[8448]{0:T(1024)}, u32[]{:S(2)}) copy-start(f32[8448]{0:T(1024)} %param.33) | copy-start | bytes 101380
  325.0 16.2 %copy-start.14 = (f32[4,48,768]{2,1,0:T(8,128)S(1)}, f32[4,48,768]{2,1,0:T(8,128)}, u32[]{:S(2)}) copy-start(f32[4,48,768]{2,1,0:T(8,128)} %get-tuple-element.62) | copy-start | bytes 1769476
  330.5 7.3 %copy-start.22 = (f32[8448]{0:T(1024)}, f32[8448]{0:T(1024)S(1)}, u32[]{:S(2)}) copy-start(f32[8448]{0:T(1024)S(1)} %get-tuple-element.77) | copy-start | bytes 101380
  339.3 0.8 copy-start.15
  341.2 5.4 %copy-start = (f32[147456]{0:T(1024)S(1)}, f32[147456]{0:T(1024)}, u32[]{:S(2)}) copy-start(f32[147456]{0:T(1024)} %param.28) | copy-start | bytes 1769476
  341.2 5.4 %copy-start.1 = (f32[147456]{0:T(1024)S(1)}, f32[147456]{0:T(1024)}, u32[]{:S(2)}) copy-start(f32[147456]{0:T(1024)} %param.29) | copy-start | bytes 1769476
  341.2 5.4 %copy-start.4 = (f32[147456]{0:T(1024)S(1)}, f32[147456]{0:T(1024)}, u32[]{:S(2)}) copy-start(f32[147456]{0:T(1024)} %param.30) | copy-start | bytes 1769476
  341.2 5.4 %copy-start.5 = (f32[73728]{0:T(1024)S(1)}, f32[73728]{0:T(1024)}, u32[]{:S(2)}) copy-start(f32[73728]{0:T(1024)} %param.23) | copy-start | bytes 884740
  341.2 5.4 %copy-start.6 = (f32[73728]{0:T(1024)S(1)}, f32[73728]{0:T(1024)}, u32[]{:S(2)}) copy-start(f32[73728]{0:T(1024)} %param.26) | copy-start | bytes 884740
  346.7 1.0 copy-start.7
  347.6 1.0 copy-start.9
  348.6 1.0 copy-start.11
  349.6 1.0 copy-start.12
  350.5 0.7 copy-start.13
  377.7 2.7 copy-start.27
  385.0 1.0 copy-start.16
  385.0 3.3 copy-start.20
  385.0 3.3 copy-start.8
  385.0 3.4 copy-start.10
  388.3 1.5 copy-start.18
  388.4 4.3 %copy-start.19 = (f32[73728]{0:T(1024)}, f32[73728]{0:T(1024)S(1)}, u32[]{:S(2)}) copy-start(f32[73728]{0:T(1024)S(1)} %reshape.203) | copy-start | bytes 884740
  388.4 2.2 copy-start.17

commit v3 on v2

--- a/solution.py
+++ b/solution.py
@@ -415,6 +415,8 @@
 F32 = jnp.float32
 MESH = pl.DeviceIdType.MESH
 NZ = 4
+AHEAD = 4
+MEM_AT = 5
 
 
 def place():
@@ -465,76 +467,106 @@
             cp.wait_send()
 
 
+LANES = 128
+
+
+def rows_of(flat, dst, j, start, stride):
+    rows, width = dst.shape[1:]
+    for i in range(width // LANES):
+        part = flat[pl.ds(start + i, rows, stride=stride), :]
+        dst[j, :, i * LANES : (i + 1) * LANES] = part.astype(dst.dtype)
+
+
+def feed_lines(j, rows, width, up):
+    per = width // LANES
+    return (j * per, 4 * per) if up else (j * rows * per, per)
+
+
 def gather_kernel(
-    self_in, cross_in, feed_in, mem_in, self_out, cross_out, feed_out, mem_out, send, recv, local
+    self_w, cross_w, feed_w, mem_in, self_out, cross_out, feed_out, mem_out,
+    self_in, cross_in, feed_in, send, recv, local,
 ):
     dp, fs, z, y, x, c = place()
+    per = self_in.shape[2] // LANES
+    rows_of(self_w, self_in, 0, 0, per)
+    rows_of(cross_w, cross_in, 0, 0, per)
+    for up in (True, False):
+
+        @pl.when(z // 2 == (0 if up else 1))
+        def _():
+            for j in range(4):
+                rows_of(feed_w, feed_in, j, *feed_lines(j, *feed_in.shape[1:], up))
+
     ndp = mem_out.shape[1]
     ex = mem_out.shape[0]
     to_y, to_x, to_c = peer_id(z, 1 - y, x, c), peer_id(z, y, 1 - x, c), peer_id(z, y, x, 1 - c)
     greet([((dp + k) % ndp, fs) for k in range(1, ndp)] + [to_x, to_c])
     cp = Copies(send, recv, local)
 
+    step = feed_in.shape[1]
+    cut = step * 2 // 3
     chunks = []
-    for src, dst, js in (
-        (self_in, self_out, (0, 1)),
-        (cross_in, cross_out, (0, 1)),
-        (feed_in, feed_out, (0, 2)),
-        (feed_in, feed_out, (2, 2)),
-    ):
-        rows = src.shape[1]
-        cut = rows * 2 // 3
-        chunks.append((src, dst, pl.ds(*js), pl.ds(0, cut), pl.ds(cut, rows - cut)))
-
-    own = [cp.here(chunk[0].at[chunk[2]], chunk[1].at[z, y, x, c, chunk[2]]) for chunk in chunks]
+    for src, dst in ((self_in, self_out), (cross_in, cross_out), (feed_in, feed_out)):
+        for j in range(src.shape[0]):
+            for first in range(0, src.shape[1], step):
+                chunks.append(
+                    (src, dst, j, pl.ds(first, step), pl.ds(first, cut), pl.ds(first + cut, step - cut))
+                )
+
+    own = [
+        cp.here(src.at[j, rows], dst.at[z, y, x, c, j, rows]) for src, dst, j, rows, _, _ in chunks
+    ]
     own_mem = cp.here(mem_in.at[pl.ds(ex * dp, ex)], mem_out.at[:, dp])
 
-    zc, s2, s3, s4 = {}, {}, {}, {}
+    zc, s2, s3, s4, mem = {}, {}, {}, {}, []
 
     def send_z(t):
-        src, dst, js, r0, r1 = chunks[t]
+        src, dst, j, rows, r0, r1 = chunks[t]
         for k in range(1, NZ):
             zc[t, k] = cp.remote(
-                src.at[js], dst.at[z, y, x, c, js], peer_id((z + k) % NZ, y, x, c)
+                src.at[j, rows], dst.at[z, y, x, c, j, rows], peer_id((z + k) % NZ, y, x, c)
             )
 
     def send_2(t, k):
-        src, dst, js, r0, r1 = chunks[t]
+        src, dst, j, rows, r0, r1 = chunks[t]
         zz = (z + NZ - k) % NZ
-        for part, rows, where in ((0, r0, to_y), (1, r1, to_x)):
-            here = src.at[js, rows] if k == 0 else dst.at[zz, y, x, c, js, rows]
-            s2[t, k, part] = cp.remote(here, dst.at[zz, y, x, c, js, rows], where)
+        for part, cut_rows, where in ((0, r0, to_y), (1, r1, to_x)):
+            here = src.at[j, cut_rows] if k == 0 else dst.at[zz, y, x, c, j, cut_rows]
+            s2[t, k, part] = cp.remote(here, dst.at[zz, y, x, c, j, cut_rows], where)
 
     def send_3(t):
-        src, dst, js, r0, r1 = chunks[t]
-        s3[t, 0] = cp.remote(
-            dst.at[:, :, x, c, js, r0], dst.at[:, :, x, c, js, r0], to_x
-        )
-        s3[t, 1] = cp.remote(
-            dst.at[:, y, :, c, js, r1], dst.at[:, y, :, c, js, r1], to_y
-        )
+        src, dst, j, rows, r0, r1 = chunks[t]
+        s3[t, 0] = cp.remote(dst.at[:, :, x, c, j, r0], dst.at[:, :, x, c, j, r0], to_x)
+        s3[t, 1] = cp.remote(dst.at[:, y, :, c, j, r1], dst.at[:, y, :, c, j, r1], to_y)
 
     def send_4(t):
-        src, dst, js, r0, r1 = chunks[t]
-        s4[t] = cp.remote(dst.at[:, :, :, c, js], dst.at[:, :, :, c, js], to_c)
+        src, dst, j, rows, r0, r1 = chunks[t]
+        s4[t] = cp.remote(dst.at[:, :, :, c, j, rows], dst.at[:, :, :, c, j, rows], to_c)
+
+    def send_mem():
+        for k in range(1, ndp):
+            mem.append(
+                cp.remote(
+                    mem_in.at[pl.ds(ex * ((dp + k) % ndp), ex)],
+                    mem_out.at[:, dp],
+                    ((dp + k) % ndp, fs),
+                )
+            )
 
     n = len(chunks)
-    for t in range(n):
+    for t in range(min(AHEAD, n)):
         send_z(t)
         send_2(t, 0)
-    mem = [
-        cp.remote(
-            mem_in.at[pl.ds(ex * ((dp + k) % ndp), ex)],
-            mem_out.at[:, dp],
-            ((dp + k) % ndp, fs),
-        )
-        for k in range(1, ndp)
-    ]
     for t in range(n + 2):
+        if t == MEM_AT:
+            send_mem()
         if t < n:
             for k in range(1, NZ):
                 zc[t, k].wait_recv()
                 send_2(t, k)
+            if t + AHEAD < n:
+                send_z(t + AHEAD)
+                send_2(t + AHEAD, 0)
         if 1 <= t <= n:
             own[t - 1].wait()
             for k in range(NZ):
@@ -553,37 +585,33 @@
     cp.drain()
 
 
-def gather_all(self_in, cross_in, feed_in, mem_in, ndp):
+def gather_all(self_w, cross_w, feed_w, mem_in, rows_a, rows_f, ndp):
     any_space = pl.BlockSpec(memory_space=pl.ANY)
-    shards_of = lambda a: jax.ShapeDtypeStruct((NZ, 2, 2, 2) + a.shape, BF)
+    vmem = pl.BlockSpec(memory_space=pltpu.VMEM)
+    width = mem_in.shape[2]
+    kinds = ((1, rows_a, width), (1, rows_a, width), (4, rows_f, width))
     ex = mem_in.shape[0] // ndp
     return pl.pallas_call(
         gather_kernel,
         out_shape=[
-            shards_of(self_in),
-            shards_of(cross_in),
-            shards_of(feed_in),
+            *[jax.ShapeDtypeStruct((NZ, 2, 2, 2) + kind, BF) for kind in kinds],
             jax.ShapeDtypeStruct((ex, ndp) + mem_in.shape[1:], BF),
         ],
-        in_specs=[any_space] * 4,
+        in_specs=[vmem] * 3 + [any_space],
         out_specs=[any_space] * 4,
         scratch_shapes=[
-            pltpu.SemaphoreType.DMA((72,)),
-            pltpu.SemaphoreType.DMA((72,)),
-            pltpu.SemaphoreType.DMA((8,)),
+            *[pltpu.VMEM(kind, BF) for kind in kinds],
+            pltpu.SemaphoreType.DMA((128,)),
+            pltpu.SemaphoreType.DMA((128,)),
+            pltpu.SemaphoreType.DMA((16,)),
         ],
         compiler_params=pltpu.CompilerParams(collective_id=1, has_side_effects=True),
         name="gather_all",
-    )(self_in, cross_in, feed_in, mem_in)
+    )(self_w, cross_w, feed_w, mem_in)
 
 
 def squares(v):
-    rows, cols = v.shape
-    w = jnp.sum((v * v).reshape(rows // 8, 8, cols), axis=0)
-    total = w[:, 0:128]
-    for i in range(1, cols // 128):
-        total = total + w[:, i * 128 : (i + 1) * 128]
-    return total
+    return jnp.sum((v * v).reshape(v.shape[0] // 8, 8, LANES), axis=0)
 
 
 def sum_everywhere(cp, mine, slots_a, slots_b, dp, fs):
@@ -609,282 +637,315 @@
     return total
 
 
+def lamb_sums(w, g, m, s, factor):
+    ratio = lamb_step(w[...], g[...], m[...], s[...], factor)[2]
+    return jnp.sum(ratio * ratio, axis=0, keepdims=True)
+
+
 def scatter_kernel(
     qkv_g, out_g, cq_g, ckv_g, co_g, up_g, dn_g, mem_g, vec,
-    self_t, cross_t, feed_t, mem_t, vec_t, sq_t,
-    send, recv, local,
-    acc_s, acc_c, acc_f0, acc_f1, r1_s, r1_c, r1_f0, r1_f1,
-    r2a_s, r2a_c, r2a_f0, r2a_f1, r2b_s, r2b_c, r2b_f0, r2b_f1,
-    r3a_s, r3a_c, r3a_f0, r3a_f1, r3b_s, r3b_c, r3b_f0, r3b_f1,
-    rz_s, rz_c, rz_f0, rz_f1,
-    v_send, v_recv, v_z, slots_a, slots_b,
+    ws, wc, wf, ms, mc, mf, ss, sc_, sf,
+    self_t, cross_t, feed_t, mem_t, vec_t, sq_t, norm_t,
+    send, recv, local, acc, r1, r2a, r2b, r3a, r3b, rz, whole,
+    v_send, v_recv, v_z, vw, qa, qb, na, nb, opt_s, opt_c, opt_f, opt_sem,
 ):
     dp, fs, z, y, x, c = place()
-    ndp = mem_g.shape[1]
+    ndp, nfs = mem_g.shape[1], qa.shape[0]
     ex = mem_g.shape[0]
+    step, width = acc.shape[4], acc.shape[5]
+    cut = step * 2 // 3
+    head, rest = pl.ds(0, cut), pl.ds(cut, step - cut)
+    per = width // LANES
     to_y, to_x, to_c = peer_id(z, 1 - y, x, c), peer_id(z, y, 1 - x, c), peer_id(z, y, x, 1 - c)
-    nfs = slots_a.shape[0]
     greet(
         [((dp + k) % ndp, fs) for k in range(1, ndp)] + [(dp, (fs + k) % nfs) for k in range(1, nfs)]
     )
     cp = Copies(send, recv, local)
 
-    def self_src(zz, j, cc):
-        return qkv_g.at[zz, :, :, cc] if zz < 3 else out_g.at[:, :, cc]
-
-    def cross_src(zz, j, cc):
-        if zz == 0:
-            return cq_g.at[:, :, cc]
-        return ckv_g.at[zz - 1, :, :, cc] if zz < 3 else co_g.at[:, :, cc]
-
-    def feed_src(first):
-        def src(zz, j, cc):
-            if zz < 2:
-                return up_g.at[first + j, zz, :, :, cc]
-            return dn_g.at[zz - 2, :, :, cc, first + j]
+    def self_src(r):
+        rows = pl.ds(r * step, step)
+        return lambda zz, cc: qkv_g.at[zz, :, :, cc, rows] if zz < 3 else out_g.at[:, :, cc, rows]
+
+    def cross_src(r):
+        rows = pl.ds(r * step, step)
+
+        def src(zz, cc):
+            if zz == 0:
+                return cq_g.at[:, :, cc, rows]
+            return ckv_g.at[zz - 1, :, :, cc, rows] if zz < 3 else co_g.at[:, :, cc, rows]
 
         return src
 
-    chunks = (
-        (feed_src(0), acc_f0, r1_f0, r2a_f0, r2b_f0, r3a_f0, r3b_f0, rz_f0),
-        (feed_src(2), acc_f1, r1_f1, r2a_f1, r2b_f1, r3a_f1, r3b_f1, rz_f1),
-        (cross_src, acc_c, r1_c, r2a_c, r2b_c, r3a_c, r3b_c, rz_c),
-        (self_src, acc_s, r1_s, r2a_s, r2b_s, r3a_s, r3b_s, rz_s),
-    )
-    n = len(chunks)
+    def feed_src(j):
+        return lambda zz, cc: up_g.at[j, zz, :, :, cc] if zz < 2 else dn_g.at[zz - 2, :, :, cc, j]
+
+    sources = [feed_src(j) for j in range(4)]
+    sources += [cross_src(r) for r in range(2)] + [self_src(r) for r in range(2)]
+    n = len(sources)
     sc, sl, s1, s2, sz = {}, {}, {}, {}, {}
 
-    vcp = cp.remote(vec, v_recv.at[0], to_c)
-    for t, (src, acc, r1, *_) in enumerate(chunks):
+    def phase_0(t):
         for zz in range(NZ):
-            for j in range(acc.shape[3]):
-                sc[t, zz, j] = cp.remote(src(zz, j, 1 - c), r1.at[zz, :, :, j], to_c)
-                sl[t, zz, j] = cp.here(src(zz, j, c), acc.at[zz, :, :, j])
+            sc[t, zz] = cp.remote(sources[t](zz, 1 - c), r1.at[t, zz], to_c)
+            sl[t, zz] = cp.here(sources[t](zz, c), acc.at[t, zz])
+
+    def add_c(t, fixed_y, fixed_x, rows):
+        def body(i, _):
+            zz, o = i // 2, i % 2
+            yy = o if fixed_y is None else fixed_y
+            xx = o if fixed_x is None else fixed_x
+            acc[t, zz, yy, xx, rows] = acc[t, zz, yy, xx, rows] + r1[t, zz, yy, xx, rows]
+            return 0
+
+        lax.fori_loop(0, NZ * 2, body, 0)
+
+    def phase_c(t):
+        for zz in range(NZ):
+            sc[t, zz].wait_recv()
+            sl[t, zz].wait()
+        add_c(t, None, 1 - x, head)
+        s1[t, 0] = cp.remote(acc.at[t, :, :, 1 - x, head], r2a.at[t], to_x)
+        add_c(t, 1 - y, None, rest)
+        s1[t, 1] = cp.remote(acc.at[t, :, 1 - y, :, rest], r2b.at[t], to_y)
+        add_c(t, None, x, head)
+        add_c(t, y, None, rest)
+
+    def add_1(t, yy, xx, rows, got, where):
+        def body(zz, _):
+            acc[t, zz, yy, xx, rows] = acc[t, zz, yy, xx, rows] + got[t, zz, where]
+            return 0
+
+        lax.fori_loop(0, NZ, body, 0)
+
+    def phase_1(t):
+        s1[t, 0].wait_recv()
+        add_1(t, 1 - y, x, head, r2a, 1 - y)
+        s2[t, 0] = cp.remote(acc.at[t, :, 1 - y, x, head], r3a.at[t], to_y)
+        s1[t, 1].wait_recv()
+        add_1(t, y, 1 - x, rest, r2b, 1 - x)
+        s2[t, 1] = cp.remote(acc.at[t, :, y, 1 - x, rest], r3b.at[t], to_x)
+        add_1(t, y, x, head, r2a, y)
+        add_1(t, y, x, rest, r2b, x)
+
+    def phase_2(t):
+        s2[t, 0].wait_recv()
+        s2[t, 1].wait_recv()
+
+        def body(zz, _):
+            acc[t, zz, y, x, head] = acc[t, zz, y, x, head] + r3a[t, zz]
+            acc[t, zz, y, x, rest] = acc[t, zz, y, x, rest] + r3b[t, zz]
+            return 0
+
+        lax.fori_loop(0, NZ, body, 0)
+        for k in range(1, NZ):
+            zt = (z + k) % NZ
+            sz[t, k] = cp.remote(acc.at[t, zt, y, x], rz.at[t, k - 1], peer_id(zt, y, x, c))
+
+    def lines_of(dst, start, stride):
+        for i in range(per):
+            dst[pl.ds(start + i, step, stride=stride), :] = whole[:, i * LANES : (i + 1) * LANES]
+
+    def phase_z(t):
+        for k in range(1, NZ):
+            sz[t, k].wait_recv()
+        total = acc[t, z, y, x].astype(F32)
+        for k in range(1, NZ):
+            total = total + rz[t, k - 1].astype(F32)
+        whole[...] = total
+        if t >= 4:
+            lines_of((cross_t, self_t)[t // 2 - 2], (t % 2) * step * per, per)
+            return
+        for up in (True, False):
+
+            @pl.when(z // 2 == (0 if up else 1))
+            def _():
+                lines_of(feed_t, *feed_lines(t, step, width, up))
+
+    ahead = 2
+    for t in range(ahead):
+        phase_0(t)
+    vec_cp = [cp.remote(vec, v_recv.at[0], to_c)]
     own_mem = cp.here(mem_g.at[:, dp], mem_t.at[pl.ds(ex * dp, ex)])
     mem = [
         cp.remote(mem_g.at[:, (dp + k) % ndp], mem_t.at[pl.ds(ex * dp, ex)], ((dp + k) % ndp, fs))
         for k in range(1, ndp)
     ]
-
-    def cuts(acc):
-        rows = acc.shape[4]
-        cut = rows * 2 // 3
-        return pl.ds(0, cut), pl.ds(cut, rows - cut)
-
-    def add_c(acc, r1, fixed_y, fixed_x, rows):
-        def body(i, _):
-            zz, o = i // 2, i % 2
-            yy = o if fixed_y is None else fixed_y
-            xx = o if fixed_x is None else fixed_x
-            for j in range(acc.shape[3]):
-                acc[zz, yy, xx, j, rows] = acc[zz, yy, xx, j, rows] + r1[zz, yy, xx, j, rows]
-            return 0
-
-        lax.fori_loop(0, NZ * 2, body, 0)
-
-    def phase_c(t):
-        src, acc, r1, r2a, r2b, *_ = chunks[t]
-        r0, r1_rows = cuts(acc)
-        for zz in range(NZ):
-            for j in range(acc.shape[3]):
-                sc[t, zz, j].wait_recv()
-                sl[t, zz, j].wait()
-        add_c(acc, r1, None, 1 - x, r0)
-        s1[t, 0] = cp.remote(acc.at[:, :, 1 - x, :, r0], r2a, to_x)
-        add_c(acc, r1, 1 - y, None, r1_rows)
-        s1[t, 1] = cp.remote(acc.at[:, 1 - y, :, :, r1_rows], r2b, to_y)
-        add_c(acc, r1, None, x, r0)
-        add_c(acc, r1, y, None, r1_rows)
-
-    def phase_1(t):
-        src, acc, r1, r2a, r2b, r3a, r3b, rz = chunks[t]
-        r0, r1_rows = cuts(acc)
-
-        def body_a(yy):
-            def body(zz, _):
-                for j in range(acc.shape[3]):
-                    acc[zz, yy, x, j, r0] = acc[zz, yy, x, j, r0] + r2a[zz, yy, j]
-                return 0
-
-            return body
-
-        def body_b(xx):
-            def body(zz, _):
-                for j in range(acc.shape[3]):
-                    acc[zz, y, xx, j, r1_rows] = acc[zz, y, xx, j, r1_rows] + r2b[zz, xx, j]
-                return 0
-
-            return body
-
-        s1[t, 0].wait_recv()
-        lax.fori_loop(0, NZ, body_a(1 - y), 0)
-        s2[t, 0] = cp.remote(acc.at[:, 1 - y, x, :, r0], r3a, to_y)
-        s1[t, 1].wait_recv()
-        lax.fori_loop(0, NZ, body_b(1 - x), 0)
-        s2[t, 1] = cp.remote(acc.at[:, y, 1 - x, :, r1_rows], r3b, to_x)
-        lax.fori_loop(0, NZ, body_a(y), 0)
-        lax.fori_loop(0, NZ, body_b(x), 0)
-
-    def phase_2(t):
-        src, acc, r1, r2a, r2b, r3a, r3b, rz = chunks[t]
-        r0, r1_rows = cuts(acc)
-        s2[t, 0].wait_recv()
-        s2[t, 1].wait_recv()
-
-        def body(zz, _):
-            for j in range(acc.shape[3]):
-                acc[zz, y, x, j, r0] = acc[zz, y, x, j, r0] + r3a[zz, j]
-                acc[zz, y, x, j, r1_rows] = acc[zz, y, x, j, r1_rows] + r3b[zz, j]
-            return 0
-
-        lax.fori_loop(0, NZ, body, 0)
-        for k in range(1, NZ):
-            zt = (z + k) % NZ
-            sz[t, k] = cp.remote(acc.at[zt, y, x], rz.at[k - 1], peer_id(zt, y, x, c))
-
-    sums = []
-
-    def phase_z(t, out, first):
-        src, acc, r1, r2a, r2b, r3a, r3b, rz = chunks[t]
-        for k in range(1, NZ):
-            sz[t, k].wait_recv()
-        for j in range(acc.shape[3]):
-            total = acc[z, y, x, j].astype(F32)
+    groups = (
+        ((ws, ms, ss), opt_s, self_t, z),
+        ((wc, mc, sc_), opt_c, cross_t, NZ + z),
+        ((wf, mf, sf), opt_f, feed_t, 2 * NZ + z // 2),
+    )
+    opt = []
+    for g, (srcs, dst, _, _) in enumerate(groups):
+        for i, src in enumerate(srcs):
+            opt.append(pltpu.make_async_copy(src, dst.at[i], opt_sem.at[3 * g + i]))
+            opt[-1].start()
+
+    def vec_step(i):
+        vec_cp[-1].wait_recv()
+        v_send[i] = (vec[...] if i == 0 else v_send[i - 1]) + v_recv[i]
+        if i < 2:
+            vec_cp.append(cp.remote(v_send.at[i], v_recv.at[i + 1], (to_x, to_y)[i]))
+        else:
+            v_z[z] = v_send[2]
             for k in range(1, NZ):
-                total = total + rz[k - 1, j].astype(F32)
-            out[first + j] = total
-            sums.append(squares(total))
-
-    def vec_step(i):
-        nonlocal vcp
-        vcp.wait_recv()
-        if i < 3:
-            before = vec[...] if i == 0 else v_send[i - 1]
-            v_send[i] = before + v_recv[i]
-            if i < 2:
-                vcp = cp.remote(v_send.at[i], v_recv.at[i + 1], (to_x, to_y)[i])
+                vec_cp.append(
+                    cp.remote(v_send.at[2], v_z.at[z], peer_id((z + k) % NZ, y, x, c))
+                )
 
     for t in range(n + 3):
         if t < n:
             phase_c(t)
-        if t < 3:
-            vec_step(t)
-        if t == 2:
-            v_z[z] = v_send[2]
-            vz = [
-                cp.remote(v_send.at[2], v_z.at[z], peer_id((z + k) % NZ, y, x, c))
-                for k in range(1, NZ)
-            ]
+            if t + ahead < n:
+                phase_0(t + ahead)
+        if 1 <= t <= 3:
+            vec_step(t - 1)
         if 1 <= t <= n:
             phase_1(t - 1)
         if 2 <= t <= n + 1:
             phase_2(t - 2)
         if t >= 3:
-            phase_z(t - 3, (feed_t, feed_t, cross_t, self_t)[t - 3], (0, 2, 0, 0)[t - 3])
-    for one in vz:
+            phase_z(t - 3)
+    for one in vec_cp[3:]:
         one.wait_recv()
-    vec_t[...] = (v_z[0] + v_z[1]) + (v_z[2] + v_z[3])
-    total = sums[0]
-    for one in sums[1:]:
-        total = total + one
-    sq_t[...] = sum_everywhere(cp, total, slots_a, slots_b, dp, fs)
+    vw[...] = (v_z[0] + v_z[1]) + (v_z[2] + v_z[3])
+    vec_t[...] = jnp.zeros_like(vec_t)
+    for i in range(per):
+        vec_t[pl.ds(i, 11, stride=per), :] = vw[0:11, i * LANES : (i + 1) * LANES]
+    sq = squares(self_t[...]) + squares(cross_t[...]) + squares(feed_t[...])
+    sq = sum_everywhere(cp, sq, qa, qb, dp, fs) + squares(vec_t[...])
+    sq_t[...] = sq
+    factor = clip_of(sq)
+    rows = lax.broadcasted_iota(jnp.int32, (32, LANES), 0)
+    tile = jnp.zeros((32, LANES), F32)
+    for one in opt:
+        one.wait()
+    for _, dst, g, row in groups:
+        w = dst[0]
+        part = lamb_sums(dst.at[0], g, dst.at[1], dst.at[2], factor)
+        tile = tile + jnp.where(rows == row, part, 0.0)
+        part = jnp.sum(w * w, axis=0, keepdims=True)
+        tile = tile + jnp.where(rows == 16 + row, part, 0.0)
+    norm_t[...] = sum_everywhere(cp, tile, na, nb, dp, fs)
     own_mem.wait()
     for one in mem:
         one.wait_recv()
     cp.drain()
 
 
-def scatter_all(grads, mem_g, vec, rows_a, rows_f, ndp, nfs):
+def norm_of(sq):
+    return jnp.sqrt(jnp.sum(jnp.sum(sq, axis=1, keepdims=True), axis=0, keepdims=True))
+
+
+def clip_of(sq):
+    return jnp.minimum(1.0, 1.0 / norm_of(sq))
+
+
+def scatter_all(grads, mem_g, vec, states, step, ndp, nfs):
     any_space = pl.BlockSpec(memory_space=pl.ANY)
     vmem = pl.BlockSpec(memory_space=pltpu.VMEM)
     ex, _, pos, width = mem_g.shape
-    kinds = ((1, rows_a), (1, rows_a), (2, rows_f), (2, rows_f))
-    acc = [pltpu.VMEM((NZ, 2, 2, j, r, width), BF) for j, r in kinds]
-    r2a = [pltpu.VMEM((NZ, 2, j, r * 2 // 3, width), BF) for j, r in kinds]
-    r2b = [pltpu.VMEM((NZ, 2, j, r - r * 2 // 3, width), BF) for j, r in kinds]
-    r3a = [pltpu.VMEM((NZ, j, r * 2 // 3, width), BF) for j, r in kinds]
-    r3b = [pltpu.VMEM((NZ, j, r - r * 2 // 3, width), BF) for j, r in kinds]
-    rz = [pltpu.VMEM((NZ - 1, j, r, width), BF) for j, r in kinds]
+    lines = [w.shape[0] for w in states[:3]]
+    cut = step * 2 // 3
+    low = lambda *dims: pltpu.VMEM(dims + (width,), BF)
+    wide = lambda *dims: pltpu.VMEM(dims, F32)
+    shape = lambda *dims: jax.ShapeDtypeStruct(dims, F32)
+    vec_lines = (vec.shape[0] * width) // LANES
     return pl.pallas_call(
         scatter_kernel,
         out_shape=[
-            jax.ShapeDtypeStruct((1, rows_a, width), F32),
-            jax.ShapeDtypeStruct((1, rows_a, width), F32),
-            jax.ShapeDtypeStruct((4, rows_f, width), F32),
+            *[shape(k, LANES) for k in lines],
             jax.ShapeDtypeStruct((ndp * ex, pos, width), BF),
-            jax.ShapeDtypeStruct(vec.shape, F32),
-            jax.ShapeDtypeStruct((8, 128), F32),
+            shape(vec_lines, LANES),
+            shape(8, LANES),
+            shape(32, LANES),
         ],
-        in_specs=[any_space] * 8 + [vmem],
-        out_specs=[vmem, vmem, vmem, any_space, vmem, vmem],
+        in_specs=[any_space] * 8 + [vmem] + [any_space] * 9,
+        out_specs=[vmem, vmem, vmem, any_space, vmem, vmem, vmem],
         scratch_shapes=[
-            pltpu.SemaphoreType.DMA((80,)),
-            pltpu.SemaphoreType.DMA((80,)),
-            pltpu.SemaphoreType.DMA((32,)),
-            *acc,
-            *acc,
-            *r2a,
-            *r2b,
-            *r3a,
-            *r3b,
-            *rz,
-            pltpu.VMEM((3,) + vec.shape, F32),
-            pltpu.VMEM((3,) + vec.shape, F32),
-            pltpu.VMEM((NZ,) + vec.shape, F32),
-            pltpu.VMEM((nfs, 8, 128), F32),
-            pltpu.VMEM((ndp, 8, 128), F32),
+            pltpu.SemaphoreType.DMA((128,)),
+            pltpu.SemaphoreType.DMA((128,)),
+            pltpu.SemaphoreType.DMA((40,)),
+            low(8, NZ, 2, 2, step),
+            low(8, NZ, 2, 2, step),
+            low(8, NZ, 2, cut),
+            low(8, NZ, 2, step - cut),
+            low(8, NZ, cut),
+            low(8, NZ, step - cut),
+            low(8, NZ - 1, step),
+            wide(step, width),
+            wide(3, *vec.shape),
+            wide(3, *vec.shape),
+            wide(NZ, *vec.shape),
+            wide(*vec.shape),
+            wide(nfs, 8, LANES),
+            wide(ndp, 8, LANES),
+            wide(nfs, 32, LANES),
+            wide(ndp, 32, LANES),
+            *[wide(3, k, LANES) for k in lines],
+            pltpu.SemaphoreType.DMA((9,)),
         ],
         compiler_params=pltpu.CompilerParams(
             collective_id=2, has_side_effects=True, vmem_limit_bytes=58 << 20
         ),
         name="scatter_all",
-    )(*grads, mem_g, vec)
-
-
-def ratio_kernel(
-    gs, gc, gf, ws, wc, wf, ms, mc, mf, vs, vc, vf, clip, out, send, recv, local, slots_a, slots_b
-):
-    dp, fs, z, y, x, c = place()
-    nfs, ndp = slots_a.shape[0], slots_b.shape[0]
-    greet(
-        [((dp + k) % ndp, fs) for k in range(1, ndp)] + [(dp, (fs + k) % nfs) for k in range(1, nfs)]
-    )
-    cp = Copies(send, recv, local)
-    factor = clip[0:1, 0:1]
-    rows = lax.broadcasted_iota(jnp.int32, (32, 128), 0)
-    tile = jnp.zeros((32, 128), F32)
-    for g, w, m, v, row in (
-        (gs, ws, ms, vs, z),
-        (gc, wc, mc, vc, NZ + z),
-        (gf, wf, mf, vf, 2 * NZ + z // 2),
-    ):
-        ratio = lamb_step(w[...], g[...], m[...], v[...], factor)[2]
-        for first, a in ((0, ratio), (16, w[...])):
-            part = jnp.sum(a * a, axis=0, keepdims=True)
-            tile = tile + jnp.where(rows == first + row, part, 0.0)
-    out[...] = sum_everywhere(cp, tile, slots_a, slots_b, dp, fs)
-    cp.drain()
-
-
-def ratio_all(args, clip, ndp, nfs):
+    )(*grads, mem_g, vec, *states)
+
+
+def update_kernel(*refs):
+    ins, outs = refs[:18], refs[18:]
+    gs, ws, ms, vs, (gv, sq, norms) = ins[0:3], ins[3:7], ins[7:11], ins[11:15], ins[15:18]
+    z = lax.axis_index("dp") // 2
+    factor = clip_of(sq[...])
+    sums = jnp.sqrt(jnp.sum(norms[...], axis=1, keepdims=True))
+    ratio_norm, weight_norm = sums[0:16], sums[16:32]
+    trust = weight_norm / (ratio_norm + trust_eps)
+    row = lax.broadcasted_iota(jnp.int32, (16, 1), 0)
+    for i, first in enumerate((z, NZ + z, 2 * NZ + z // 2)):
+        g = gs[i][...]
+        w = ws[i][...]
+        m, v, ratio = lamb_step(w, g, ms[i][...], vs[i][...], factor)
+        rate = jnp.sum(jnp.where(row == first, trust, 0.0), axis=0, keepdims=True)
+        for ref, value in zip(outs[4 * i : 4 * i + 4], (g, m, v, w - learn_rate * rate * ratio)):
+            ref[...] = value
+    w = ws[3][...]
+    g = gv[0 : w.shape[0], :]
+    m, v, ratio = lamb_step(w, g, ms[3][...], vs[3][...], factor)
+    line = lax.broadcasted_iota(jnp.int32, w.shape, 0)
+    spread = lax.broadcasted_iota(jnp.int32, (16, LANES), 1)
+    pick = spread == lax.broadcasted_iota(jnp.int32, (16, LANES), 0)
+    lanes = spread[0:1]
+    on_row = lambda a: jnp.sum(jnp.where(pick, a, 0.0), axis=0, keepdims=True)
+    weight_row, ratio_row = on_row(weight_norm), on_row(ratio_norm)
+    rate = jnp.zeros(w.shape, F32)
+    per = D // LANES
+    for i in range(8):
+        mine = (line >= i * per) & (line < ((i + 1) * per if i < 7 else w.shape[0]))
+        norm = lambda a: norm_of(jnp.where(mine, a * a, 0.0))
+        wn, rn = norm(w), norm(ratio)
+        rate = jnp.where(mine, wn / (rn + trust_eps), rate)
+        weight_row = jnp.where(lanes == 10 + i, wn, weight_row)
+        ratio_row = jnp.where(lanes == 10 + i, rn, ratio_row)
+    for ref, value in zip(outs[12:16], (g, m, v, w - learn_rate * rate * ratio)):
+        ref[...] = value
+    outs[16][0:1, :] = weight_row[:, 0:18]
+    outs[16][1:2, :] = ratio_row[:, 0:18]
+    outs[17][...] = norm_of(sq[...])
+
+
+def update_all(totals, weights, moments, seconds, vec_total, sq, norms):
     vmem = pl.BlockSpec(memory_space=pltpu.VMEM)
+    shape = lambda a: jax.ShapeDtypeStruct(a.shape, F32)
+    outs = [shape(a) for a in weights for _ in range(4)]
+    outs += [jax.ShapeDtypeStruct((2, 18), F32), jax.ShapeDtypeStruct((1, 1), F32)]
     return pl.pallas_call(
-        ratio_kernel,
-        out_shape=jax.ShapeDtypeStruct((32, 128), F32),
-        in_specs=[vmem] * 13,
-        out_specs=vmem,
-        scratch_shapes=[
-            pltpu.SemaphoreType.DMA((16,)),
-            pltpu.SemaphoreType.DMA((16,)),
-            pltpu.SemaphoreType.DMA((1,)),
-            pltpu.VMEM((nfs, 32, 128), F32),
-            pltpu.VMEM((ndp, 32, 128), F32),
-        ],
-        compiler_params=pltpu.CompilerParams(
-            collective_id=3, has_side_effects=True, vmem_limit_bytes=40 << 20
-        ),
-        name="ratio_all",
-    )(*args, clip)
+        update_kernel,
+        out_shape=outs,
+        in_specs=[vmem] * 18,
+        out_specs=[vmem] * len(outs),
+        compiler_params=pltpu.CompilerParams(vmem_limit_bytes=40 << 20),
+        name="update_all",
+    )(*totals, *weights, *moments, *seconds, vec_total, sq, norms)
 
 
 def dot_nn(a, b):
@@ -1030,6 +1091,8 @@
         ring[slot] = value.astype(BF)
         pending.append(pltpu.make_async_copy(ring.at[slot], dst, stores.at[slot]))
         pending[-1].start()
+
+    vecg_ref[8:16] = jnp.zeros((8, D), F32)
 
     def row(i):
         return vec_ref[i : i + 1, :]
@@ -1141,7 +1204,7 @@
         out_shape=[
             shape(rows, D, dtype=F32),
             shape(rows, D, dtype=F32),
-            shape(*vec.shape, dtype=F32),
+            shape(16, D, dtype=F32),
             shape(3, D, D),
             shape(D, D),
             shape(D, D),
@@ -1194,19 +1257,12 @@
     owners = ndp * nfs
     attn_shard, feed_shard = self_weights.shape[0], feed_weights.shape[0]
     rows_a, rows_f = attn_shard // D, feed_shard // (4 * D)
-    shard_index = lax.axis_index(("dp", "fsdp"))
-    feed_low = feed_weights.astype(BF)
-    feed_in = jnp.where(
-        shard_index < owners // 2,
-        feed_low.reshape(rows_f, 4, D).transpose(1, 0, 2),
-        feed_low.reshape(4, rows_f, D),
-    )
+    flat = lambda *group: [a.reshape(-1, 128) for a in group]
+    weights = flat(self_weights, cross_weights, feed_weights, vectors)
+    moments = flat(self_moment, cross_moment, feed_moment, vector_moment)
+    seconds = flat(self_second, cross_second, feed_second, vector_second)
     self_full, cross_full, feed_full, own_memory = gather_all(
-        self_weights.astype(BF).reshape(1, rows_a, D),
-        cross_weights.astype(BF).reshape(1, rows_a, D),
-        feed_in,
-        memory[0],
-        ndp,
+        *weights[:3], memory[0], rows_a, rows_f, ndp
     )
     lens = lambda a: jnp.broadcast_to(a[0][:, None, None], (EX_DEV, 8, 128))
     (
@@ -1224,11 +1280,8 @@
         feed_full.reshape(8, D, D),
         own_memory.reshape(EX_DEV * MEMLEN, D),
     )
-    vec_rows = vectors.shape[0] // 128
-    vec_pad = (vec_rows + 7) // 8 * 8
-    vector_in = jnp.pad(vector_partial.reshape(vec_rows, 128), ((0, vec_pad - vec_rows), (0, 0)))
     split = (2, 2, 2)
-    self_total, cross_total, feed_total, memory_back, vec_sum, squared = scatter_all(
+    *totals, memory_back, vec_sum, squared, norms = scatter_all(
         (
             qkv_g.reshape((3,) + split + (rows_a, D)),
             wo_g.reshape(split + (rows_a, D)),
@@ -1239,80 +1292,22 @@
             dn_g.reshape((2,) + split + (4, rows_f, D)),
         ),
         mem_g.reshape(EX_DEV, ndp, MEMLEN // ndp, D),
-        vector_in,
-        rows_a,
+        vector_partial,
+        weights[:3] + moments[:3] + seconds[:3],
         rows_f,
         ndp,
         nfs,
     )
-    memory_gradient = memory_back.astype(F32)[None]
-    self_total = self_total.reshape(-1)
-    cross_total = cross_total.reshape(-1)
-    feed_total = jnp.where(
-        shard_index < owners // 2, feed_total.transpose(1, 0, 2).reshape(-1), feed_total.reshape(-1)
-    )
-    vector_total = vec_sum[:vec_rows].reshape(-1)
-    squared_total = jnp.sum(squared) + jnp.sum(vector_total * vector_total)
-    global_norm = jnp.sqrt(squared_total)
-    clip_factor = jnp.minimum(1.0, 1.0 / global_norm)
-    flat = lambda *group: [a.reshape(-1, 128) for a in group]
-    sums = ratio_all(
-        flat(
-            self_total, cross_total, feed_total,
-            self_weights, cross_weights, feed_weights,
-            self_moment, cross_moment, feed_moment,
-            self_second, cross_second, feed_second,
-        ),
-        jnp.broadcast_to(clip_factor, (8, 128)),
-        ndp,
-        nfs,
-    )
-    norms = jnp.sqrt(jnp.sum(sums, axis=1))
-    ratio_norms, weight_norms = norms[0:10], norms[16:26]
-    trust_ratio = weight_norms / (ratio_norms + trust_eps)
-    z = shard_index // 8
-    new = []
-    for weights, total, moment, second, row in (
-        (self_weights, self_total, self_moment, self_second, z),
-        (cross_weights, cross_total, cross_moment, cross_second, 4 + z),
-        (feed_weights, feed_total, feed_moment, feed_second, 8 + z // 2),
-    ):
-        momentum, variance, ratio = lamb_step(weights, total, moment, second, clip_factor)
-        new += [total, momentum, variance, weights - learn_rate * trust_ratio[row] * ratio]
-    vector_momentum, vector_variance, vector_ratio = lamb_step(
-        vectors, vector_total, vector_moment, vector_second, clip_factor
-    )
-    edges = [0, D, 2 * D, 3 * D, 4 * D, 5 * D, 6 * D, 7 * D, 7 * D + FF]
-    vector_wn = []
-    vector_rn = []
-    new_pieces = []
-    for segment in range(8):
-        weight_part = vectors[edges[segment] : edges[segment + 1]]
-        ratio_part = vector_ratio[edges[segment] : edges[segment + 1]]
-        weight_norm = jnp.sqrt(jnp.sum(weight_part * weight_part))
-        ratio_norm = jnp.sqrt(jnp.sum(ratio_part * ratio_part))
-        piece_trust = weight_norm / (ratio_norm + trust_eps)
-        vector_wn.append(weight_norm)
-        vector_rn.append(ratio_norm)
-        new_pieces.append(weight_part - learn_rate * piece_trust * ratio_part)
-    vector_master = jnp.concatenate(new_pieces)
-    tensor_norms = jnp.stack(
-        [
-            jnp.concatenate([weight_norms, jnp.stack(vector_wn)]),
-            jnp.concatenate([ratio_norms, jnp.stack(vector_rn)]),
-        ]
+    *new, tensor_norms, global_norm = update_all(
+        totals, weights, moments, seconds, vec_sum, squared, norms
     )
     return (
         layer_output.reshape(1, EX_DEV, SUF, D),
         suffix_gradient.reshape(1, EX_DEV, SUF, D),
-        memory_gradient,
-        *new,
-        vector_total,
-        vector_momentum,
-        vector_variance,
-        vector_master,
+        memory_back.astype(F32)[None],
+        *[a.reshape(-1) for a in new],
         tensor_norms,
-        global_norm,
+        global_norm.reshape(()),
     )
 
 

time: 402 us -> 319 us (0.79)
  Pallas kernels: 328 us -> 301 us
  other arithmetic: 25 us -> 3.6 us
  local copies, waits for them, and re-layouts: 24 us -> 6.33 us
  between operations: 17.3 us -> 1.35 us
    pallas_call x3, Pallas kernels: 269 us -> 242 us  [the longest x1 128 us: scatter_all(): pl.pallas_call(scatter_kernel, out_shape=[*[shape(k, LANES) for k in line...]
    reshape x11 -> x0, local copies, waits for them, and re-layouts: 8.93 us -> none  [the longest x2 2.77 us: fast_shards(): feed_total.reshape(-1)]
    reduce_sum x7 -> x0, other arithmetic: 6.81 us -> none  [the longest x2 2.76 us: fast_shards(): weight_norm = jnp.sqrt(jnp.sum(weight_part * weight_part))]
    unnamed x8 -> x0, other arithmetic: 5.04 us -> none
where the time goes in v3:
time: 319 us; the launch traced here: 313 us
  Pallas kernels  301 us (94%)
  local copies, waits for them, and re-layouts  6.33 us (2%)
  other arithmetic  3.6 us (1%)
    pallas_call x1, Pallas kernels, scatter_all(): pl.pallas_call(scatter_kernel, out_shape=[*[shape(k, LANES) for k in line...  128 us
    pallas_call x1, Pallas kernels, gather_all(): pl.pallas_call(gather_kernel, out_shape=[*[jax.ShapeDtypeStruct((NZ, 2, 2...  111 us
    pallas_call x1, Pallas kernels, layer_all(): pl.pallas_call(layer_kernel, out_shape=[shape(rows, D, dtype=F32), shape(...  58.9 us

profile of v3, /device:TPU:0, one launch (start us, length us, event | category | flops | bytes accessed | tf_op | source)
XLA Modules:
  0.0 312.6 jit_solution(17935464088156874378)
XLA Ops:
  0.7 1.3 broadcast_in_dim.23.plen_ref
  2.0 1.3 broadcast_in_dim.21.slen_ref
  3.3 1.4 reshape.187.vec_ref
  4.7 111.1 %gather_all.1 = (bf16[4,2,2,2,1,96,768]{6,5,4,3,2,1,0:T(8,128)(2,1)}, bf16[4,2,2,2,1,96,768]{6,5,4,3,2,1,0:T(8,128)(2,1)}, bf16[4,2,2,2,4,48,768]{6,5,4,3,2,1,0:T(8,128)(2,1)}, bf16[4,8,32,768]{3,2,1,0:T(8,128)(2,1)}) custom-call(f32[576,128]{1,0:T(8,128)} %bitcast.55, f32[576,128]{1,0:T(8,128)} %bitcast.58, f32[1152,128]{1,0:T(8,128)} %bitcast.52, ...), custom_call_target="tpu_custom_call" | custom-call | tf_op jit(solution)/shard_map/gather_all/pallas_call | solution.py:594
  115.8 58.9 %layer_all.1 = (f32[256,768]{1,0:T(8,128)}, f32[256,768]{1,0:T(8,128)}, f32[16,768]{1,0:T(8,128)}, bf16[3,768,768]{2,1,0:T(8,128)(2,1)}, bf16[768,768]{1,0:T(8,1...) custom-call(bf16[256,768]{1,0:T(8,128)(2,1)} %bitcast.90, ...), custom_call_target="tpu_custom_call" | custom-call | tf_op jit(solution)/shard_map/layer_all/pallas_call | solution.py:1202
  174.7 0.0 copy-start.12
  174.8 0.0 copy-start.14
  174.8 0.0 copy-start.15
  174.8 128.5 %scatter_all.1 = (f32[576,128]{1,0:T(8,128)}, f32[576,128]{1,0:T(8,128)}, f32[1152,128]{1,0:T(8,128)}, bf16[32,32,768]{2,1,0:T(8,128)(2,1)}, f32[96,128]{1,0:T(8...) custom-call(bf16[3,2,2,2,96,768]{5,4,3,2,1,0:T(8,128)(2,1)} %bitcast.82, bf16[2,2,2,96,768]{4,3,2,1,0:T(8,128)(2,1)} %bitcast.87, ...), custom_call_target="tpu_custom_call" | custom-call | tf_op jit(solution)/shard_map/scatter_all/pallas_call | solution.py:854
  303.3 0.0 copy-start
  303.3 0.0 copy-start.1
  303.3 0.0 copy-start.2
  303.3 0.0 copy-start.3
  303.3 0.0 copy-start.4
  303.3 0.0 copy-start.5
  303.3 0.0 copy-start.6
  303.3 0.0 copy-start.7
  303.4 0.0 copy-start.8
  303.4 0.0 copy-start.9
  303.4 0.0 copy-start.10
  303.4 0.0 copy-start.11
  303.4 3.6 %bitcast_convert_fusion = f32[1,32,32,768]{3,2,1,0:T(8,128)} fusion(bf16[32,32,768]{2,1,0:T(8,128)(2,1)} %get-tuple-element.76), kind=kLoop, calls=%fused_computation | loop fusion | flops 786432 | bytes 4718592 | tf_op jit(solution)/shard_map/broadcast_in_dim | solution.py:1307
  307.0 0.0 copy-done.12
  307.0 0.0 copy-done.14
  307.0 0.0 copy-done.15
  307.0 0.0 copy-done
  307.0 0.0 copy-done.1
  307.0 0.0 copy-done.2
  307.0 0.0 copy-done.3
  307.1 0.0 copy-done.4
  307.1 0.0 copy-done.5
  307.1 0.0 copy-done.6
  307.1 0.0 copy-done.7
  307.1 0.0 copy-done.8
  307.1 0.0 copy-done.9
  307.1 0.0 copy-done.10
  307.1 0.0 copy-done.11
  307.1 0.0 copy-start.13
  307.1 0.8 copy-done.13
  307.9 0.0 copy-start.16
  307.9 0.7 copy-done.16
  308.6 0.0 copy-start.17
  308.7 0.7 copy-done.17
  309.3 2.9 update_all.1
Async XLA Ops:
  174.7 132.3 %copy-start.12 = (f32[8448]{0:T(1024)S(1)}, f32[8448]{0:T(1024)}, u32[]{:S(2)}) copy-start(f32[8448]{0:T(1024)} %param.31) | copy-start | bytes 101380
  174.8 132.2 %copy-start.14 = (f32[8448]{0:T(1024)S(1)}, f32[8448]{0:T(1024)}, u32[]{:S(2)}) copy-start(f32[8448]{0:T(1024)} %param.32) | copy-start | bytes 101380
  174.8 132.2 %copy-start.15 = (f32[8448]{0:T(1024)S(1)}, f32[8448]{0:T(1024)}, u32[]{:S(2)}) copy-start(f32[8448]{0:T(1024)} %param.33) | copy-start | bytes 101380
  303.3 3.8 %copy-start = (f32[147456]{0:T(1024)S(1)}, f32[147456]{0:T(1024)}, u32[]{:S(2)}) copy-start(f32[147456]{0:T(1024)} %param.28) | copy-start | bytes 1769476
  303.3 3.8 %copy-start.1 = (f32[73728]{0:T(1024)S(1)}, f32[73728]{0:T(1024)}, u32[]{:S(2)}) copy-start(f32[73728]{0:T(1024)} %param.22) | copy-start | bytes 884740
  303.3 3.8 %copy-start.2 = (f32[73728]{0:T(1024)S(1)}, f32[73728]{0:T(1024)}, u32[]{:S(2)}) copy-start(f32[73728]{0:T(1024)} %param.25) | copy-start | bytes 884740
  303.3 3.8 %copy-start.3 = (f32[147456]{0:T(1024)S(1)}, f32[147456]{0:T(1024)}, u32[]{:S(2)}) copy-start(f32[147456]{0:T(1024)} %param.29) | copy-start | bytes 1769476
  303.3 3.7 %copy-start.4 = (f32[147456]{0:T(1024)S(1)}, f32[147456]{0:T(1024)}, u32[]{:S(2)}) copy-start(f32[147456]{0:T(1024)} %param.30) | copy-start | bytes 1769476
  303.3 3.7 %copy-start.5 = (f32[73728]{0:T(1024)S(1)}, f32[73728]{0:T(1024)}, u32[]{:S(2)}) copy-start(f32[73728]{0:T(1024)} %param.23) | copy-start | bytes 884740
  303.3 3.7 %copy-start.6 = (f32[73728]{0:T(1024)S(1)}, f32[73728]{0:T(1024)}, u32[]{:S(2)}) copy-start(f32[73728]{0:T(1024)} %param.26) | copy-start | bytes 884740
  303.3 3.7 %copy-start.7 = (f32[73728]{0:T(1024)S(1)}, f32[73728]{0:T(1024)}, u32[]{:S(2)}) copy-start(f32[73728]{0:T(1024)} %param.24) | copy-start | bytes 884740
  303.4 3.7 %copy-start.8 = (f32[73728]{0:T(1024)S(1)}, f32[73728]{0:T(1024)}, u32[]{:S(2)}) copy-start(f32[73728]{0:T(1024)} %param.27) | copy-start | bytes 884740
  303.4 3.7 %copy-start.9 = (f32[1152,128]{1,0:T(8,128)S(1)}, f32[1152,128]{1,0:T(8,128)}, u32[]{:S(2)}) copy-start(f32[1152,128]{1,0:T(8,128)} %get-tuple-element.79.refs_2_) | copy-start | bytes 1769476
  303.4 3.7 %copy-start.10 = (f32[576,128]{1,0:T(8,128)S(1)}, f32[576,128]{1,0:T(8,128)}, u32[]{:S(2)}) copy-start(f32[576,128]{1,0:T(8,128)} %get-tuple-element.77.refs_0_) | copy-start | bytes 884740
  303.4 3.7 %copy-start.11 = (f32[576,128]{1,0:T(8,128)S(1)}, f32[576,128]{1,0:T(8,128)}, u32[]{:S(2)}) copy-start(f32[576,128]{1,0:T(8,128)} %get-tuple-element.78.refs_1_) | copy-start | bytes 884740
  307.1 0.8 copy-start.13
  307.9 0.7 copy-start.16
  308.6 0.7 copy-start.17

commit v4 on v0

--- a/solution.py
+++ b/solution.py
@@ -1,6 +1,8 @@
 import jax
 import jax.numpy as jnp
 from jax import lax
+from jax.experimental import pallas as pl
+from jax.experimental.pallas import tpu as pltpu
 from jax.sharding import PartitionSpec as P
 
 D = 768
@@ -409,9 +411,1100 @@
     )
 
 
+BF = jnp.bfloat16
+F32 = jnp.float32
+MESH = pl.DeviceIdType.MESH
+NZ = 4
+AHEAD = 6
+MEM_AT = 3
+
+
+def place():
+    dp, fs = lax.axis_index("dp"), lax.axis_index("fsdp")
+    return dp, fs, dp // 2, dp % 2, fs // 2, fs % 2
+
+
+def peer_id(z, y, x, c):
+    return (z * 2 + y, x * 2 + c)
+
+
+def greet(ids):
+    bar = pltpu.get_barrier_semaphore()
+    for where in ids:
+        pl.semaphore_signal(bar, inc=1, device_id=where, device_id_type=MESH)
+    pl.semaphore_wait(bar, len(ids))
+
+
+class Copies:
+    def __init__(self, send, recv, local):
+        self.send, self.recv, self.local = send, recv, local
+        self.remotes, self.locals = 0, 0
+        self.open = []
+
+    def remote(self, src, dst, where):
+        i = self.remotes
+        self.remotes += 1
+        cp = pltpu.make_async_remote_copy(
+            src_ref=src,
+            dst_ref=dst,
+            send_sem=self.send.at[i],
+            recv_sem=self.recv.at[i],
+            device_id=where,
+            device_id_type=MESH,
+        )
+        cp.start()
+        self.open.append(cp)
+        return cp
+
+    def here(self, src, dst):
+        cp = pltpu.make_async_copy(src, dst, self.local.at[self.locals])
+        self.locals += 1
+        cp.start()
+        return cp
+
+    def drain(self):
+        for cp in self.open:
+            cp.wait_send()
+
+
+LANES = 128
+
+
+def rows_of(flat, dst, j, start, stride):
+    rows, width = dst.shape[1:]
+    for i in range(width // LANES):
+        part = flat[pl.ds(start + i, rows, stride=stride), :]
+        dst[j, :, i * LANES : (i + 1) * LANES] = part.astype(dst.dtype)
+
+
+def feed_lines(j, rows, width, up):
+    per = width // LANES
+    return (j * per, 4 * per) if up else (j * rows * per, per)
+
+
+def squares(v):
+    return jnp.sum((v * v).reshape(v.shape[0] // 8, 8, LANES), axis=0)
+
+
+def sum_everywhere(cp, mine, slots_a, slots_b, dp, fs):
+    nfs, ndp = slots_a.shape[0], slots_b.shape[0]
+    slots_a[fs] = mine
+    got = [
+        cp.remote(slots_a.at[fs], slots_a.at[fs], (dp, (fs + k) % nfs)) for k in range(1, nfs)
+    ]
+    for one in got:
+        one.wait_recv()
+    total = slots_a[0]
+    for k in range(1, nfs):
+        total = total + slots_a[k]
+    slots_b[dp] = total
+    got = [
+        cp.remote(slots_b.at[dp], slots_b.at[dp], ((dp + k) % ndp, fs)) for k in range(1, ndp)
+    ]
+    for one in got:
+        one.wait_recv()
+    total = slots_b[0]
+    for k in range(1, ndp):
+        total = total + slots_b[k]
+    return total
+
+
+def lamb_sums(w, g, m, s, factor):
+    ratio = lamb_step(w[...], g[...], m[...], s[...], factor)[2]
+    return jnp.sum(ratio * ratio, axis=0, keepdims=True)
+
+
+def norm_of(sq):
+    return jnp.sqrt(jnp.sum(jnp.sum(sq, axis=1, keepdims=True), axis=0, keepdims=True))
+
+
+def clip_of(sq):
+    return jnp.minimum(1.0, 1.0 / norm_of(sq))
+
+
+def dot_nn(a, b):
+    return lax.dot_general(a, b, (((1,), (0,)), ((), ())), preferred_element_type=F32)
+
+
+def dot_nt(a, b):
+    return lax.dot_general(a, b, (((1,), (1,)), ((), ())), preferred_element_type=F32)
+
+
+def dot_tn(a, b):
+    return lax.dot_general(a, b, (((0,), (0,)), ((), ())), preferred_element_type=F32)
+
+
+def norm_parts(values):
+    centred = values - jnp.mean(values, axis=-1, keepdims=True)
+    scale = lax.rsqrt(jnp.mean(centred * centred, axis=-1, keepdims=True) + norm_eps)
+    return centred * scale, scale
+
+
+def norm_back(unit, scale, gain, grad):
+    e = grad * gain
+    return scale * (
+        e
+        - jnp.mean(e, axis=-1, keepdims=True)
+        - unit * jnp.mean(e * unit, axis=-1, keepdims=True)
+    )
+
+
+def column_sum(values):
+    return jnp.sum(values, axis=0, keepdims=True)
+
+
+def split_heads(pair):
+    low = lax.broadcasted_iota(jnp.int32, pair.shape, 1) < HD
+    zero = jnp.zeros_like(pair)
+    return jnp.concatenate([jnp.where(low, pair, zero), jnp.where(low, zero, pair)], axis=0)
+
+
+def join_heads(stacked):
+    rows = stacked.shape[0] // 2
+    low = lax.broadcasted_iota(jnp.int32, (rows, 2 * HD), 1) < HD
+    return jnp.where(low, stacked[:rows], stacked[rows:])
+
+
+def soft_rows(scores, allowed):
+    scores = jnp.where(allowed, scores * HD ** (-0.5), masked_score)
+    top = jnp.max(scores, axis=-1, keepdims=True)
+    p = jnp.exp(scores - top)
+    return p / jnp.sum(p, axis=-1, keepdims=True)
+
+
+def self_mask(lens):
+    shape = (2 * SUF, SUF)
+    query = lax.broadcasted_iota(jnp.int32, shape, 0) % SUF
+    key = lax.broadcasted_iota(jnp.int32, shape, 1)
+    return (key <= query) & (key < lens[0:1, 0:SUF])
+
+
+def cross_mask(lens):
+    key = lax.broadcasted_iota(jnp.int32, (2 * SUF, MEMLEN), 1)
+    seen = jnp.concatenate([lens[0:1]] * (MEMLEN // 128), axis=1)
+    return key < PATCH + seen
+
+
+PAIRS = H // 2
+
+
+def gelu_parts(u):
+    rate = (2.0 / jnp.pi) ** 0.5
+    square = u * u
+    t = jnp.tanh(rate * (u + 0.044715 * u * square))
+    half = 0.5 * (1.0 + t)
+    slope = half + 0.5 * u * (1.0 - t * t) * (rate * (1.0 + 3 * 0.044715 * square))
+    return u * half, slope
+
+
+def head_rows(ex, key_rows):
+    rows = pl.ds(pl.multiple_of(ex * SUF, SUF), SUF)
+    return rows, pl.ds(pl.multiple_of(ex * key_rows, key_rows), key_rows)
+
+
+def attend(mask_of, lens, q_ref, k_ref, v_ref, o_ref, key_rows):
+    def body(ex, _):
+        allowed = mask_of(lens[ex])
+        rows, keys = head_rows(ex, key_rows)
+        for pair in range(PAIRS):
+            lanes = pl.ds(pair * 2 * HD, 2 * HD)
+            p = soft_rows(dot_nt(split_heads(q_ref[rows, lanes]), k_ref[keys, lanes]), allowed)
+            o_ref[rows, lanes] = join_heads(dot_nn(p.astype(BF), v_ref[keys, lanes])).astype(BF)
+        return 0
+
+    lax.fori_loop(0, EX_DEV, body, 0)
+
+
+def attend_back(first, count, mask_of, lens, q_ref, k_ref, v_ref, do_ref, key_rows):
+    scale = HD ** (-0.5)
+
+    def body(ex, _):
+        allowed = mask_of(lens[ex])
+        rows, keys = head_rows(ex, key_rows)
+        for pair in range(PAIRS):
+            lanes = pl.ds(pair * 2 * HD, 2 * HD)
+            q, k, v = split_heads(q_ref[rows, lanes]), k_ref[keys, lanes], v_ref[keys, lanes]
+            p = soft_rows(dot_nt(q, k), allowed)
+            d_out = split_heads(do_ref[rows, lanes])
+            v_ref[keys, lanes] = dot_tn(p.astype(BF), d_out).astype(BF)
+            dp = dot_nt(d_out, v)
+            ds = (p * (dp - jnp.sum(p * dp, axis=-1, keepdims=True))).astype(BF)
+            q_ref[rows, lanes] = (join_heads(dot_nn(ds, k)) * scale).astype(BF)
+            k_ref[keys, lanes] = (dot_tn(ds, q) * scale).astype(BF)
+        return 0
+
+    lax.fori_loop(first, first + count, body, 0)
+
+
+def seed_of(cot_ref, lens, ex):
+    line = lax.broadcasted_iota(jnp.int32, (SUF, D), 0)
+    length = jnp.concatenate([lens[ex, 0:1]] * (D // LANES), axis=1)
+    return cot_ref[pl.ds(ex * SUF, SUF)].astype(F32) * (line < length).astype(F32)
+
+
+class Local:
+    def __init__(self, sems):
+        self.sems, self.used, self.open = sems, 0, []
+
+    def start(self, src, dst):
+        cp = pltpu.make_async_copy(src, dst, self.sems.at[self.used])
+        self.used += 1
+        cp.start()
+        return cp
+
+    def out(self, src, dst):
+        self.open.append(self.start(src, dst))
+
+    def drain(self):
+        for cp in self.open:
+            cp.wait()
+
+
+def forward_kernel(
+    self_w, cross_w, feed_w, mem_in, x_ref, cot_ref, vec_ref, slen_ref, plen_ref,
+    attn_h, feed_h, mem_h, q1_h, k1_h, v1_h, o1_h, q2_h, o2_h, a3_h, k2_h, v2_h, z_h, slope_h,
+    h1_h, h2_h, dn_g,
+    self_in, cross_in, feed_in, self_v, cross_v, feed_v, mem_v, a1, q1, k1, v1, o1, a2, q2, o2, a3,
+    e3, k2, v2, z_v, slope_v, h1, h2, ring, send, recv, local,
+):
+    dp, fs, z, y, x, c = place()
+    ex, ndp = mem_v.shape[0], mem_v.shape[1]
+    to_y, to_x, to_c = peer_id(z, 1 - y, x, c), peer_id(z, y, 1 - x, c), peer_id(z, y, x, 1 - c)
+    per = D // LANES
+    cp, loc = Copies(send, recv, None), Local(local)
+    rows_of(self_w, self_in, 0, 0, per)
+    greet([((dp + k) % ndp, fs) for k in range(1, ndp)] + [to_x, to_c])
+
+    step = feed_in.shape[1]
+    cut = step * 2 // 3
+    chunks = []
+    for src, dst in ((self_in, self_v), (cross_in, cross_v), (feed_in, feed_v)):
+        for j in range(src.shape[0]):
+            for first in range(0, src.shape[1], step):
+                chunks.append(
+                    (src, dst, j, pl.ds(first, step), pl.ds(first, cut), pl.ds(first + cut, step - cut))
+                )
+    zc, s2, s3, s4, mem, own = {}, {}, {}, {}, [], {}
+
+    def send_z(t):
+        src, dst, j, rows, r0, r1 = chunks[t]
+        own[t] = loc.start(src.at[j, rows], dst.at[z, y, x, c, j, rows])
+        for k in range(1, NZ):
+            zc[t, k] = cp.remote(
+                src.at[j, rows], dst.at[z, y, x, c, j, rows], peer_id((z + k) % NZ, y, x, c)
+            )
+        send_2(t, 0)
+
+    def send_2(t, k):
+        src, dst, j, rows, r0, r1 = chunks[t]
+        zz = (z + NZ - k) % NZ
+        for part, cut_rows, where in ((0, r0, to_y), (1, r1, to_x)):
+            here = src.at[j, cut_rows] if k == 0 else dst.at[zz, y, x, c, j, cut_rows]
+            s2[t, k, part] = cp.remote(here, dst.at[zz, y, x, c, j, cut_rows], where)
+
+    def send_3(t):
+        src, dst, j, rows, r0, r1 = chunks[t]
+        s3[t, 0] = cp.remote(dst.at[:, :, x, c, j, r0], dst.at[:, :, x, c, j, r0], to_x)
+        s3[t, 1] = cp.remote(dst.at[:, y, :, c, j, r1], dst.at[:, y, :, c, j, r1], to_y)
+
+    def send_4(t):
+        src, dst, j, rows, r0, r1 = chunks[t]
+        s4[t] = cp.remote(dst.at[:, :, :, c, j, rows], dst.at[:, :, :, c, j, rows], to_c)
+
+    def send_mem():
+        mem.append(loc.start(mem_in.at[pl.ds(ex * dp, ex)], mem_v.at[:, dp]))
+        for k in range(1, ndp):
+            mem.append(
+                cp.remote(
+                    mem_in.at[pl.ds(ex * ((dp + k) % ndp), ex)],
+                    mem_v.at[:, dp],
+                    ((dp + k) % ndp, fs),
+                )
+            )
+
+    row = lambda i: vec_ref[i : i + 1, :]
+    g1, b1, g2, b2, g3, b3 = [row(i) for i in range(6)]
+    square = lambda a: a.reshape(D, D)
+    self_mat = lambda m: square(self_v[m])
+    cross_mat = lambda m: square(cross_v[m])
+    mem_rows = lambda: mem_v[...].reshape(ex * MEMLEN, D)
+
+    def begin():
+        unit, _ = norm_parts(x_ref[...].astype(F32))
+        a1[...] = (unit * g1 + b1).astype(BF)
+        for i in range(EX_DEV):
+            e3[pl.ds(i * SUF, SUF)] = seed_of(cot_ref, slen_ref, i).astype(BF)
+
+    def self_qkv():
+        s4[0].wait_recv()
+        s4[1].wait_recv()
+        loc.out(self_v.at[:, :, :, :, 0], attn_h.at[pl.ds(0, 4)])
+        for i, (ref, dst) in enumerate(((q1, q1_h), (k1, k1_h), (v1, v1_h))):
+            ref[...] = dot_nn(a1[...], self_mat(i)).astype(BF)
+            loc.out(ref, dst)
+
+    def self_attention():
+        attend(self_mask, slen_ref, q1, k1, v1, o1, SUF)
+        loc.out(o1, o1_h)
+        h1[...] = x_ref[...].astype(F32) + dot_nn(o1[...], self_mat(3))
+        loc.out(h1, h1_h)
+        unit, _ = norm_parts(h1[...])
+        a2[...] = (unit * g2 + b2).astype(BF)
+
+    def cross_query():
+        s4[2].wait_recv()
+        s4[3].wait_recv()
+        loc.out(cross_v.at[:, :, :, :, 0], attn_h.at[pl.ds(4, 4)])
+        q2[...] = dot_nn(a2[...], cross_mat(0)).astype(BF)
+        loc.out(q2, q2_h)
+
+    def cross_keys():
+        mem[0].wait()
+        for one in mem[1:]:
+            one.wait_recv()
+        loc.out(mem_v, mem_h)
+        for i, ref, dst in ((1, k2, k2_h), (2, v2, v2_h)):
+            ref[...] = dot_nn(mem_rows(), cross_mat(i)).astype(BF)
+            loc.out(ref, dst)
+
+    def cross_attention():
+        attend(cross_mask, plen_ref, q2, k2, v2, o2, MEMLEN)
+        loc.out(o2, o2_h)
+
+    def cross_out():
+        h2[...] = h1[...] + dot_nn(o2[...], cross_mat(3))
+        loc.out(h2, h2_h)
+        unit, _ = norm_parts(h2[...])
+        a3[...] = (unit * g3 + b3).astype(BF)
+        loc.out(a3, a3_h)
+
+    def feed(j):
+        s4[4 + j].wait_recv()
+        u = dot_nn(a3[...], square(feed_v[0:2, :, :, :, j])) + row(7 + j)
+        act, bend = gelu_parts(u)
+        z_v[j] = act.astype(BF)
+        slope_v[j] = bend
+        loc.out(z_v.at[j], z_h.at[j])
+        loc.out(slope_v.at[j], slope_h.at[j])
+        ring[j] = dot_tn(z_v[j], e3[...]).astype(BF).reshape(ring.shape[1:])
+        loc.out(ring.at[j], dn_g.at[j // 2, j % 2])
+        if j == 3:
+            loc.out(feed_v, feed_h)
+
+    slots = {
+        0: [begin],
+        4: [self_qkv],
+        5: [self_attention],
+        6: [cross_query],
+        7: [cross_keys],
+        8: [cross_attention],
+        9: [cross_out, lambda: feed(0), lambda: feed(1), lambda: feed(2), lambda: feed(3)],
+    }
+    n = len(chunks)
+    send_z(0)
+    send_z(1)
+    rows_of(cross_w, cross_in, 0, 0, per)
+    send_z(2)
+    send_z(3)
+    for up in (True, False):
+
+        @pl.when(z // 2 == (0 if up else 1))
+        def _():
+            for j in range(4):
+                rows_of(feed_w, feed_in, j, *feed_lines(j, *feed_in.shape[1:], up))
+
+    for t in range(4, min(AHEAD, n)):
+        send_z(t)
+    for t in range(n + 2):
+        if t == MEM_AT:
+            send_mem()
+        if t < n:
+            for k in range(1, NZ):
+                zc[t, k].wait_recv()
+                send_2(t, k)
+            if t + AHEAD < n:
+                send_z(t + AHEAD)
+        if 1 <= t <= n:
+            own[t - 1].wait()
+            for k in range(NZ):
+                for part in (0, 1):
+                    s2[t - 1, k, part].wait_recv()
+            send_3(t - 1)
+        if t >= 2:
+            s3[t - 2, 0].wait_recv()
+            s3[t - 2, 1].wait_recv()
+            send_4(t - 2)
+        for piece in slots.get(t, ()):
+            piece()
+    loc.drain()
+    cp.drain()
+
+
+def forward_all(weights, mem_in, x, cot, vec, slen, plen, rows_a, rows_f, ndp):
+    anywhere = pl.BlockSpec(memory_space=pl.ANY)
+    vmem = pl.BlockSpec(memory_space=pltpu.VMEM)
+    rows = x.shape[0]
+    ex = mem_in.shape[0] // ndp
+    count = ex * MEMLEN
+    split = (2, 2, 2)
+    arrays = {
+        "attn": ((8,) + split + (rows_a, D), BF),
+        "feed": ((NZ,) + split + (4, rows_f, D), BF),
+        "mem": ((ex, ndp) + mem_in.shape[1:], BF),
+        "low": ((rows, D), BF),
+        "keys": ((count, D), BF),
+        "z": ((4, rows, D), BF),
+        "slope": ((4, rows, D), F32),
+        "wide": ((rows, D), F32),
+        "dn": ((2,) + split + (4, rows_f, D), BF),
+    }
+    kinds = ["attn", "feed", "mem"] + ["low"] * 7 + ["keys"] * 2 + ["z", "slope", "wide", "wide", "dn"]
+    low = pltpu.VMEM((rows, D), BF)
+    return pl.pallas_call(
+        forward_kernel,
+        out_shape=[jax.ShapeDtypeStruct(*arrays[k]) for k in kinds],
+        in_specs=[vmem] * 3 + [anywhere] + [vmem] * 5,
+        out_specs=[anywhere] * len(kinds),
+        scratch_shapes=[
+            pltpu.VMEM((1, rows_a, D), BF),
+            pltpu.VMEM((1, rows_a, D), BF),
+            pltpu.VMEM((4, rows_f, D), BF),
+            pltpu.VMEM((NZ,) + split + (1, rows_a, D), BF),
+            pltpu.VMEM((NZ,) + split + (1, rows_a, D), BF),
+            pltpu.VMEM(*arrays["feed"]),
+            pltpu.VMEM(*arrays["mem"]),
+            *[low] * 10,
+            pltpu.VMEM(*arrays["keys"]),
+            pltpu.VMEM(*arrays["keys"]),
+            pltpu.VMEM(*arrays["z"]),
+            pltpu.VMEM(*arrays["slope"]),
+            pltpu.VMEM(*arrays["wide"]),
+            pltpu.VMEM(*arrays["wide"]),
+            pltpu.VMEM((4, 2, 2, 4, rows_f, D), BF),
+            pltpu.SemaphoreType.DMA((128,)),
+            pltpu.SemaphoreType.DMA((128,)),
+            pltpu.SemaphoreType.DMA((48,)),
+        ],
+        compiler_params=pltpu.CompilerParams(
+            collective_id=1, has_side_effects=True, vmem_limit_bytes=60 << 20
+        ),
+        name="forward_all",
+    )(*weights, mem_in, x, cot, vec, slen, plen)
+
+
+def backward_kernel(
+    attn_h, dn_h, up_h, mem_h, q1_h, k1_h, v1_h, o1_h, q2_h, o2_h, a3_h, k2_h, v2_h, z_h, slope_h,
+    h1_h, h2_h, dn_g, x_ref, cot_ref, vec_ref, slen_ref, plen_ref,
+    ws, wc, wf, ms, mc, mf, ss, sc_, sf,
+    out_ref, sg_ref, self_t, cross_t, feed_t, mem_t, vec_t, sq_t, norm_t, attn_g, up_g,
+    wr, ur, mem_v, q1, k1, v1, o1, q2, o2, a1, a2, a3, k2, v2, z_v, slope_v, h1, h2, e3, du, db,
+    ring_a, ring_u, held, r1, r2a, r2b, r3a, r3b, rz, whole, vecg, v_send, v_recv, v_z,
+    qa, qb, na, nb, opt_s, opt_c, opt_f, send, recv, local,
+):
+    dp, fs, z, y, x, c = place()
+    ex_count, ndp = mem_v.shape[0], mem_v.shape[1]
+    nfs = qa.shape[0]
+    step, width = r1.shape[4], r1.shape[5]
+    cut = step * 2 // 3
+    head, rest = pl.ds(0, cut), pl.ds(cut, step - cut)
+    per = width // LANES
+    to_y, to_x, to_c = peer_id(z, 1 - y, x, c), peer_id(z, y, 1 - x, c), peer_id(z, y, x, 1 - c)
+    cp, loc = Copies(send, recv, None), Local(local)
+
+    fetch_order = [dn_h.at[4 + j] for j in range(4)] + [
+        attn_h.at[m] for m in (7, 5, 6, 4, 3, 0, 1, 2)
+    ]
+    depth = wr.shape[0]
+    fetched, used = [], [0]
+    up_got = []
+
+    def fetch():
+        if len(fetched) < len(fetch_order):
+            i = len(fetched)
+            fetched.append(loc.start(fetch_order[i], wr.at[i % depth]))
+
+    def weight():
+        i = used[0]
+        used[0] += 1
+        fetched[i].wait()
+        return wr[i % depth]
+
+    def fetch_up():
+        i = len(up_got)
+        if i < 4:
+            up_got.append(loc.start(up_h.at[pl.ds(0, ur.shape[1]), i], ur.at[i % ur.shape[0]]))
+
+    fetch()
+    a3_ok = loc.start(a3_h, a3)
+    slope_ok = [loc.start(slope_h.at[0], slope_v.at[0])]
+    for j in range(1, 4):
+        fetch()
+        slope_ok.append(loc.start(slope_h.at[j], slope_v.at[j]))
+    for _ in range(ur.shape[0]):
+        fetch_up()
+    z_ok = loc.start(z_h, z_v)
+    h2_ok = loc.start(h2_h, h2)
+    cross_ok = [
+        loc.start(a, b)
+        for a, b in ((o2_h, o2), (q2_h, q2), (k2_h, k2), (v2_h, v2), (mem_h, mem_v), (h1_h, h1))
+    ]
+    self_ok = [loc.start(a, b) for a, b in ((o1_h, o1), (q1_h, q1), (k1_h, k1), (v1_h, v1))]
+    groups = (
+        ((ws, ms, ss), opt_s, self_t, z),
+        ((wc, mc, sc_), opt_c, cross_t, NZ + z),
+        ((wf, mf, sf), opt_f, feed_t, 2 * NZ + z // 2),
+    )
+    opt = [
+        loc.start(src, dst.at[i]) for srcs, dst, _, _ in groups for i, src in enumerate(srcs)
+    ]
+    greet(
+        [((dp + k) % ndp, fs) for k in range(1, ndp)] + [(dp, (fs + k) % nfs) for k in range(1, nfs)]
+    )
+
+    def attn_src(base, r):
+        rows = pl.ds(r * step, step)
+        return lambda zz, cc: attn_g.at[base + zz, :, :, cc, rows]
+
+    def feed_src(j):
+        return lambda zz, cc: up_g.at[j, zz, :, :, cc] if zz < 2 else dn_g.at[zz - 2, :, :, cc, j]
+
+    sources = [feed_src(j) for j in range(4)] + [attn_src(b, r) for b in (4, 0) for r in range(2)]
+    n = len(sources)
+    sc, sl, s1, s2, sz = {}, {}, {}, {}, {}
+
+    def phase_0(t):
+        for zz in range(NZ):
+            sc[t, zz] = cp.remote(sources[t](zz, 1 - c), r1.at[t, zz], to_c)
+            sl[t, zz] = loc.start(sources[t](zz, c), held.at[t % held.shape[0], zz])
+
+    def add_c(t, fixed_y, fixed_x, rows):
+        slot = t % held.shape[0]
+
+        def body(i, _):
+            zz, o = i // 2, i % 2
+            yy = o if fixed_y is None else fixed_y
+            xx = o if fixed_x is None else fixed_x
+            r1[t, zz, yy, xx, rows] = r1[t, zz, yy, xx, rows] + held[slot, zz, yy, xx, rows]
+            return 0
+
+        lax.fori_loop(0, NZ * 2, body, 0)
+
+    def phase_c(t):
+        for zz in range(NZ):
+            sc[t, zz].wait_recv()
+            sl[t, zz].wait()
+        add_c(t, None, 1 - x, head)
+        s1[t, 0] = cp.remote(r1.at[t, :, :, 1 - x, head], r2a.at[t], to_x)
+        add_c(t, 1 - y, None, rest)
+        s1[t, 1] = cp.remote(r1.at[t, :, 1 - y, :, rest], r2b.at[t], to_y)
+        add_c(t, None, x, head)
+        add_c(t, y, None, rest)
+
+    def add_1(t, yy, xx, rows, got, where):
+        def body(zz, _):
+            r1[t, zz, yy, xx, rows] = r1[t, zz, yy, xx, rows] + got[t, zz, where]
+            return 0
+
+        lax.fori_loop(0, NZ, body, 0)
+
+    def phase_1(t):
+        s1[t, 0].wait_recv()
+        add_1(t, 1 - y, x, head, r2a, 1 - y)
+        s2[t, 0] = cp.remote(r1.at[t, :, 1 - y, x, head], r3a.at[t], to_y)
+        s1[t, 1].wait_recv()
+        add_1(t, y, 1 - x, rest, r2b, 1 - x)
+        s2[t, 1] = cp.remote(r1.at[t, :, y, 1 - x, rest], r3b.at[t], to_x)
+        add_1(t, y, x, head, r2a, y)
+        add_1(t, y, x, rest, r2b, x)
+
+    def phase_2(t):
+        s2[t, 0].wait_recv()
+        s2[t, 1].wait_recv()
+
+        def body(zz, _):
+            r1[t, zz, y, x, head] = r1[t, zz, y, x, head] + r3a[t, zz]
+            r1[t, zz, y, x, rest] = r1[t, zz, y, x, rest] + r3b[t, zz]
+            return 0
+
+        lax.fori_loop(0, NZ, body, 0)
+        for k in range(1, NZ):
+            zt = (z + k) % NZ
+            sz[t, k] = cp.remote(r1.at[t, zt, y, x], rz.at[t, k - 1], peer_id(zt, y, x, c))
+
+    def lines_of(dst, start, stride):
+        for i in range(per):
+            dst[pl.ds(start + i, step, stride=stride), :] = whole[:, i * LANES : (i + 1) * LANES]
+
+    def phase_z(t):
+        for k in range(1, NZ):
+            sz[t, k].wait_recv()
+        total = r1[t, z, y, x].astype(F32)
+        for k in range(1, NZ):
+            total = total + rz[t, k - 1].astype(F32)
+        whole[...] = total
+        if t >= 4:
+            lines_of((cross_t, self_t)[t // 2 - 2], (t % 2) * step * per, per)
+            return
+        for up in (True, False):
+
+            @pl.when(z // 2 == (0 if up else 1))
+            def _():
+                lines_of(feed_t, *feed_lines(t, step, width, up))
+
+    row = lambda i: vec_ref[i : i + 1, :]
+    gains = [row(2 * i) for i in range(3)]
+    shifts = [row(2 * i + 1) for i in range(3)]
+    mem_rows = lambda: mem_v[...].reshape(ex_count * MEMLEN, D)
+    up_mat = lambda j: ur[j % ur.shape[0]].reshape(D, D)
+    stores, order_a, waited = {}, [], set()
+
+    def stored(*which):
+        for m in which:
+            if m not in waited:
+                stores[m].wait()
+                waited.add(m)
+
+    def give(m, value):
+        slots, i = ring_a.shape[0], len(order_a)
+        if i >= slots:
+            stored(order_a[i - slots])
+        ring_a[i % slots] = value.astype(BF).reshape(ring_a.shape[1:])
+        order_a.append(m)
+        stores[m] = loc.start(ring_a.at[i % slots], attn_g.at[m])
+
+    def begin():
+        for i in range(EX_DEV):
+            rows = pl.ds(i * SUF, SUF)
+            seed = seed_of(cot_ref, slen_ref, i)
+            sg_ref[rows] = seed
+            e3[rows] = seed.astype(BF)
+        vecg[...] = jnp.zeros_like(vecg)
+        vecg[6:7] = column_sum(e3[...].astype(F32))
+
+    def feed(j):
+        dn = weight()
+        if j == 0:
+            a3_ok.wait()
+        slope_ok[j].wait()
+        du[j] = (dot_nt(e3[...], dn) * slope_v[j]).astype(BF)
+        slot = j % ring_u.shape[0]
+        if j >= ring_u.shape[0]:
+            stored(8 + j - ring_u.shape[0])
+        ring_u[slot] = dot_tn(a3[...], du[j]).astype(BF).reshape(ring_u.shape[1:])
+        stores[8 + j] = loc.start(ring_u.at[slot], up_g.at[j])
+        vecg[7 + j : 8 + j] = column_sum(du[j].astype(F32))
+        if j == 0:
+            z_ok.wait()
+            h2_ok.wait()
+            out_ref[...] = h2[...] + row(6)
+        out_ref[...] += dot_nn(z_v[j], dn)
+        fetch()
+
+    def feed_down():
+        unit, scale = norm_parts(h2[...])
+        for j in range(4):
+            up_got[j].wait()
+            part = dot_nt(du[j], up_mat(j))
+            if j == 0:
+                h2[...] = part
+            else:
+                h2[...] += part
+            fetch_up()
+        grad = h2[...]
+        vecg[4:5] = column_sum(grad * unit)
+        vecg[5:6] = column_sum(grad)
+        sg_ref[...] += norm_back(unit, scale, gains[2], grad)
+        db[...] = sg_ref[...].astype(BF)
+
+    def cross_begin():
+        cross_ok[0].wait()
+        give(7, dot_tn(o2[...], db[...]))
+        e3[...] = dot_nt(db[...], weight()).astype(BF)
+        fetch()
+        for one in cross_ok[1:4]:
+            one.wait()
+
+    def cross_part(first, count):
+        attend_back(first, count, cross_mask, plen_ref, q2, k2, v2, e3, MEMLEN)
+
+    def cross_query():
+        cross_ok[5].wait()
+        unit, _ = norm_parts(h1[...])
+        a2[...] = (unit * gains[1] + shifts[1]).astype(BF)
+        give(4, dot_tn(a2[...], q2[...]))
+
+    def cross_key():
+        cross_ok[4].wait()
+        give(5, dot_tn(mem_rows(), k2[...]))
+
+    def cross_value():
+        give(6, dot_tn(mem_rows(), v2[...]))
+
+    mem_sent = []
+
+    def cross_memory():
+        key_mat, value_mat = weight(), weight()
+        for i in range(ex_count):
+            keys = pl.ds(i * MEMLEN, MEMLEN)
+            part = dot_nt(k2[keys], key_mat) + dot_nt(v2[keys], value_mat)
+            mem_v[i] = part.astype(BF).reshape(mem_v.shape[1:])
+        fetch()
+        fetch()
+        mem_sent.append(loc.start(mem_v.at[:, dp], mem_t.at[pl.ds(ex_count * dp, ex_count)]))
+        for k in range(1, ndp):
+            mem_sent.append(
+                cp.remote(
+                    mem_v.at[:, (dp + k) % ndp],
+                    mem_t.at[pl.ds(ex_count * dp, ex_count)],
+                    ((dp + k) % ndp, fs),
+                )
+            )
+
+    def cross_end():
+        grad = dot_nt(q2[...], weight())
+        fetch()
+        unit, scale = norm_parts(h1[...])
+        vecg[2:3] = column_sum(grad * unit)
+        vecg[3:4] = column_sum(grad)
+        sg_ref[...] += norm_back(unit, scale, gains[1], grad)
+        db[...] = sg_ref[...].astype(BF)
+
+    def self_begin():
+        for one in self_ok:
+            one.wait()
+        give(3, dot_tn(o1[...], db[...]))
+        e3[...] = dot_nt(db[...], weight()).astype(BF)
+        fetch()
+        unit, _ = norm_parts(x_ref[...].astype(F32))
+        a1[...] = (unit * gains[0] + shifts[0]).astype(BF)
+
+    def self_part():
+        attend_back(0, EX_DEV, self_mask, slen_ref, q1, k1, v1, e3, SUF)
+
+    def self_weights():
+        for i, ref in enumerate((q1, k1, v1)):
+            give(i, dot_tn(a1[...], ref[...]))
+
+    def self_end():
+        grad = dot_nt(q1[...], weight())
+        grad = grad + dot_nt(k1[...], weight())
+        grad = grad + dot_nt(v1[...], weight())
+        unit, scale = norm_parts(x_ref[...].astype(F32))
+        vecg[0:1] = column_sum(grad * unit)
+        vecg[1:2] = column_sum(grad)
+        sg_ref[...] += norm_back(unit, scale, gains[0], grad)
+
+    vec_cp = []
+
+    def vec_step(i):
+        if i == 0:
+            vec_cp.append(cp.remote(vecg, v_recv.at[0], to_c))
+            return
+        vec_cp[-1].wait_recv()
+        i -= 1
+        v_send[i] = (vecg[...] if i == 0 else v_send[i - 1]) + v_recv[i]
+        if i < 2:
+            vec_cp.append(cp.remote(v_send.at[i], v_recv.at[i + 1], (to_x, to_y)[i]))
+        else:
+            v_z[z] = v_send[2]
+            for k in range(1, NZ):
+                vec_cp.append(cp.remote(v_send.at[2], v_z.at[z], peer_id((z + k) % NZ, y, x, c)))
+
+    begin()
+    feed(0)
+    feed(1)
+    stored(8)
+    phase_0(0)
+    feed(2)
+    stored(9)
+    phase_0(1)
+    phase_c(0)
+    feed(3)
+    stored(10)
+    phase_0(2)
+    phase_c(1)
+    stored(11)
+    phase_0(3)
+    feed_down()
+    phase_c(2)
+    cross_begin()
+    phase_c(3)
+    cross_part(0, 2)
+    phase_1(0)
+    cross_part(2, 2)
+    cross_query()
+    phase_2(0)
+    phase_1(1)
+    cross_key()
+    cross_value()
+    stored(4, 5, 6, 7)
+    phase_0(4)
+    phase_0(5)
+    cross_memory()
+    phase_2(1)
+    phase_c(4)
+    phase_1(2)
+    phase_z(0)
+    cross_end()
+    self_begin()
+    phase_c(5)
+    self_part()
+    self_weights()
+    stored(0, 1, 2, 3)
+    phase_0(6)
+    phase_0(7)
+    phase_2(2)
+    phase_1(3)
+    self_end()
+    vec_step(0)
+    phase_z(1)
+    phase_c(6)
+    phase_c(7)
+    vec_step(1)
+    phase_2(3)
+    phase_1(4)
+    phase_z(2)
+    vec_step(2)
+    phase_1(5)
+    phase_2(4)
+    phase_z(3)
+    vec_step(3)
+    phase_1(6)
+    phase_2(5)
+    phase_z(4)
+    phase_1(7)
+    phase_2(6)
+    phase_z(5)
+    phase_2(7)
+    phase_z(6)
+    for one in vec_cp[3:]:
+        one.wait_recv()
+    whole[0:16] = (v_z[0] + v_z[1]) + (v_z[2] + v_z[3])
+    vec_t[...] = jnp.zeros_like(vec_t)
+    for i in range(per):
+        vec_t[pl.ds(i, 11, stride=per), :] = whole[0:11, i * LANES : (i + 1) * LANES]
+    phase_z(7)
+    sq = squares(self_t[...]) + squares(cross_t[...]) + squares(feed_t[...])
+    sq = sum_everywhere(cp, sq, qa, qb, dp, fs) + squares(vec_t[...])
+    sq_t[...] = sq
+    factor = clip_of(sq)
+    rows = lax.broadcasted_iota(jnp.int32, (32, LANES), 0)
+    tile = jnp.zeros((32, LANES), F32)
+    for one in opt:
+        one.wait()
+    for _, dst, g, line in groups:
+        w = dst[0]
+        ratio = lamb_step(w, g[...], dst[1], dst[2], factor)[2]
+        for first, a in ((0, ratio), (16, w)):
+            part = jnp.sum(a * a, axis=0, keepdims=True)
+            tile = tile + jnp.where(rows == first + line, part, 0.0)
+    norm_t[...] = sum_everywhere(cp, tile, na, nb, dp, fs)
+    mem_sent[0].wait()
+    for one in mem_sent[1:]:
+        one.wait_recv()
+    cp.drain()
+
+
+def backward_all(kept, x, cot, vec, slen, plen, states, rows_a, rows_f, ndp, nfs):
+    anywhere = pl.BlockSpec(memory_space=pl.ANY)
+    vmem = pl.BlockSpec(memory_space=pltpu.VMEM)
+    mem = kept[3]
+    ex, _, pos, width = mem.shape
+    rows = x.shape[0]
+    lines = [w.shape[0] for w in states[:3]]
+    step = rows_f
+    cut = step * 2 // 3
+    split = (2, 2, 2)
+    low = lambda *dims: pltpu.VMEM(dims + (width,), BF)
+    wide = lambda *dims: pltpu.VMEM(dims, F32)
+    shape = lambda *dims: jax.ShapeDtypeStruct(dims, F32)
+    vec_rows = 16
+    return pl.pallas_call(
+        backward_kernel,
+        out_shape=[
+            shape(rows, width),
+            shape(rows, width),
+            *[shape(k, LANES) for k in lines],
+            jax.ShapeDtypeStruct((ndp * ex, pos, width), BF),
+            shape(vec_rows * width // LANES, LANES),
+            shape(8, LANES),
+            shape(32, LANES),
+            jax.ShapeDtypeStruct((8,) + split + (rows_a, width), BF),
+            jax.ShapeDtypeStruct((4, 2) + split + (rows_f, width), BF),
+        ],
+        in_specs=[anywhere] * 18 + [vmem] * 5 + [anywhere] * 9,
+        out_specs=[vmem] * 5 + [anywhere] + [vmem] * 3 + [anywhere] * 2,
+        scratch_shapes=[
+            low(4, width),
+            low(2, up_rows(kept[2]), rows_f),
+            low(ex, ndp, pos),
+            *[low(rows)] * 9,
+            low(ex * MEMLEN),
+            low(ex * MEMLEN),
+            low(4, rows),
+            wide(4, rows, width),
+            wide(rows, width),
+            wide(rows, width),
+            low(rows),
+            low(4, rows),
+            low(rows),
+            low(2, *split, rows_a),
+            low(2, 2, *split, rows_f),
+            low(2, NZ, 2, 2, step),
+            low(8, NZ, 2, 2, step),
+            low(8, NZ, 2, cut),
+            low(8, NZ, 2, step - cut),
+            low(8, NZ, cut),
+            low(8, NZ, step - cut),
+            low(8, NZ - 1, step),
+            wide(step, width),
+            wide(vec_rows, width),
+            wide(3, vec_rows, width),
+            wide(3, vec_rows, width),
+            wide(NZ, vec_rows, width),
+            wide(nfs, 8, LANES),
+            wide(ndp, 8, LANES),
+            wide(nfs, 32, LANES),
+            wide(ndp, 32, LANES),
+            *[wide(3, k, LANES) for k in lines],
+            pltpu.SemaphoreType.DMA((128,)),
+            pltpu.SemaphoreType.DMA((128,)),
+            pltpu.SemaphoreType.DMA((96,)),
+        ],
+        compiler_params=pltpu.CompilerParams(
+            collective_id=2, has_side_effects=True, vmem_limit_bytes=60 << 20
+        ),
+        name="backward_all",
+    )(*kept, x, cot, vec, slen, plen, *states)
+
+
+def up_rows(view):
+    return view.shape[0] // 2
+
+
+def update_kernel(*refs):
+    ins, outs = refs[:18], refs[18:]
+    gs, ws, ms, vs, (gv, sq, norms) = ins[0:3], ins[3:7], ins[7:11], ins[11:15], ins[15:18]
+    z = lax.axis_index("dp") // 2
+    factor = clip_of(sq[...])
+    sums = jnp.sqrt(jnp.sum(norms[...], axis=1, keepdims=True))
+    ratio_norm, weight_norm = sums[0:16], sums[16:32]
+    trust = weight_norm / (ratio_norm + trust_eps)
+    row = lax.broadcasted_iota(jnp.int32, (16, 1), 0)
+    for i, first in enumerate((z, NZ + z, 2 * NZ + z // 2)):
+        g = gs[i][...]
+        w = ws[i][...]
+        m, v, ratio = lamb_step(w, g, ms[i][...], vs[i][...], factor)
+        rate = jnp.sum(jnp.where(row == first, trust, 0.0), axis=0, keepdims=True)
+        for ref, value in zip(outs[4 * i : 4 * i + 4], (g, m, v, w - learn_rate * rate * ratio)):
+            ref[...] = value
+    w = ws[3][...]
+    g = gv[0 : w.shape[0], :]
+    m, v, ratio = lamb_step(w, g, ms[3][...], vs[3][...], factor)
+    line = lax.broadcasted_iota(jnp.int32, w.shape, 0)
+    spread = lax.broadcasted_iota(jnp.int32, (16, LANES), 1)
+    pick = spread == lax.broadcasted_iota(jnp.int32, (16, LANES), 0)
+    lanes = spread[0:1]
+    on_row = lambda a: jnp.sum(jnp.where(pick, a, 0.0), axis=0, keepdims=True)
+    weight_row, ratio_row = on_row(weight_norm), on_row(ratio_norm)
+    rate = jnp.zeros(w.shape, F32)
+    per = D // LANES
+    for i in range(8):
+        mine = (line >= i * per) & (line < ((i + 1) * per if i < 7 else w.shape[0]))
+        norm = lambda a: norm_of(jnp.where(mine, a * a, 0.0))
+        wn, rn = norm(w), norm(ratio)
+        rate = jnp.where(mine, wn / (rn + trust_eps), rate)
+        weight_row = jnp.where(lanes == 10 + i, wn, weight_row)
+        ratio_row = jnp.where(lanes == 10 + i, rn, ratio_row)
+    for ref, value in zip(outs[12:16], (g, m, v, w - learn_rate * rate * ratio)):
+        ref[...] = value
+    outs[16][0:1, :] = weight_row[:, 0:18]
+    outs[16][1:2, :] = ratio_row[:, 0:18]
+    outs[17][...] = norm_of(sq[...])
+
+
+def update_all(totals, weights, moments, seconds, vec_total, sq, norms):
+    vmem = pl.BlockSpec(memory_space=pltpu.VMEM)
+    shape = lambda a: jax.ShapeDtypeStruct(a.shape, F32)
+    outs = [shape(a) for a in weights for _ in range(4)]
+    outs += [jax.ShapeDtypeStruct((2, 18), F32), jax.ShapeDtypeStruct((1, 1), F32)]
+    return pl.pallas_call(
+        update_kernel,
+        out_shape=outs,
+        in_specs=[vmem] * 18,
+        out_specs=[vmem] * len(outs),
+        compiler_params=pltpu.CompilerParams(vmem_limit_bytes=40 << 20),
+        name="update_all",
+    )(*totals, *weights, *moments, *seconds, vec_total, sq, norms)
+
+
+def fast_shards(
+    suffix,
+    memory,
+    prefix_lengths,
+    suffix_lengths,
+    cotangent,
+    self_weights,
+    self_moment,
+    self_second,
+    cross_weights,
+    cross_moment,
+    cross_second,
+    feed_weights,
+    feed_moment,
+    feed_second,
+    vectors,
+    vector_moment,
+    vector_second,
+):
+    row_count = EX_DEV * SUF
+    ndp, nfs = lax.axis_size("dp"), lax.axis_size("fsdp")
+    owners = ndp * nfs
+    rows_a, rows_f = self_weights.shape[0] // D, feed_weights.shape[0] // (4 * D)
+    flat = lambda *group: [a.reshape(-1, LANES) for a in group]
+    weights = flat(self_weights, cross_weights, feed_weights, vectors)
+    moments = flat(self_moment, cross_moment, feed_moment, vector_moment)
+    seconds = flat(self_second, cross_second, feed_second, vector_second)
+    lens = lambda a: jnp.broadcast_to(a[0][:, None, None], (EX_DEV, 8, LANES))
+    common = (
+        suffix.reshape(row_count, D),
+        cotangent.reshape(row_count, D),
+        vectors.reshape(-1, D),
+        lens(suffix_lengths),
+        lens(prefix_lengths),
+    )
+    attn, feed, *kept = forward_all(weights[:3], memory[0], *common, rows_a, rows_f, ndp)
+    kept = [
+        attn.reshape(8, D, D),
+        feed.reshape(8, D, D),
+        feed.reshape(owners, 4, rows_f, D),
+        *kept,
+    ]
+    layer_output, suffix_gradient, *totals, memory_back, vec_sum, squared, norms, _, _ = backward_all(
+        kept, *common, weights[:3] + moments[:3] + seconds[:3], rows_a, rows_f, ndp, nfs
+    )
+    *new, tensor_norms, global_norm = update_all(
+        totals, weights, moments, seconds, vec_sum, squared, norms
+    )
+    return (
+        layer_output.reshape(1, EX_DEV, SUF, D),
+        suffix_gradient.reshape(1, EX_DEV, SUF, D),
+        memory_back.astype(F32)[None],
+        *[a.reshape(-1) for a in new],
+        tensor_norms,
+        global_norm.reshape(()),
+    )
+
+
+def pick(mesh):
+    if mesh.shape["dp"] == 8 and mesh.shape["fsdp"] == 4:
+        return fast_shards
+    return shards
+
+
 def solution(mesh):
     return jax.shard_map(
-        shards,
+        pick(mesh),
         mesh=mesh,
         in_specs=(
             P("fsdp", "dp", None, None),

time: 1280 us -> 323 us (0.25)
  waiting for transfers between devices: 718 us -> 0 us
  Pallas kernels: 0 us -> 306 us
  local copies, waits for them, and re-layouts: 235 us -> 6.71 us
  other arithmetic: 102 us -> 3.6 us
  matrix products: 85.7 us -> 0 us
  blocking collectives: 79.9 us -> 0 us
  between operations: 29 us -> 1.21 us
    unnamed x5 -> x0, waiting for transfers between devices: 573 us -> none
    pallas_call x0 -> x3, Pallas kernels: none -> 306 us  [the longest x1 175 us: backward_all(): pl.pallas_call(backward_kernel, out_shape=[shape(rows, width), shape(rows...]
    all_gather x3 -> x0, waiting for transfers between devices: 107 us -> none  [the longest x1 43.2 us: shards(): lax.all_gather(cross_weights.astype(jnp.bfloat16), ('dp', 'fsdp'), axis=0...]
    dot_general x33 -> x0, matrix products: 85.7 us -> none  [the longest x1 6.8 us: shards(): jnp.einsum('rf,rd->fd', activated, seed_low, preferred_element_type=jnp.f...]
    psum x2 -> x0, blocking collectives: 79.9 us -> none  [the longest x1 40.7 us: shards(): lax.psum((vector_partial, grad_squares, weight_squares), ('dp', 'fsdp'))]
    unnamed x265 -> x42, local copies, waits for them, and re-layouts: 55.1 us -> 2.66 us
    slice x19 -> x0, local copies, waits for them, and re-layouts: 51.9 us -> none  [the longest x2 16.5 us: shards(): up_mat = feed_full[:D * FF].reshape(D, FF)]
    concatenate x7 -> x0, local copies, waits for them, and re-layouts: 42.3 us -> none  [the longest x2 21.5 us: shards(): feed_flat = jnp.concatenate([up_grad.reshape(-1), down_grad.reshape(-1)])]
  transfers between devices with their start and end apart: 6 -> 0, of which waited for: 5 -> 0; matrix products, arithmetic and copies ran while one was open for 9% -> 0% of each run, Pallas kernels for 0% -> 0%
where the time goes in v4:
time: 323 us; the launch traced here: 318 us
  Pallas kernels  306 us (95%)
  local copies, waits for them, and re-layouts  6.71 us (2%)
  other arithmetic  3.6 us (1%)
    pallas_call x1, Pallas kernels, backward_all(): pl.pallas_call(backward_kernel, out_shape=[shape(rows, width), shape(rows...  175 us
    pallas_call x1, Pallas kernels, forward_all(): pl.pallas_call(forward_kernel, out_shape=[jax.ShapeDtypeStruct(*arrays[k]...  128 us

profile of v4, /device:TPU:0, one launch (start us, length us, event | category | flops | bytes accessed | tf_op | source)
XLA Modules:
  0.0 317.6 jit_solution(1427487888021891422)
XLA Ops:
  0.7 1.3 broadcast_in_dim.23.plen_ref
  2.0 1.3 broadcast_in_dim.21.slen_ref
  3.3 1.4 reshape.160.vec_ref
  4.7 128.4 %forward_all.1 = (bf16[8,2,2,2,96,768]{5,4,3,2,1,0:T(8,128)(2,1)}, bf16[4,2,2,2,4,48,768]{6,5,4,3,2,1,0:T(8,128)(2,1)}, bf16[4,8,32,768]{3,2,1,0:T(8,128)(2,1)},...) custom-call(f32[576,128]{1,0:T(8,128)} %bitcast.45, ...), custom_call_target="tpu_custom_call" | custom-call | tf_op jit(solution)/shard_map/forward_all/pallas_call | solution.py:863
  133.1 0.0 copy-start.12
  133.2 0.0 copy-start.14
  133.2 0.0 copy-start.15
  133.2 174.8 %backward_all.1 = (f32[256,768]{1,0:T(8,128)}, f32[256,768]{1,0:T(8,128)}, f32[576,128]{1,0:T(8,128)}, f32[576,128]{1,0:T(8,128)}, f32[1152,128]{1,0:T(8,128)}, ...) custom-call(bf16[8,768,768]{2,1,0:T(8,128)(2,1)} %bitcast.68, ...), custom_call_target="tpu_custom_call" | custom-call | tf_op jit(solution)/shard_map/backward_all/pallas_call | solution.py:1322
  308.0 0.0 copy-start
  308.0 0.0 copy-start.1
  308.0 0.0 copy-start.2
  308.0 0.0 copy-start.3
  308.1 0.0 copy-start.4
  308.1 0.0 copy-start.5
  308.1 0.0 copy-start.6
  308.1 0.0 copy-start.7
  308.1 0.0 copy-start.8
  308.1 0.0 copy-start.9
  308.1 0.0 copy-start.10
  308.1 0.0 copy-start.11
  308.1 0.0 copy-start.16
  308.2 0.0 copy-start.17
  308.2 3.6 %bitcast_convert_fusion = f32[1,32,32,768]{3,2,1,0:T(8,128)} fusion(bf16[32,32,768]{2,1,0:T(8,128)(2,1)} %get-tuple-element.84), kind=kLoop, calls=%fused_computation | loop fusion | flops 786432 | bytes 4718592 | tf_op jit(solution)/shard_map/broadcast_in_dim | solution.py:1492
  311.8 0.0 copy-done.12
  311.8 0.0 copy-done.14
  311.8 0.0 copy-done.15
  311.8 0.0 copy-done
  311.8 0.0 copy-done.1
  311.8 0.0 copy-done.2
  311.8 0.0 copy-done.3
  311.8 0.0 copy-done.4
  311.8 0.0 copy-done.5
  311.8 0.0 copy-done.6
  311.9 0.0 copy-done.7
  311.9 0.0 copy-done.8
  311.9 0.0 copy-done.9
  311.9 0.0 copy-done.10
  311.9 0.0 copy-done.11
  311.9 0.0 copy-done.16
  311.9 0.0 copy-done.17
  311.9 0.0 copy-start.13
  311.9 0.8 copy-done.13
  312.7 0.0 copy-start.19
  312.7 0.0 copy-start.18
  312.7 2.9 update_all.1
  315.6 0.0 copy-done.19
  315.6 0.9 copy.40
  316.5 0.0 copy-done.18
  316.5 0.9 copy.41
Async XLA Ops:
  133.1 178.6 %copy-start.12 = (f32[8448]{0:T(1024)S(1)}, f32[8448]{0:T(1024)}, u32[]{:S(2)}) copy-start(f32[8448]{0:T(1024)} %param.31) | copy-start | bytes 101380
  133.2 178.6 %copy-start.14 = (f32[8448]{0:T(1024)S(1)}, f32[8448]{0:T(1024)}, u32[]{:S(2)}) copy-start(f32[8448]{0:T(1024)} %param.32) | copy-start | bytes 101380
  133.2 178.6 %copy-start.15 = (f32[8448]{0:T(1024)S(1)}, f32[8448]{0:T(1024)}, u32[]{:S(2)}) copy-start(f32[8448]{0:T(1024)} %param.33) | copy-start | bytes 101380
  308.0 3.8 %copy-start = (f32[147456]{0:T(1024)S(1)}, f32[147456]{0:T(1024)}, u32[]{:S(2)}) copy-start(f32[147456]{0:T(1024)} %param.28) | copy-start | bytes 1769476
  308.0 3.8 %copy-start.1 = (f32[73728]{0:T(1024)S(1)}, f32[73728]{0:T(1024)}, u32[]{:S(2)}) copy-start(f32[73728]{0:T(1024)} %param.22) | copy-start | bytes 884740
  308.0 3.8 %copy-start.2 = (f32[73728]{0:T(1024)S(1)}, f32[73728]{0:T(1024)}, u32[]{:S(2)}) copy-start(f32[73728]{0:T(1024)} %param.25) | copy-start | bytes 884740
  308.0 3.8 %copy-start.3 = (f32[147456]{0:T(1024)S(1)}, f32[147456]{0:T(1024)}, u32[]{:S(2)}) copy-start(f32[147456]{0:T(1024)} %param.29) | copy-start | bytes 1769476
  308.1 3.8 %copy-start.4 = (f32[147456]{0:T(1024)S(1)}, f32[147456]{0:T(1024)}, u32[]{:S(2)}) copy-start(f32[147456]{0:T(1024)} %param.30) | copy-start | bytes 1769476
  308.1 3.8 %copy-start.5 = (f32[73728]{0:T(1024)S(1)}, f32[73728]{0:T(1024)}, u32[]{:S(2)}) copy-start(f32[73728]{0:T(1024)} %param.23) | copy-start | bytes 884740
  308.1 3.8 %copy-start.6 = (f32[73728]{0:T(1024)S(1)}, f32[73728]{0:T(1024)}, u32[]{:S(2)}) copy-start(f32[73728]{0:T(1024)} %param.26) | copy-start | bytes 884740
  308.1 3.8 %copy-start.7 = (f32[73728]{0:T(1024)S(1)}, f32[73728]{0:T(1024)}, u32[]{:S(2)}) copy-start(f32[73728]{0:T(1024)} %param.24) | copy-start | bytes 884740
  308.1 3.8 %copy-start.8 = (f32[73728]{0:T(1024)S(1)}, f32[73728]{0:T(1024)}, u32[]{:S(2)}) copy-start(f32[73728]{0:T(1024)} %param.27) | copy-start | bytes 884740
  308.1 3.8 %copy-start.9 = (f32[1152,128]{1,0:T(8,128)S(1)}, f32[1152,128]{1,0:T(8,128)}, u32[]{:S(2)}) copy-start(f32[1152,128]{1,0:T(8,128)} %get-tuple-element.87.refs_2_) | copy-start | bytes 1769476
  308.1 3.8 %copy-start.10 = (f32[576,128]{1,0:T(8,128)S(1)}, f32[576,128]{1,0:T(8,128)}, u32[]{:S(2)}) copy-start(f32[576,128]{1,0:T(8,128)} %get-tuple-element.85.refs_0_) | copy-start | bytes 884740
  308.1 3.8 %copy-start.11 = (f32[576,128]{1,0:T(8,128)S(1)}, f32[576,128]{1,0:T(8,128)}, u32[]{:S(2)}) copy-start(f32[576,128]{1,0:T(8,128)} %get-tuple-element.86.refs_1_) | copy-start | bytes 884740
  308.1 3.8 %copy-start.16 = (f32[32,128]{1,0:T(8,128)S(1)}, f32[32,128]{1,0:T(8,128)}, u32[]{:S(2)}) copy-start(f32[32,128]{1,0:T(8,128)} %get-tuple-element.90.refs_17_) | copy-start | bytes 49156
  308.2 3.8 %copy-start.17 = (f32[8,128]{1,0:T(8,128)S(1)}, f32[8,128]{1,0:T(8,128)}, u32[]{:S(2)}) copy-start(f32[8,128]{1,0:T(8,128)} %get-tuple-element.89.refs_16_) | copy-start | bytes 12292
  311.9 0.8 copy-start.13
  312.7 2.9 copy-start.19
  312.7 3.7 %copy-start.18 = (f32[256,768]{1,0:T(8,128)S(1)}, f32[256,768]{1,0:T(8,128)}, u32[]{:S(2)}) copy-start(f32[256,768]{1,0:T(8,128)} %get-tuple-element.83) | copy-start | bytes 2359300

commit v5 on v4

--- a/solution.py
+++ b/solution.py
@@ -602,38 +602,49 @@
     return rows, pl.ds(pl.multiple_of(ex * key_rows, key_rows), key_rows)
 
 
+def attend_back(mask_of, lens, q_ref, k_ref, v_ref, do_ref, key_rows):
+    scale = HD ** (-0.5)
+
+    def body(ex, _):
+        allowed = mask_of(lens[ex])
+        rows, keys = head_rows(ex, key_rows)
+        lanes = [pl.ds(m * 2 * HD, 2 * HD) for m in range(PAIRS)]
+        qs = [split_heads(q_ref[rows, at]) for at in lanes]
+        ks = [k_ref[keys, at] for at in lanes]
+        vs = [v_ref[keys, at] for at in lanes]
+        ds_out = [split_heads(do_ref[rows, at]) for at in lanes]
+        scores = [dot_nt(q, k) for q, k in zip(qs, ks)]
+        dps = [dot_nt(d, v) for d, v in zip(ds_out, vs)]
+        ps = [soft_rows(s, allowed) for s in scores]
+        dss = [
+            (p * (dp - jnp.sum(p * dp, axis=-1, keepdims=True))).astype(BF) for p, dp in zip(ps, dps)
+        ]
+        dvs = [dot_tn(p.astype(BF), d) for p, d in zip(ps, ds_out)]
+        dqs = [join_heads(dot_nn(ds, k)) * scale for ds, k in zip(dss, ks)]
+        dks = [dot_tn(ds, q) * scale for ds, q in zip(dss, qs)]
+        for at, dq, dk, dv in zip(lanes, dqs, dks, dvs):
+            v_ref[keys, at] = dv.astype(BF)
+            q_ref[rows, at] = dq.astype(BF)
+            k_ref[keys, at] = dk.astype(BF)
+        return 0
+
+    lax.fori_loop(0, EX_DEV, body, 0)
+
+
 def attend(mask_of, lens, q_ref, k_ref, v_ref, o_ref, key_rows):
     def body(ex, _):
         allowed = mask_of(lens[ex])
         rows, keys = head_rows(ex, key_rows)
-        for pair in range(PAIRS):
-            lanes = pl.ds(pair * 2 * HD, 2 * HD)
-            p = soft_rows(dot_nt(split_heads(q_ref[rows, lanes]), k_ref[keys, lanes]), allowed)
-            o_ref[rows, lanes] = join_heads(dot_nn(p.astype(BF), v_ref[keys, lanes])).astype(BF)
+        lanes = [pl.ds(m * 2 * HD, 2 * HD) for m in range(PAIRS)]
+        qs = [split_heads(q_ref[rows, at]) for at in lanes]
+        scores = [dot_nt(q, k_ref[keys, at]) for q, at in zip(qs, lanes)]
+        ps = [soft_rows(s, allowed).astype(BF) for s in scores]
+        outs = [join_heads(dot_nn(p, v_ref[keys, at])).astype(BF) for p, at in zip(ps, lanes)]
+        for at, out in zip(lanes, outs):
+            o_ref[rows, at] = out
         return 0
 
     lax.fori_loop(0, EX_DEV, body, 0)
-
-
-def attend_back(first, count, mask_of, lens, q_ref, k_ref, v_ref, do_ref, key_rows):
-    scale = HD ** (-0.5)
-
-    def body(ex, _):
-        allowed = mask_of(lens[ex])
-        rows, keys = head_rows(ex, key_rows)
-        for pair in range(PAIRS):
-            lanes = pl.ds(pair * 2 * HD, 2 * HD)
-            q, k, v = split_heads(q_ref[rows, lanes]), k_ref[keys, lanes], v_ref[keys, lanes]
-            p = soft_rows(dot_nt(q, k), allowed)
-            d_out = split_heads(do_ref[rows, lanes])
-            v_ref[keys, lanes] = dot_tn(p.astype(BF), d_out).astype(BF)
-            dp = dot_nt(d_out, v)
-            ds = (p * (dp - jnp.sum(p * dp, axis=-1, keepdims=True))).astype(BF)
-            q_ref[rows, lanes] = (join_heads(dot_nn(ds, k)) * scale).astype(BF)
-            k_ref[keys, lanes] = (dot_tn(ds, q) * scale).astype(BF)
-        return 0
-
-    lax.fori_loop(first, first + count, body, 0)
 
 
 def seed_of(cot_ref, lens, ex):
@@ -791,51 +802,47 @@
         if j == 3:
             loc.out(feed_v, feed_h)
 
-    slots = {
-        0: [begin],
-        4: [self_qkv],
-        5: [self_attention],
-        6: [cross_query],
-        7: [cross_keys],
-        8: [cross_attention],
-        9: [cross_out, lambda: feed(0), lambda: feed(1), lambda: feed(2), lambda: feed(3)],
-    }
-    n = len(chunks)
-    send_z(0)
-    send_z(1)
-    rows_of(cross_w, cross_in, 0, 0, per)
-    send_z(2)
-    send_z(3)
-    for up in (True, False):
-
-        @pl.when(z // 2 == (0 if up else 1))
-        def _():
-            for j in range(4):
-                rows_of(feed_w, feed_in, j, *feed_lines(j, *feed_in.shape[1:], up))
-
-    for t in range(4, min(AHEAD, n)):
-        send_z(t)
-    for t in range(n + 2):
-        if t == MEM_AT:
-            send_mem()
-        if t < n:
-            for k in range(1, NZ):
-                zc[t, k].wait_recv()
-                send_2(t, k)
-            if t + AHEAD < n:
-                send_z(t + AHEAD)
-        if 1 <= t <= n:
-            own[t - 1].wait()
-            for k in range(NZ):
-                for part in (0, 1):
-                    s2[t - 1, k, part].wait_recv()
-            send_3(t - 1)
-        if t >= 2:
-            s3[t - 2, 0].wait_recv()
-            s3[t - 2, 1].wait_recv()
-            send_4(t - 2)
-        for piece in slots.get(t, ()):
-            piece()
+    def prepare_cross():
+        rows_of(cross_w, cross_in, 0, 0, per)
+
+    def prepare_feed():
+        for up in (True, False):
+
+            @pl.when(z // 2 == (0 if up else 1))
+            def _():
+                for j in range(4):
+                    rows_of(feed_w, feed_in, j, *feed_lines(j, *feed_in.shape[1:], up))
+
+    def pass_2(t, k):
+        zc[t, k].wait_recv()
+        send_2(t, k)
+
+    def pass_3(t):
+        own[t].wait()
+        for k in range(NZ):
+            for part in (0, 1):
+                s2[t, k, part].wait_recv()
+        send_3(t)
+
+    def pass_4(t):
+        s3[t, 0].wait_recv()
+        s3[t, 1].wait_recv()
+        send_4(t)
+
+    for step_of, *which in (
+        (send_z, 0), (send_z, 1), (begin,), (prepare_cross,), (send_z, 2), (pass_2, 0, 1),
+        (pass_2, 0, 2), (pass_2, 0, 3), (send_z, 3), (pass_2, 1, 1), (pass_3, 0), (pass_2, 1, 2),
+        (pass_2, 1, 3), (prepare_feed,), (send_z, 4), (pass_2, 2, 1), (pass_2, 2, 2),
+        (pass_2, 2, 3), (pass_4, 0), (send_z, 5), (pass_3, 1), (pass_2, 3, 1), (pass_3, 2),
+        (pass_2, 3, 2), (pass_2, 3, 3), (send_z, 6), (pass_2, 4, 1), (pass_2, 4, 2), (pass_4, 1),
+        (pass_2, 4, 3), (send_z, 7), (pass_2, 5, 1), (self_qkv,), (pass_2, 5, 2),
+        (self_attention,), (pass_4, 2), (pass_2, 5, 3), (pass_2, 6, 1), (send_mem,), (pass_3, 3),
+        (pass_2, 6, 2), (pass_3, 4), (pass_2, 6, 3), (pass_3, 5), (pass_2, 7, 1), (pass_2, 7, 2),
+        (pass_2, 7, 3), (pass_4, 3), (cross_query,), (pass_4, 4), (pass_3, 6), (pass_4, 5),
+        (pass_3, 7), (pass_4, 6), (cross_keys,), (cross_attention,), (cross_out,), (feed, 0),
+        (pass_4, 7), (feed, 1), (feed, 2), (feed, 3),
+    ):
+        step_of(*which)
     loc.drain()
     cp.drain()
 
@@ -898,7 +905,7 @@
     ws, wc, wf, ms, mc, mf, ss, sc_, sf,
     out_ref, sg_ref, self_t, cross_t, feed_t, mem_t, vec_t, sq_t, norm_t, attn_g, up_g,
     wr, ur, mem_v, q1, k1, v1, o1, q2, o2, a1, a2, a3, k2, v2, z_v, slope_v, h1, h2, e3, du, db,
-    ring_a, ring_u, held, r1, r2a, r2b, r3a, r3b, rz, whole, vecg, v_send, v_recv, v_z,
+    ring_a, ring_u, held, r1, r2a, r2b, r3a, r3b, rz, whole, vw, vecg, v_send, v_recv, v_z,
     qa, qb, na, nb, opt_s, opt_c, opt_f, send, recv, local,
 ):
     dp, fs, z, y, x, c = place()
@@ -973,6 +980,7 @@
     sc, sl, s1, s2, sz = {}, {}, {}, {}, {}
 
     def phase_0(t):
+        stored(*((8 + t,) if t < 4 else (4, 5, 6, 7) if t < 6 else (0, 1, 2, 3)))
         for zz in range(NZ):
             sc[t, zz] = cp.remote(sources[t](zz, 1 - c), r1.at[t, zz], to_c)
             sl[t, zz] = loc.start(sources[t](zz, c), held.at[t % held.shape[0], zz])
@@ -1124,8 +1132,8 @@
         for one in cross_ok[1:4]:
             one.wait()
 
-    def cross_part(first, count):
-        attend_back(first, count, cross_mask, plen_ref, q2, k2, v2, e3, MEMLEN)
+    def cross_part():
+        attend_back(cross_mask, plen_ref, q2, k2, v2, e3, MEMLEN)
 
     def cross_query():
         cross_ok[5].wait()
@@ -1150,6 +1158,8 @@
             mem_v[i] = part.astype(BF).reshape(mem_v.shape[1:])
         fetch()
         fetch()
+
+    def send_mem():
         mem_sent.append(loc.start(mem_v.at[:, dp], mem_t.at[pl.ds(ex_count * dp, ex_count)]))
         for k in range(1, ndp):
             mem_sent.append(
@@ -1179,7 +1189,7 @@
         a1[...] = (unit * gains[0] + shifts[0]).astype(BF)
 
     def self_part():
-        attend_back(0, EX_DEV, self_mask, slen_ref, q1, k1, v1, e3, SUF)
+        attend_back(self_mask, slen_ref, q1, k1, v1, e3, SUF)
 
     def self_weights():
         for i, ref in enumerate((q1, k1, v1)):
@@ -1199,6 +1209,14 @@
     def vec_step(i):
         if i == 0:
             vec_cp.append(cp.remote(vecg, v_recv.at[0], to_c))
+            return
+        if i == 4:
+            for one in vec_cp[3:]:
+                one.wait_recv()
+            vw[...] = (v_z[0] + v_z[1]) + (v_z[2] + v_z[3])
+            vec_t[...] = jnp.zeros_like(vec_t)
+            for i in range(per):
+                vec_t[pl.ds(i, 11, stride=per), :] = vw[0:11, i * LANES : (i + 1) * LANES]
             return
         vec_cp[-1].wait_recv()
         i -= 1
@@ -1210,80 +1228,20 @@
             for k in range(1, NZ):
                 vec_cp.append(cp.remote(v_send.at[2], v_z.at[z], peer_id((z + k) % NZ, y, x, c)))
 
-    begin()
-    feed(0)
-    feed(1)
-    stored(8)
-    phase_0(0)
-    feed(2)
-    stored(9)
-    phase_0(1)
-    phase_c(0)
-    feed(3)
-    stored(10)
-    phase_0(2)
-    phase_c(1)
-    stored(11)
-    phase_0(3)
-    feed_down()
-    phase_c(2)
-    cross_begin()
-    phase_c(3)
-    cross_part(0, 2)
-    phase_1(0)
-    cross_part(2, 2)
-    cross_query()
-    phase_2(0)
-    phase_1(1)
-    cross_key()
-    cross_value()
-    stored(4, 5, 6, 7)
-    phase_0(4)
-    phase_0(5)
-    cross_memory()
-    phase_2(1)
-    phase_c(4)
-    phase_1(2)
-    phase_z(0)
-    cross_end()
-    self_begin()
-    phase_c(5)
-    self_part()
-    self_weights()
-    stored(0, 1, 2, 3)
-    phase_0(6)
-    phase_0(7)
-    phase_2(2)
-    phase_1(3)
-    self_end()
-    vec_step(0)
-    phase_z(1)
-    phase_c(6)
-    phase_c(7)
-    vec_step(1)
-    phase_2(3)
-    phase_1(4)
-    phase_z(2)
-    vec_step(2)
-    phase_1(5)
-    phase_2(4)
-    phase_z(3)
-    vec_step(3)
-    phase_1(6)
-    phase_2(5)
-    phase_z(4)
-    phase_1(7)
-    phase_2(6)
-    phase_z(5)
-    phase_2(7)
-    phase_z(6)
-    for one in vec_cp[3:]:
-        one.wait_recv()
-    whole[0:16] = (v_z[0] + v_z[1]) + (v_z[2] + v_z[3])
-    vec_t[...] = jnp.zeros_like(vec_t)
-    for i in range(per):
-        vec_t[pl.ds(i, 11, stride=per), :] = whole[0:11, i * LANES : (i + 1) * LANES]
-    phase_z(7)
+    for step_of, *which in (
+        (begin,), (feed, 0), (phase_0, 0), (feed, 1), (feed, 2), (phase_c, 0), (feed, 3),
+        (phase_0, 1), (feed_down,), (cross_begin,), (cross_part,), (phase_1, 0), (phase_0, 2),
+        (cross_query,), (phase_c, 1), (cross_key,), (phase_c, 2), (phase_2, 0), (cross_value,),
+        (cross_memory,), (send_mem,), (phase_0, 3), (cross_end,), (phase_0, 4), (self_begin,),
+        (self_part,), (phase_c, 3), (phase_1, 2), (self_weights,), (phase_0, 5), (phase_c, 5),
+        (self_end,), (phase_1, 1), (phase_0, 7), (phase_2, 2), (phase_c, 7), (vec_step, 0),
+        (phase_1, 3), (phase_2, 1), (phase_1, 7), (phase_1, 5), (phase_2, 3), (phase_c, 4),
+        (phase_0, 6), (vec_step, 1), (phase_c, 6), (phase_2, 7), (phase_z, 3), (phase_2, 5),
+        (vec_step, 2), (vec_step, 3), (phase_1, 4), (phase_z, 5), (phase_z, 0), (phase_z, 2),
+        (phase_2, 4), (phase_1, 6), (phase_z, 7), (phase_2, 6), (phase_z, 1), (phase_z, 4),
+        (vec_step, 4), (phase_z, 6),
+    ):
+        step_of(*which)
     sq = squares(self_t[...]) + squares(cross_t[...]) + squares(feed_t[...])
     sq = sum_everywhere(cp, sq, qa, qb, dp, fs) + squares(vec_t[...])
     sq_t[...] = sq
@@ -1359,6 +1317,7 @@
             low(8, NZ - 1, step),
             wide(step, width),
             wide(vec_rows, width),
+            wide(vec_rows, width),
             wide(3, vec_rows, width),
             wide(3, vec_rows, width),
             wide(NZ, vec_rows, width),
@@ -1372,7 +1331,7 @@
             pltpu.SemaphoreType.DMA((96,)),
         ],
         compiler_params=pltpu.CompilerParams(
-            collective_id=2, has_side_effects=True, vmem_limit_bytes=60 << 20
+            collective_id=2, has_side_effects=True, vmem_limit_bytes=62 << 20
         ),
         name="backward_all",
     )(*kept, x, cot, vec, slen, plen, *states)

time: 323 us -> 277 us (0.86)
  Pallas kernels: 306 us -> 261 us
    pallas_call x1, Pallas kernels: 175 us -> 143 us  [backward_all(): pl.pallas_call(backward_kernel, out_shape=[shape(rows, width), shape(rows...]
    pallas_call x1, Pallas kernels: 128 us -> 115 us  [forward_all(): pl.pallas_call(forward_kernel, out_shape=[jax.ShapeDtypeStruct(*arrays[k]...]
where the time goes in v5:
time: 277 us; the launch traced here: 272 us
  Pallas kernels  261 us (94%)
  local copies, waits for them, and re-layouts  6.71 us (2%)
  other arithmetic  3.6 us (1%)
    pallas_call x1, Pallas kernels, backward_all(): pl.pallas_call(backward_kernel, out_shape=[shape(rows, width), shape(rows...  143 us
    pallas_call x1, Pallas kernels, forward_all(): pl.pallas_call(forward_kernel, out_shape=[jax.ShapeDtypeStruct(*arrays[k]...  115 us

profile of v5, /device:TPU:0, one launch (start us, length us, event | category | flops | bytes accessed | tf_op | source)
XLA Modules:
  0.0 272.5 jit_solution(2170337133716908228)
XLA Ops:
  0.7 1.3 broadcast_in_dim.23.plen_ref
  2.0 1.3 broadcast_in_dim.21.slen_ref
  3.3 1.4 reshape.160.vec_ref
  4.7 115.2 %forward_all.1 = (bf16[8,2,2,2,96,768]{5,4,3,2,1,0:T(8,128)(2,1)}, bf16[4,2,2,2,4,48,768]{6,5,4,3,2,1,0:T(8,128)(2,1)}, bf16[4,8,32,768]{3,2,1,0:T(8,128)(2,1)},...) custom-call(f32[576,128]{1,0:T(8,128)} %bitcast.45, ...), custom_call_target="tpu_custom_call" | custom-call | tf_op jit(solution)/shard_map/forward_all/pallas_call | solution.py:870
  119.9 0.0 copy-start.12
  119.9 0.0 copy-start.14
  119.9 0.0 copy-start.15
  119.9 142.9 %backward_all.1 = (f32[256,768]{1,0:T(8,128)}, f32[256,768]{1,0:T(8,128)}, f32[576,128]{1,0:T(8,128)}, f32[576,128]{1,0:T(8,128)}, f32[1152,128]{1,0:T(8,128)}, ...) custom-call(bf16[8,768,768]{2,1,0:T(8,128)(2,1)} %bitcast.68, ...), custom_call_target="tpu_custom_call" | custom-call | tf_op jit(solution)/shard_map/backward_all/pallas_call | solution.py:1280
  262.8 0.0 copy-start
  262.9 0.0 copy-start.1
  262.9 0.0 copy-start.2
  262.9 0.0 copy-start.3
  262.9 0.0 copy-start.4
  262.9 0.0 copy-start.5
  262.9 0.0 copy-start.6
  262.9 0.0 copy-start.7
  262.9 0.0 copy-start.8
  263.0 0.0 copy-start.9
  263.0 0.0 copy-start.10
  263.0 0.0 copy-start.11
  263.0 0.0 copy-start.16
  263.0 0.0 copy-start.17
  263.0 3.6 %bitcast_convert_fusion = f32[1,32,32,768]{3,2,1,0:T(8,128)} fusion(bf16[32,32,768]{2,1,0:T(8,128)(2,1)} %get-tuple-element.84), kind=kLoop, calls=%fused_computation | loop fusion | flops 786432 | bytes 4718592 | tf_op jit(solution)/shard_map/broadcast_in_dim | solution.py:1451
  266.6 0.0 copy-done.12
  266.6 0.0 copy-done.14
  266.6 0.0 copy-done.15
  266.6 0.0 copy-done
  266.6 0.0 copy-done.1
  266.6 0.0 copy-done.2
  266.6 0.0 copy-done.3
  266.7 0.0 copy-done.4
  266.7 0.0 copy-done.5
  266.7 0.0 copy-done.6
  266.7 0.0 copy-done.7
  266.7 0.0 copy-done.8
  266.7 0.0 copy-done.9
  266.7 0.0 copy-done.10
  266.7 0.0 copy-done.11
  266.7 0.0 copy-done.16
  266.8 0.0 copy-done.17
  266.8 0.0 copy-start.13
  266.8 0.8 copy-done.13
  267.6 0.0 copy-start.19
  267.6 0.0 copy-start.18
  267.6 2.9 %update_all.1 = (f32[576,128]{1,0:T(8,128)}, f32[576,128]{1,0:T(8,128)}, f32[576,128]{1,0:T(8,128)}, f32[576,128]{1,0:T(8,128)}, f32[576,128]{1,0:T(8,128)}, /*i...) custom-call(f32[576,128]{1,0:T(8,128)S(1)} %copy-done.10, ...), custom_call_target="tpu_custom_call" | custom-call | tf_op jit(solution)/shard_map/update_all/pallas_call | solution.py:1390
  270.4 0.0 copy-done.19
  270.4 0.9 copy.40
  271.3 0.0 copy-done.18
  271.3 0.9 copy.41
Async XLA Ops:
  119.9 146.7 %copy-start.12 = (f32[8448]{0:T(1024)S(1)}, f32[8448]{0:T(1024)}, u32[]{:S(2)}) copy-start(f32[8448]{0:T(1024)} %param.31) | copy-start | bytes 101380
  119.9 146.7 %copy-start.14 = (f32[8448]{0:T(1024)S(1)}, f32[8448]{0:T(1024)}, u32[]{:S(2)}) copy-start(f32[8448]{0:T(1024)} %param.32) | copy-start | bytes 101380
  119.9 146.7 %copy-start.15 = (f32[8448]{0:T(1024)S(1)}, f32[8448]{0:T(1024)}, u32[]{:S(2)}) copy-start(f32[8448]{0:T(1024)} %param.33) | copy-start | bytes 101380
  262.8 3.8 %copy-start = (f32[147456]{0:T(1024)S(1)}, f32[147456]{0:T(1024)}, u32[]{:S(2)}) copy-start(f32[147456]{0:T(1024)} %param.28) | copy-start | bytes 1769476
  262.9 3.8 %copy-start.1 = (f32[73728]{0:T(1024)S(1)}, f32[73728]{0:T(1024)}, u32[]{:S(2)}) copy-start(f32[73728]{0:T(1024)} %param.22) | copy-start | bytes 884740
  262.9 3.8 %copy-start.2 = (f32[73728]{0:T(1024)S(1)}, f32[73728]{0:T(1024)}, u32[]{:S(2)}) copy-start(f32[73728]{0:T(1024)} %param.25) | copy-start | bytes 884740
  262.9 3.8 %copy-start.3 = (f32[147456]{0:T(1024)S(1)}, f32[147456]{0:T(1024)}, u32[]{:S(2)}) copy-start(f32[147456]{0:T(1024)} %param.29) | copy-start | bytes 1769476
  262.9 3.8 %copy-start.4 = (f32[147456]{0:T(1024)S(1)}, f32[147456]{0:T(1024)}, u32[]{:S(2)}) copy-start(f32[147456]{0:T(1024)} %param.30) | copy-start | bytes 1769476
  262.9 3.8 %copy-start.5 = (f32[73728]{0:T(1024)S(1)}, f32[73728]{0:T(1024)}, u32[]{:S(2)}) copy-start(f32[73728]{0:T(1024)} %param.23) | copy-start | bytes 884740
  262.9 3.8 %copy-start.6 = (f32[73728]{0:T(1024)S(1)}, f32[73728]{0:T(1024)}, u32[]{:S(2)}) copy-start(f32[73728]{0:T(1024)} %param.26) | copy-start | bytes 884740
  262.9 3.8 %copy-start.7 = (f32[73728]{0:T(1024)S(1)}, f32[73728]{0:T(1024)}, u32[]{:S(2)}) copy-start(f32[73728]{0:T(1024)} %param.24) | copy-start | bytes 884740
  262.9 3.8 %copy-start.8 = (f32[73728]{0:T(1024)S(1)}, f32[73728]{0:T(1024)}, u32[]{:S(2)}) copy-start(f32[73728]{0:T(1024)} %param.27) | copy-start | bytes 884740
  263.0 3.8 %copy-start.9 = (f32[1152,128]{1,0:T(8,128)S(1)}, f32[1152,128]{1,0:T(8,128)}, u32[]{:S(2)}) copy-start(f32[1152,128]{1,0:T(8,128)} %get-tuple-element.87.refs_2_) | copy-start | bytes 1769476
  263.0 3.8 %copy-start.10 = (f32[576,128]{1,0:T(8,128)S(1)}, f32[576,128]{1,0:T(8,128)}, u32[]{:S(2)}) copy-start(f32[576,128]{1,0:T(8,128)} %get-tuple-element.85.refs_0_) | copy-start | bytes 884740
  263.0 3.8 %copy-start.11 = (f32[576,128]{1,0:T(8,128)S(1)}, f32[576,128]{1,0:T(8,128)}, u32[]{:S(2)}) copy-start(f32[576,128]{1,0:T(8,128)} %get-tuple-element.86.refs_1_) | copy-start | bytes 884740
  263.0 3.8 %copy-start.16 = (f32[32,128]{1,0:T(8,128)S(1)}, f32[32,128]{1,0:T(8,128)}, u32[]{:S(2)}) copy-start(f32[32,128]{1,0:T(8,128)} %get-tuple-element.90.refs_17_) | copy-start | bytes 49156
  263.0 3.8 %copy-start.17 = (f32[8,128]{1,0:T(8,128)S(1)}, f32[8,128]{1,0:T(8,128)}, u32[]{:S(2)}) copy-start(f32[8,128]{1,0:T(8,128)} %get-tuple-element.89.refs_16_) | copy-start | bytes 12292
  266.8 0.8 copy-start.13
  267.6 2.9 %copy-start.19 = (f32[256,768]{1,0:T(8,128)S(1)}, f32[256,768]{1,0:T(8,128)}, u32[]{:S(2)}) copy-start(f32[256,768]{1,0:T(8,128)} %get-tuple-element.82) | copy-start | bytes 2359300
  267.6 3.7 %copy-start.18 = (f32[256,768]{1,0:T(8,128)S(1)}, f32[256,768]{1,0:T(8,128)}, u32[]{:S(2)}) copy-start(f32[256,768]{1,0:T(8,128)} %get-tuple-element.83) | copy-start | bytes 2359300
